TPU v7x, 512 devices: a whole 4x8x8 slice. The times are simulated.
512 devices in a mesh: section: 16 (over y_hi, x), strip: 32 (over z, y_lo, core).
Axes of the slice: x: 4, y: 8 (y_hi: 4, y_lo: 2; y = y_hi * 2 + y_lo), z: 8, core: 2. Of those that a mesh axis runs over, the one named last changes fastest.
Arguments:
- images: bfloat16 [2, 128, 32, 256], P(None, 'strip'), may hold values from -6 to 6
- conv_first: bfloat16 [16, 9, 256, 256], P('section'), may hold values from -0.1875 to 0.1875
- conv_skip: bfloat16 [16, 9, 256, 256], P('section'), may hold values from -0.09375 to 0.09375
- conv_second: bfloat16 [16, 9, 256, 256], P('section'), may hold values from -0.1875 to 0.1875
- bias_first: float32 [16, 256], P('section'), may hold values from -0.8 to 0.8
- bias_second: float32 [16, 256], P('section'), may hold values from -0.8 to 0.8
Outputs:
- activations: bfloat16 [16, 2, 128, 32, 256], P('section', None, 'strip')
All inputs are finite; a program needn't handle non-finite values.
Results may differ from a plain program's by a relative error of at most 0.02.
Values may be sent and summed in bfloat16 or wider, within the bound.
No kernel may reach another device: no remote copies, remote signals or barrier semaphores. Data moves between devices by JAX's collectives and lax.ppermute only.
A program may use at most 64 MiB of HBM per device.

v0:
```python
import jax
import jax.numpy as jnp
from jax import lax
from jax.experimental import pallas as pl
from jax.experimental.pallas import tpu as pltpu
from jax.sharding import PartitionSpec as P


BF16 = jnp.bfloat16
F32 = jnp.float32
ROWS = 4
COLS = 32
CH = 256
BLOCK = ROWS * COLS
TAPS = 9 * CH
HALF = TAPS // 2
SECTIONS = 16
STRIPS = 32
HEIGHT = ROWS * STRIPS
GROUPS = SECTIONS // 2
JOINT = ("section", "strip")


def place(group, micro):
    first = 4 * (group // 2)
    return first + (micro if group % 2 == 0 else 3 - micro)


def route(moves):
    pairs = []
    for source, target, shift in moves:
        for micro in range(2):
            for strip in range(STRIPS):
                if 0 <= strip + shift < STRIPS:
                    pairs.append(
                        (
                            place(source, micro) * STRIPS + strip,
                            place(target, micro) * STRIPS + strip + shift,
                        )
                    )
    return pairs


def send(block, moves):
    return lax.ppermute(block, JOINT, route(moves))


def spread(dest, at, value, rows):
    size = rows * COLS
    column = lax.broadcasted_iota(jnp.int32, (size, CH), 0) & (COLS - 1)
    left = jnp.where(column == 0, 0.0, pltpu.roll(value, 1, 0))
    right = jnp.where(column == COLS - 1, 0.0, pltpu.roll(value, size - 1, 0))
    dest[at : at + size, 0:CH] = left.astype(BF16)
    dest[at : at + size, CH : 2 * CH] = value.astype(BF16)
    dest[at : at + size, 2 * CH : 3 * CH] = right.astype(BF16)


def conv(source, weight, rows):
    size = rows * COLS
    total = None
    for tap in range(3):
        part = jnp.dot(
            source[tap * COLS : tap * COLS + size, :],
            weight[tap * 3 * CH : (tap + 1) * 3 * CH, :],
            preferred_element_type=F32,
        )
        total = part if total is None else total + part
    return total


def finish(total, bias, rows, first, period=None):
    size = rows * COLS
    value = jnp.maximum(total + bias, 0.0)
    row = lax.broadcasted_iota(jnp.int32, (size, CH), 0) >> 5
    if period is not None:
        row = jnp.where(row < period, row, row - period)
    row = row + first
    value = jnp.where((row >= 0) & (row < HEIGHT), value, 0.0)
    return value.astype(BF16).astype(F32)


def single_kernel(halo):
    tall = ROWS + 2 * halo
    out_rows = tall - 4

    def kernel(info, *refs):
        blocks = refs[:-5]
        bias, first, second, out, work = refs[-5:]

        @pl.when(info[0] == 0)
        def _():
            out[...] = jnp.zeros(out.shape, BF16)

        @pl.when(info[0] != 0)
        def _():
            for micro in range(2):
                at = micro * tall * COLS
                for ref in blocks:
                    rows = ref.shape[1] // COLS
                    spread(work, at, ref[micro].astype(F32), rows)
                    at += rows * COLS
            top = info[1] - halo + 1
            value = finish(conv(work, first, 2 * tall - 2), bias[0:1, :], 2 * tall - 2, top, tall)
            spread(work, 0, value, 2 * tall - 2)
            value = finish(conv(work, second, 2 * tall - 4), bias[1:2, :], 2 * tall - 4, top + 1, tall)
            value = value.astype(BF16)
            for micro in range(2):
                at = micro * tall * COLS
                out[micro] = value[at : at + out_rows * COLS]

    def call(info, blocks, bias, first, second):
        vmem = pl.BlockSpec(memory_space=pltpu.VMEM)
        operands = [info, *blocks, bias, first, second]
        return pl.pallas_call(
            kernel,
            out_shape=jax.ShapeDtypeStruct((2, out_rows * COLS, CH), BF16),
            in_specs=[pl.BlockSpec(memory_space=pltpu.SMEM)] + [vmem] * (len(operands) - 1),
            out_specs=vmem,
            scratch_shapes=[pltpu.VMEM((2 * tall * COLS, 3 * CH), BF16)],
            compiler_params=pltpu.CompilerParams(vmem_limit_bytes=40 * 1024 * 1024),
        )(*operands)

    return call


def phase_kernel(decoder, doubled=False):
    kinds = 3 if decoder else 2

    def kernel(*refs):
        refs = list(refs)
        info = refs.pop(0)
        xs = [refs.pop(0) for _ in range(6 if doubled else 3)]
        if decoder:
            skip_wide = [refs.pop(0) for _ in range(3)]
            skip_narrow = refs.pop(0)
        bias = refs.pop(0)
        weights = [refs.pop(0) for _ in range(2 * kinds)]
        prev0 = refs.pop(0)
        prev1 = refs.pop(0)
        out0 = refs.pop(0)
        out1 = refs.pop(0)
        work = refs.pop(0)
        if decoder:
            skip_work = refs.pop(0)

        active = info[0]
        top = info[1]

        @pl.when(active == 0)
        def _():
            out0[...] = prev0[...]
            out1[...] = prev1[...]

        @pl.when(active != 0)
        def _():
            for index in range(3):
                value = xs[index][...].astype(F32)
                if doubled:
                    value = jnp.where(info[2] == 0, value, xs[index + 3][...].astype(F32))
                spread(work, index * BLOCK, value, ROWS)
            if decoder:
                for index, ref in enumerate(skip_wide):
                    spread(skip_work, index * BLOCK, ref[...].astype(F32), ROWS)
            for section in range(2):
                base = section * kinds
                rows = 10 - 4 * section
                start = 2 * section - 3
                total = conv(work, weights[base], rows)
                if decoder:
                    total = total + conv(skip_work, weights[base + 2], rows)
                value = finish(total, bias[2 * section : 2 * section + 1, :], rows, top + start)
                spread(work, 0, value, rows)
                if decoder and section == 0:
                    spread(skip_work, 0, skip_narrow[...].astype(F32), 2 * ROWS)
                value = finish(
                    conv(work, weights[base + 1], rows - 2),
                    bias[2 * section + 1 : 2 * section + 2, :],
                    rows - 2,
                    top + start + 1,
                )
                if section == 0:
                    out0[...] = value.astype(BF16)
                    spread(work, 0, value, rows - 2)
                else:
                    out1[...] = value.astype(BF16)

    def call(info, xs, skips, bias, weights, prev0, prev1):
        operands = [info, *xs, *skips, bias, *weights, prev0, prev1]
        vmem = pl.BlockSpec(memory_space=pltpu.VMEM)
        specs = [pl.BlockSpec(memory_space=pltpu.SMEM)] + [vmem] * (len(operands) - 1)
        scratch = [pltpu.VMEM((3 * BLOCK, 3 * CH), BF16)]
        if decoder:
            scratch.append(pltpu.VMEM((3 * BLOCK, 3 * CH), BF16))
        return pl.pallas_call(
            kernel,
            out_shape=(
                jax.ShapeDtypeStruct((2 * BLOCK, CH), BF16),
                jax.ShapeDtypeStruct((BLOCK, CH), BF16),
            ),
            in_specs=specs,
            out_specs=(vmem, vmem),
            scratch_shapes=scratch,
            compiler_params=pltpu.CompilerParams(vmem_limit_bytes=40 * 1024 * 1024),
            name="decode" if decoder else "encode",
        )(*operands)

    return call


def body(images, conv_first, conv_skip, conv_second, bias_first, bias_second):
    section = lax.axis_index("section")
    strip = lax.axis_index("strip")
    core = strip % 2
    parity = section % 2
    group = section // 2
    micro = jnp.where(group % 2 == 0, parity, 1 - parity)
    own = [w.reshape(TAPS, CH) for w in (conv_first[0], conv_second[0], conv_skip[0])]
    decoders = range(SECTIONS // 2, SECTIONS)
    pairs_from = range(2, SECTIONS)
    cores = [(i, i ^ 1) for i in range(STRIPS)]

    def shift_in_section(block, which, shift):
        return lax.ppermute(
            block,
            JOINT,
            [
                (which * STRIPS + p, which * STRIPS + p + shift)
                for p in range(STRIPS)
                if 0 <= p + shift < STRIPS
            ],
        )

    def partner(block, sections=range(SECTIONS)):
        return lax.ppermute(block, "section", [(i, i ^ 1) for i in sections])

    both = jnp.concatenate([bias_first, bias_second], axis=0)
    image = images.reshape(2, BLOCK, CH)
    below = shift_in_section(image, 0, -1)
    above = shift_in_section(image, 0, 1)
    other = partner(both, pairs_from)
    halves = [lax.dynamic_slice_in_dim(w, core * HALF, HALF, axis=0) for w in own]
    fetched = [
        partner(halves[0], pairs_from),
        partner(halves[1], pairs_from),
        partner(halves[2], decoders),
    ]

    def solo_info(which):
        active = (section == which).astype(jnp.int32)
        return jnp.stack([active, strip * ROWS]).astype(jnp.int32)

    wide = single_kernel(4)(solo_info(0), (above, image, below), both, own[0], own[1])
    handed = lax.ppermute(wide, JOINT, [(p, STRIPS + p) for p in range(STRIPS)])
    close = single_kernel(2)(solo_info(1), (handed,), both, own[0], own[1])
    xs = [None] * 6
    for shift in (1, -1, 0):
        for to in range(2):
            xs[3 * to + 1 - shift] = lax.ppermute(
                close[to],
                JOINT,
                [
                    (STRIPS + p, place(1, to) * STRIPS + p + shift)
                    for p in range(STRIPS)
                    if 0 <= p + shift < STRIPS
                ],
            )
    give = jnp.where(parity == 0, wide[1], jnp.concatenate([close[0], close[0]], axis=0))
    got = partner(give, range(2))
    level0 = jnp.where(parity == 0, wide[0], got)
    level1 = jnp.where(parity == 0, got[:BLOCK], close[1])

    swapped = [
        lax.ppermute(
            half,
            JOINT,
            [
                (s * STRIPS + a, s * STRIPS + b)
                for s in (decoders if index == 2 else pairs_from)
                for a, b in cores
            ],
        )
        for index, half in enumerate(fetched)
    ]
    bias = jnp.where(
        parity == 0,
        jnp.concatenate([both, other], axis=0),
        jnp.concatenate([other, both], axis=0),
    )

    def joined(mine, half, other_half):
        remote = jnp.where(
            core == 0,
            jnp.concatenate([half, other_half], axis=0),
            jnp.concatenate([other_half, half], axis=0),
        )
        return jnp.where(parity == 0, mine, remote), jnp.where(parity == 0, remote, mine)

    by_kind = [joined(*parts) for parts in zip(own, fetched, swapped)]
    all_weights = [pair[0] for pair in by_kind] + [pair[1] for pair in by_kind]
    encode_weights = all_weights[0:2] + all_weights[3:5]

    def info_of(phase):
        active = (group == phase).astype(jnp.int32)
        return jnp.stack([active, strip * ROWS, micro]).astype(jnp.int32)

    decode = phase_kernel(True)
    out0 = jnp.zeros((2 * BLOCK, CH), BF16)
    out1 = jnp.zeros((BLOCK, CH), BF16)
    middle = GROUPS // 2

    def onward(block, phase):
        pieces = {d: send(block, [(phase, phase + 1, d)]) for d in (1, -1, 0)}
        return (pieces[1], pieces[0], pieces[-1])

    for phase in range(1, middle):
        encode = phase_kernel(False, phase == 1)
        out0, out1 = encode(info_of(phase), xs, (), bias, encode_weights, out0, out1)
        xs = onward(out1, phase)
    mirror = [(g, GROUPS - 1 - g) for g in range(middle - 1)]
    narrow = send(out0, [(middle - 1, middle, 0)])
    out0 = jnp.where(group == 0, level0, out0)
    out1 = jnp.where(group == 0, level1, out1)
    late_wide = tuple(send(out1, [(a, b, shift) for a, b in mirror]) for shift in (1, 0, -1))
    late_narrow = send(out0, [(a, b, 0) for a, b in mirror])
    for phase in range(middle, GROUPS):
        skips = (*xs, narrow) if phase == middle else (*late_wide, late_narrow)
        out0, out1 = decode(info_of(phase), xs, skips, bias, all_weights, out0, out1)
        if phase + 1 < GROUPS:
            xs = onward(out1, phase)

    inner = out0[BLOCK // 2 : BLOCK // 2 + BLOCK]
    mine = jnp.where(parity == 0, inner, out1)
    theirs = partner(jnp.where(parity == 0, out1, inner))
    result = jnp.where(
        micro == 0, jnp.stack([mine, theirs]), jnp.stack([theirs, mine])
    )
    return result.reshape(1, 2, ROWS, COLS, CH)


def solution(mesh):
    placed = (
        P(None, "strip", None, None),
        P("section", None, None, None),
        P("section", None, None, None),
        P("section", None, None, None),
        P("section", None),
        P("section", None),
    )

    return jax.shard_map(
        body,
        mesh=mesh,
        in_specs=placed,
        out_specs=P("section", None, "strip", None, None),
        check_vma=False,
    )
```

profile of v0, /device:TPU:2, one launch (start us, length us, event | category | flops | bytes accessed | tf_op | source)
XLA Modules:
  0.0 202.7 jit_solution(16868253716745072846)
XLA Ops:
  1.5 1.9 constant_dynamic-slice_fusion.1
  3.4 18.8 %collective-permute-start.12 = (bf16[1152,256]{1,0:T(8,128)(2,1)}, bf16[1152,256]{1,0:T(8,128)(2,1)}, u32[]{:S(2)}, u32[]{:S(2)}) collective-permute-start(bf16[1152,256]{1,0:T(8,128)(2,1)} %constant_dynamic-slice_fusion.1), channel_id=1, source_target_pairs={{64,96},{96,64},{128,160},{160,128},{192,224},{224,192},{256,288},... | collective-permute-start | bytes 1769480 | tf_op jit(solution)/shard_map/ppermute | solution.py:234
  23.0 16.8 %collective-permute-start.10 = (bf16[1152,256]{1,0:T(8,128)(2,1)}, bf16[1152,256]{1,0:T(8,128)(2,1)}, u32[]{:S(2)}, u32[]{:S(2)}) collective-permute-start(bf16[1152,256]{1,0:T(8,128)(2,1)} %constant_dynamic-slice_fusion.2), channel_id=1, source_target_pairs={{64,96},{96,64},{128,160},{160,128},{192,224},{224,192},{256,288},... | collective-permute-start | bytes 1769480 | tf_op jit(solution)/shard_map/ppermute | solution.py:234
  39.9 15.9 %collective-permute-start.9 = (f32[2,256]{1,0:T(2,128)S(1)}, f32[2,256]{1,0:T(2,128)S(1)}, u32[]{:S(2)}, u32[]{:S(2)}) collective-permute-start(f32[2,256]{1,0:T(2,128)S(1)} %pad_maximum_fusion.refs_3_.refs_1_), channel_id=1, source_target_pairs={{64,96},{96,64},{128,160},{160,128},{192,224},{224,192},{256,288},... | collective-permute-start | bytes 6152 | tf_op jit(solution)/shard_map/ppermute | solution.py:234
  55.8 1.9 constant_dynamic-slice_fusion
  57.9 1.5 collective-permute-start.24
  59.9 1.3 collective-permute-start.2
  61.3 1.5 collective-permute-start.13
  62.9 10.2 %collective-permute-done.2.refs_0_ = bf16[2,256,256]{2,1,0:T(8,128)(2,1)S(1)} collective-permute-done((bf16[2,256,256]{2,1,0:T(8,128)(2,1)S(1)}, bf16[2,256,256]{2,1,0:T(8,128)(2,1)S(1)}, u32[]{:S(2)}, u32[]{:S(2)}) %collective-permute-start.2) | collective-permute-done | bytes 262176 | tf_op jit(solution)/shard_map/ppermute | solution.py:253
  73.1 2.7 %shard_map.65 = bf16[2,128,256]{2,1,0:T(8,128)(2,1)S(1)} custom-call(s32[2]{0:T(128)S(1)} %pad_add_fusion.info, bf16[2,256,256]{2,1,0:T(8,128)(2,1)S(1)} %collective-permute-done.2.refs_0_, f32[2,256]{1,0:T(2,128)S(1)} %pad_maximum_fusion.refs_3_.refs_1_, bf16[2304,256]{1,0:T(8,128)(2,1)S(1)} %bitcast.44, bf16[2304,256]{1,0:T(8,128)(2,1)S(1)} %bitcast.41), custom_call_target="tpu_custom_call" | custom-call | tf_op jit(solution)/shard_map/pallas_call | solution.py:114
  75.8 1.3 collective-permute-start.3
  77.1 1.3 collective-permute-start.4
  80.6 2.1 %broadcast_select_fusion.2 = (bf16[2304,256]{1,0:T(8,128)(2,1)S(1)}, bf16[2304,256]{1,0:T(8,128)(2,1)S(1)}) fusion(pred[]{:T(512)S(6)} %eq.62, bf16[1152,256]{1,0:T(8,128)(2,1)} %collective-permute-done.12, bf16[1152,256]{1,0:T(8,128)(2,1)} %collective-permute-done.13, pred[]{:T(512)S(6)} %eq.72, bf16[1,9,256,256]{3,2,1,0:T(8,128)(2,1)S(1)} %copy-done.2), kind=kLoop, calls=%fused_computation.5 | loop fusion | flops 6488064 | bytes 4718594 | tf_op jit(solution)/shard_map/jit(_where)/select_n | solution.py:296
  82.8 1.3 collective-permute-start.6
  84.1 1.3 collective-permute-start.7
  86.1 1.8 broadcast_select_fusion.3
  87.9 1.9 collective-permute-start.26
  89.8 1.5 collective-permute-start.25
  91.4 1.2 encode.3
  93.2 1.3 collective-permute-start.14
  94.5 1.3 collective-permute-start.15
  95.8 1.3 collective-permute-start.16
  97.1 1.3 copy-done.1
  99.3 1.0 encode.4
  105.9 0.9 fusion.2.refs_15_
  107.7 1.3 collective-permute-start.30
  109.0 1.3 collective-permute-start.31
  110.3 1.3 collective-permute-start.33
  111.6 2.1 %broadcast_select_fusion = (bf16[2304,256]{1,0:T(8,128)(2,1)S(1)}, bf16[2304,256]{1,0:T(8,128)(2,1)S(1)}) fusion(pred[]{:T(512)S(6)} %eq.62, bf16[1152,256]{1,0:T(8,128)(2,1)} %collective-permute-done.24, bf16[1152,256]{1,0:T(8,128)(2,1)} %collective-permute-done.25, pred[]{:T(512)S(6)} %eq.72, bf16[1,9,256,256]{3,2,1,0:T(8,128)(2,1)S(1)} %copy-done.12), kind=kLoop, calls=%fused_computation.3 | loop fusion | flops 6488064 | bytes 4718594 | tf_op jit(solution)/shard_map/jit(_where)/select_n | solution.py:296
  115.7 2.3 %collective-permute-done.30.refs_4_ = bf16[128,256]{1,0:T(8,128)(2,1)S(1)} collective-permute-done((bf16[128,256]{1,0:T(8,128)(2,1)S(1)}, bf16[128,256]{1,0:T(8,128)(2,1)S(1)}, u32[]{:S(2)}, u32[]{:S(2)}) %collective-permute-start.30) | collective-permute-done | bytes 65568 | tf_op jit(solution)/shard_map/ppermute | solution.py:45
  126.6 69.0 %collective-permute-start.40 = (bf16[128,256]{1,0:T(8,128)(2,1)S(1)}, bf16[128,256]{1,0:T(8,128)(2,1)S(1)}, u32[]{:S(2)}, u32[]{:S(2)}) collective-permute-start(bf16[128,256]{1,0:T(8,128)(2,1)S(1)} %get-tuple-element.40), channel_id=1, source_target_pairs={{0,32},{32,0},{64,96},{96,64},{128,160},{160,128},{192,224},{224,1... | collective-permute-start | bytes 196616 | tf_op jit(solution)/shard_map/ppermute | solution.py:234
  195.7 6.4 %collective-permute-done.40 = bf16[128,256]{1,0:T(8,128)(2,1)S(1)} collective-permute-done((bf16[128,256]{1,0:T(8,128)(2,1)S(1)}, bf16[128,256]{1,0:T(8,128)(2,1)S(1)}, u32[]{:S(2)}, u32[]{:S(2)}) %collective-permute-start.40) | collective-permute-done | bytes 65568 | tf_op jit(solution)/shard_map/ppermute | solution.py:234
  (114 shorter events, 25.2 us)
Async XLA Ops:
  0.0 57.8 %collective-permute-start = (bf16[2,128,256]{2,1,0:T(8,128)(2,1)}, bf16[2,128,256]{2,1,0:T(8,128)(2,1)S(1)}, u32[]{:S(2)}, u32[]{:S(2)}) collective-permute-start(bf16[2,128,256]{2,1,0:T(8,128)(2,1)} %bitcast.45), channel_id=1, source_target_pairs={{0,1},{1,2},{2,3},{3,4},{4,5},{5,6},{6,7},{7,8},{8,9},{9,10},{10,1... | collective-permute-start | bytes 393224 | tf_op jit(solution)/shard_map/ppermute | solution.py:223
  0.8 58.5 %collective-permute-start.1 = (bf16[2,128,256]{2,1,0:T(8,128)(2,1)}, bf16[2,128,256]{2,1,0:T(8,128)(2,1)S(1)}, u32[]{:S(2)}, u32[]{:S(2)}) collective-permute-start(bf16[2,128,256]{2,1,0:T(8,128)(2,1)} %bitcast.46), channel_id=1, source_target_pairs={{1,0},{2,1},{3,2},{4,3},{5,4},{6,5},{7,6},{8,7},{9,8},{10,9},{11,1... | collective-permute-start | bytes 393224 | tf_op jit(solution)/shard_map/ppermute | solution.py:223
  3.4 57.9 %collective-permute-start.12 = (bf16[1152,256]{1,0:T(8,128)(2,1)}, bf16[1152,256]{1,0:T(8,128)(2,1)}, u32[]{:S(2)}, u32[]{:S(2)}) collective-permute-start(bf16[1152,256]{1,0:T(8,128)(2,1)} %constant_dynamic-slice_fusion.1), channel_id=1, source_target_pairs={{64,96},{96,64},{128,160},{160,128},{192,224},{224,192},{256,288},... | collective-permute-start | bytes 1769480 | tf_op jit(solution)/shard_map/ppermute | solution.py:234
  23.0 56.1 %collective-permute-start.10 = (bf16[1152,256]{1,0:T(8,128)(2,1)}, bf16[1152,256]{1,0:T(8,128)(2,1)}, u32[]{:S(2)}, u32[]{:S(2)}) collective-permute-start(bf16[1152,256]{1,0:T(8,128)(2,1)} %constant_dynamic-slice_fusion.2), channel_id=1, source_target_pairs={{64,96},{96,64},{128,160},{160,128},{192,224},{224,192},{256,288},... | collective-permute-start | bytes 1769480 | tf_op jit(solution)/shard_map/ppermute | solution.py:234
  39.9 23.0 %collective-permute-start.9 = (f32[2,256]{1,0:T(2,128)S(1)}, f32[2,256]{1,0:T(2,128)S(1)}, u32[]{:S(2)}, u32[]{:S(2)}) collective-permute-start(f32[2,256]{1,0:T(2,128)S(1)} %pad_maximum_fusion.refs_3_.refs_1_), channel_id=1, source_target_pairs={{64,96},{96,64},{128,160},{160,128},{192,224},{224,192},{256,288},... | collective-permute-start | bytes 6152 | tf_op jit(solution)/shard_map/ppermute | solution.py:234
  57.9 32.0 %collective-permute-start.24 = (bf16[1152,256]{1,0:T(8,128)(2,1)}, bf16[1152,256]{1,0:T(8,128)(2,1)}, u32[]{:S(2)}, u32[]{:S(2)}) collective-permute-start(bf16[1152,256]{1,0:T(8,128)(2,1)} %constant_dynamic-slice_fusion), channel_id=1, source_target_pairs={{256,288},{288,256},{320,352},{352,320},{384,416},{416,384},{448,4... | collective-permute-start | bytes 1769480 | tf_op jit(solution)/shard_map/ppermute | solution.py:234
  59.9 13.1 %collective-permute-start.2 = (bf16[2,256,256]{2,1,0:T(8,128)(2,1)S(1)}, bf16[2,256,256]{2,1,0:T(8,128)(2,1)S(1)}, u32[]{:S(2)}, u32[]{:S(2)}) collective-permute-start(bf16[2,256,256]{2,1,0:T(8,128)(2,1)S(1)} %shard_map.64), channel_id=1, source_target_pairs={{0,32},{1,33},{2,34},{3,35},{4,36},{5,37},{6,38},{7,39},{8,40},{9,... | collective-permute-start | bytes 786440 | tf_op jit(solution)/shard_map/ppermute | solution.py:253
  61.3 18.6 %collective-permute-start.13 = (bf16[1152,256]{1,0:T(8,128)(2,1)}, bf16[1152,256]{1,0:T(8,128)(2,1)}, u32[]{:S(2)}, u32[]{:S(2)}) collective-permute-start(bf16[1152,256]{1,0:T(8,128)(2,1)} %collective-permute-done.12), channel_id=1, source_target_pairs={{64,65},{65,64},{66,67},{67,66},{68,69},{69,68},{70,71},{71,70},{7... | collective-permute-start | bytes 1769480 | tf_op jit(solution)/shard_map/ppermute | solution.py:273
  75.8 7.0 %collective-permute-start.3 = (bf16[128,256]{1,0:T(8,128)(2,1)S(1)}, bf16[128,256]{1,0:T(8,128)(2,1)S(1)}, u32[]{:S(2)}, u32[]{:S(2)}) collective-permute-start(bf16[128,256]{1,0:T(8,128)(2,1)S(1)} %get-tuple-element.42), channel_id=1, source_target_pairs={{32,97},{33,98},{34,99},{35,100},{36,101},{37,102},{38,103},{39,10... | collective-permute-start | bytes 196616 | tf_op jit(solution)/shard_map/ppermute | solution.py:258
  77.1 7.0 %collective-permute-start.4 = (bf16[128,256]{1,0:T(8,128)(2,1)S(1)}, bf16[128,256]{1,0:T(8,128)(2,1)S(1)}, u32[]{:S(2)}, u32[]{:S(2)}) collective-permute-start(bf16[128,256]{1,0:T(8,128)(2,1)S(1)} %get-tuple-element.42), channel_id=1, source_target_pairs={{32,96},{33,97},{34,98},{35,99},{36,100},{37,101},{38,102},{39,103... | collective-permute-start | bytes 196616 | tf_op jit(solution)/shard_map/ppermute | solution.py:258
  79.1 8.8 %collective-permute-start.5 = (bf16[128,256]{1,0:T(8,128)(2,1)S(1)}, bf16[128,256]{1,0:T(8,128)(2,1)S(1)}, u32[]{:S(2)}, u32[]{:S(2)}) collective-permute-start(bf16[128,256]{1,0:T(8,128)(2,1)S(1)} %get-tuple-element.42), channel_id=1, source_target_pairs={{33,96},{34,97},{35,98},{36,99},{37,100},{38,101},{39,102},{40,103... | collective-permute-start | bytes 196616 | tf_op jit(solution)/shard_map/ppermute | solution.py:258
  79.9 5.5 %collective-permute-start.11 = (bf16[1152,256]{1,0:T(8,128)(2,1)}, bf16[1152,256]{1,0:T(8,128)(2,1)S(1)}, u32[]{:S(2)}, u32[]{:S(2)}) collective-permute-start(bf16[1152,256]{1,0:T(8,128)(2,1)} %collective-permute-done.10), channel_id=1, source_target_pairs={{64,65},{65,64},{66,67},{67,66},{68,69},{69,68},{70,71},{71,70},{7... | collective-permute-start | bytes 1769480 | tf_op jit(solution)/shard_map/ppermute | solution.py:273
  82.8 8.5 %collective-permute-start.6 = (bf16[128,256]{1,0:T(8,128)(2,1)S(1)}, bf16[128,256]{1,0:T(8,128)(2,1)S(1)}, u32[]{:S(2)}, u32[]{:S(2)}) collective-permute-start(bf16[128,256]{1,0:T(8,128)(2,1)S(1)} %get-tuple-element.41), channel_id=1, source_target_pairs={{32,65},{33,66},{34,67},{35,68},{36,69},{37,70},{38,71},{39,72},{4... | collective-permute-start | bytes 196616 | tf_op jit(solution)/shard_map/ppermute | solution.py:258
  84.1 7.2 %collective-permute-start.7 = (bf16[128,256]{1,0:T(8,128)(2,1)S(1)}, bf16[128,256]{1,0:T(8,128)(2,1)S(1)}, u32[]{:S(2)}, u32[]{:S(2)}) collective-permute-start(bf16[128,256]{1,0:T(8,128)(2,1)S(1)} %get-tuple-element.41), channel_id=1, source_target_pairs={{32,64},{33,65},{34,66},{35,67},{36,68},{37,69},{38,70},{39,71},{4... | collective-permute-start | bytes 196616 | tf_op jit(solution)/shard_map/ppermute | solution.py:258
  85.4 5.9 %collective-permute-start.8 = (bf16[128,256]{1,0:T(8,128)(2,1)S(1)}, bf16[128,256]{1,0:T(8,128)(2,1)S(1)}, u32[]{:S(2)}, u32[]{:S(2)}) collective-permute-start(bf16[128,256]{1,0:T(8,128)(2,1)S(1)} %get-tuple-element.41), channel_id=1, source_target_pairs={{33,64},{34,65},{35,66},{36,67},{37,68},{38,69},{39,70},{40,71},{4... | collective-permute-start | bytes 196616 | tf_op jit(solution)/shard_map/ppermute | solution.py:258
  87.9 17.3 %collective-permute-start.26 = (bf16[256,256]{1,0:T(8,128)(2,1)}, bf16[256,256]{1,0:T(8,128)(2,1)}, u32[]{:S(2)}, u32[]{:S(2)}) collective-permute-start(bf16[256,256]{1,0:T(8,128)(2,1)} %fusion), channel_id=1, source_target_pairs={{0,32},{32,0},{1,33},{33,1},{2,34},{34,2},{3,35},{35,3},{4,36},{36... | collective-permute-start | bytes 393224 | tf_op jit(solution)/shard_map/ppermute | solution.py:234
  89.8 17.9 %collective-permute-start.25 = (bf16[1152,256]{1,0:T(8,128)(2,1)}, bf16[1152,256]{1,0:T(8,128)(2,1)}, u32[]{:S(2)}, u32[]{:S(2)}) collective-permute-start(bf16[1152,256]{1,0:T(8,128)(2,1)} %collective-permute-done.24), channel_id=1, source_target_pairs={{256,257},{257,256},{258,259},{259,258},{260,261},{261,260},{262,2... | collective-permute-start | bytes 1769480 | tf_op jit(solution)/shard_map/ppermute | solution.py:273
  93.2 3.9 %collective-permute-start.14 = (bf16[128,256]{1,0:T(8,128)(2,1)}, bf16[128,256]{1,0:T(8,128)(2,1)}, u32[]{:S(2)}, u32[]{:S(2)}) collective-permute-start(bf16[128,256]{1,0:T(8,128)(2,1)} %get-tuple-element.19.refs_10_), channel_id=1, source_target_pairs={{96,129},{97,130},{98,131},{99,132},{100,133},{101,134},{102,135},... | collective-permute-start | bytes 196616 | tf_op jit(solution)/shard_map/ppermute | solution.py:45
  94.5 2.6 %collective-permute-start.15 = (bf16[128,256]{1,0:T(8,128)(2,1)}, bf16[128,256]{1,0:T(8,128)(2,1)}, u32[]{:S(2)}, u32[]{:S(2)}) collective-permute-start(bf16[128,256]{1,0:T(8,128)(2,1)} %get-tuple-element.19.refs_10_), channel_id=1, source_target_pairs={{96,128},{97,129},{98,130},{99,131},{100,132},{101,133},{102,134},... | collective-permute-start | bytes 196616 | tf_op jit(solution)/shard_map/ppermute | solution.py:45
  103.0 6.0 %collective-permute-start.20 = (bf16[128,256]{1,0:T(8,128)(2,1)S(1)}, bf16[128,256]{1,0:T(8,128)(2,1)S(1)}, u32[]{:S(2)}, u32[]{:S(2)}) collective-permute-start(bf16[128,256]{1,0:T(8,128)(2,1)S(1)} %get-tuple-element.23), channel_id=1, source_target_pairs={{224,257},{225,258},{226,259},{227,260},{228,261},{229,262},{230,2... | collective-permute-start | bytes 196616 | tf_op jit(solution)/shard_map/ppermute | solution.py:45
  103.7 6.7 %collective-permute-start.21 = (bf16[128,256]{1,0:T(8,128)(2,1)S(1)}, bf16[128,256]{1,0:T(8,128)(2,1)S(1)}, u32[]{:S(2)}, u32[]{:S(2)}) collective-permute-start(bf16[128,256]{1,0:T(8,128)(2,1)S(1)} %get-tuple-element.23), channel_id=1, source_target_pairs={{224,256},{225,257},{226,258},{227,259},{228,260},{229,261},{230,2... | collective-permute-start | bytes 196616 | tf_op jit(solution)/shard_map/ppermute | solution.py:45
  104.5 9.3 %collective-permute-start.22 = (bf16[128,256]{1,0:T(8,128)(2,1)S(1)}, bf16[128,256]{1,0:T(8,128)(2,1)S(1)}, u32[]{:S(2)}, u32[]{:S(2)}) collective-permute-start(bf16[128,256]{1,0:T(8,128)(2,1)S(1)} %get-tuple-element.23), channel_id=1, source_target_pairs={{225,256},{226,257},{227,258},{228,259},{229,260},{230,261},{231,2... | collective-permute-start | bytes 196616 | tf_op jit(solution)/shard_map/ppermute | solution.py:45
  105.2 9.3 %collective-permute-start.23 = (bf16[256,256]{1,0:T(8,128)(2,1)S(1)}, bf16[256,256]{1,0:T(8,128)(2,1)S(1)}, u32[]{:S(2)}, u32[]{:S(2)}) collective-permute-start(bf16[256,256]{1,0:T(8,128)(2,1)S(1)} %get-tuple-element.24), channel_id=1, source_target_pairs={{224,256},{225,257},{226,258},{227,259},{228,260},{229,261},{230,2... | collective-permute-start | bytes 393224 | tf_op jit(solution)/shard_map/ppermute | solution.py:45
  107.7 10.3 %collective-permute-start.30 = (bf16[128,256]{1,0:T(8,128)(2,1)S(1)}, bf16[128,256]{1,0:T(8,128)(2,1)S(1)}, u32[]{:S(2)}, u32[]{:S(2)}) collective-permute-start(bf16[128,256]{1,0:T(8,128)(2,1)S(1)} %fusion.3.refs_16_), channel_id=1, source_target_pairs={{0,481},{1,482},{2,483},{3,484},{4,485},{5,486},{6,487},{7,488},{8... | collective-permute-start | bytes 196616 | tf_op jit(solution)/shard_map/ppermute | solution.py:45
  109.0 10.2 %collective-permute-start.31 = (bf16[128,256]{1,0:T(8,128)(2,1)S(1)}, bf16[128,256]{1,0:T(8,128)(2,1)S(1)}, u32[]{:S(2)}, u32[]{:S(2)}) collective-permute-start(bf16[128,256]{1,0:T(8,128)(2,1)S(1)} %fusion.3.refs_16_), channel_id=1, source_target_pairs={{0,480},{1,481},{2,482},{3,483},{4,484},{5,485},{6,486},{7,487},{8... | collective-permute-start | bytes 196616 | tf_op jit(solution)/shard_map/ppermute | solution.py:45
  110.3 10.3 %collective-permute-start.33 = (bf16[256,256]{1,0:T(8,128)(2,1)S(1)}, bf16[256,256]{1,0:T(8,128)(2,1)S(1)}, u32[]{:S(2)}, u32[]{:S(2)}) collective-permute-start(bf16[256,256]{1,0:T(8,128)(2,1)S(1)} %fusion.2.refs_15_), channel_id=1, source_target_pairs={{0,480},{1,481},{2,482},{3,483},{4,484},{5,485},{6,486},{7,487},{8... | collective-permute-start | bytes 393224 | tf_op jit(solution)/shard_map/ppermute | solution.py:45
  113.8 6.2 %collective-permute-start.32 = (bf16[128,256]{1,0:T(8,128)(2,1)S(1)}, bf16[128,256]{1,0:T(8,128)(2,1)S(1)}, u32[]{:S(2)}, u32[]{:S(2)}) collective-permute-start(bf16[128,256]{1,0:T(8,128)(2,1)S(1)} %fusion.3.refs_16_), channel_id=1, source_target_pairs={{1,480},{2,481},{3,482},{4,483},{5,484},{6,485},{7,486},{8,487},{9... | collective-permute-start | bytes 196616 | tf_op jit(solution)/shard_map/ppermute | solution.py:45
  115.1 5.6 %collective-permute-start.27 = (bf16[128,256]{1,0:T(8,128)(2,1)S(1)}, bf16[128,256]{1,0:T(8,128)(2,1)S(1)}, u32[]{:S(2)}, u32[]{:S(2)}) collective-permute-start(bf16[128,256]{1,0:T(8,128)(2,1)S(1)} %get-tuple-element.25.refs_16_), channel_id=1, source_target_pairs={{256,353},{257,354},{258,355},{259,356},{260,357},{261,358},{262,3... | collective-permute-start | bytes 196616 | tf_op jit(solution)/shard_map/ppermute | solution.py:45
  118.1 2.6 %collective-permute-start.28 = (bf16[128,256]{1,0:T(8,128)(2,1)S(1)}, bf16[128,256]{1,0:T(8,128)(2,1)S(1)}, u32[]{:S(2)}, u32[]{:S(2)}) collective-permute-start(bf16[128,256]{1,0:T(8,128)(2,1)S(1)} %get-tuple-element.25.refs_16_), channel_id=1, source_target_pairs={{256,352},{257,353},{258,354},{259,355},{260,356},{261,357},{262,3... | collective-permute-start | bytes 196616 | tf_op jit(solution)/shard_map/ppermute | solution.py:45
  121.2 2.1 %collective-permute-start.34 = (bf16[128,256]{1,0:T(8,128)(2,1)S(1)}, bf16[128,256]{1,0:T(8,128)(2,1)S(1)}, u32[]{:S(2)}, u32[]{:S(2)}) collective-permute-start(bf16[128,256]{1,0:T(8,128)(2,1)S(1)} %get-tuple-element.27.refs_16_), channel_id=1, source_target_pairs={{352,385},{353,386},{354,387},{355,388},{356,389},{357,390},{358,3... | collective-permute-start | bytes 196616 | tf_op jit(solution)/shard_map/ppermute | solution.py:45
  123.9 2.1 %collective-permute-start.37 = (bf16[128,256]{1,0:T(8,128)(2,1)S(1)}, bf16[128,256]{1,0:T(8,128)(2,1)S(1)}, u32[]{:S(2)}, u32[]{:S(2)}) collective-permute-start(bf16[128,256]{1,0:T(8,128)(2,1)S(1)} %get-tuple-element.29.refs_16_), channel_id=1, source_target_pairs={{384,481},{385,482},{386,483},{387,484},{388,485},{389,486},{390,4... | collective-permute-start | bytes 196616 | tf_op jit(solution)/shard_map/ppermute | solution.py:45
  126.6 75.4 %collective-permute-start.40 = (bf16[128,256]{1,0:T(8,128)(2,1)S(1)}, bf16[128,256]{1,0:T(8,128)(2,1)S(1)}, u32[]{:S(2)}, u32[]{:S(2)}) collective-permute-start(bf16[128,256]{1,0:T(8,128)(2,1)S(1)} %get-tuple-element.40), channel_id=1, source_target_pairs={{0,32},{32,0},{64,96},{96,64},{128,160},{160,128},{192,224},{224,1... | collective-permute-start | bytes 196616 | tf_op jit(solution)/shard_map/ppermute | solution.py:234
  (24 other events, 238.9 us)
where the time goes:
time: 204 us; the launch traced here: 203 us
  starting transfers between devices  156 us (76%)
  waiting for transfers between devices  20.2 us (10%)
  other arithmetic  9.96 us (5%)
  Pallas kernels  8.27 us (4%)
  local copies, waits for them, and re-layouts  7.59 us (4%)
    ppermute x6, starting transfers between devices, partner(): return lax.ppermute(block, 'section', [(i, i ^ 1) for i in sections])  124 us
    ppermute x23, starting transfers between devices, send(): return lax.ppermute(block, JOINT, route(moves))  19.2 us
    ppermute x1, waiting for transfers between devices, body(): handed = lax.ppermute(wide, JOINT, [(p, STRIPS + p) for p in range(STRIPS)])  10.2 us
    ppermute x6, starting transfers between devices, body(): lax.ppermute(close[to], JOINT, [(STRIPS + p, place(1, to) * STRIPS + p +...  6.62 us
    ppermute x6, waiting for transfers between devices, partner(): return lax.ppermute(block, 'section', [(i, i ^ 1) for i in sections])  6.4 us
    select_n x3, other arithmetic, joined(): jnp.where(parity == 0, remote, mine)  6.06 us
    pallas_call x7, Pallas kernels, call(): pl.pallas_call(kernel, out_shape=(jax.ShapeDtypeStruct((2 * BLOCK, CH), B...  5 us
    dynamic_slice x3, local copies, waits for them, and re-layouts, body(): lax.dynamic_slice_in_dim(w, core * HALF, HALF, axis=0)  4.69 us
  transfers between devices with their start and end apart: 41, of which 5 were waited for; matrix products, arithmetic and copies ran while one was open for 7% of the time, Pallas kernels for 3%

commit v1 on v0

--- a/solution.py
+++ b/solution.py
@@ -123,7 +123,7 @@
     return call
 
 
-def phase_kernel(decoder, doubled=False):
+def phase_kernel(decoder, doubled=False, shared=False):
     kinds = 3 if decoder else 2
 
     def kernel(*refs):
@@ -131,12 +131,14 @@
         info = refs.pop(0)
         xs = [refs.pop(0) for _ in range(6 if doubled else 3)]
         if decoder:
-            skip_wide = [refs.pop(0) for _ in range(3)]
-            skip_narrow = refs.pop(0)
+            skips = xs if shared else [refs.pop(0) for _ in range(3)]
+            skip_narrow = skips[1].at[0 : 2 * BLOCK]
+            skip_wide = [skips[0], skips[1].at[2 * BLOCK : 3 * BLOCK], skips[2]]
+        if shared:
+            xs = skip_wide
         bias = refs.pop(0)
         weights = [refs.pop(0) for _ in range(2 * kinds)]
         prev0 = refs.pop(0)
-        prev1 = refs.pop(0)
         out0 = refs.pop(0)
         out1 = refs.pop(0)
         work = refs.pop(0)
@@ -149,7 +151,7 @@
         @pl.when(active == 0)
         def _():
             out0[...] = prev0[...]
-            out1[...] = prev1[...]
+            out1[...] = prev0[2 * BLOCK : 3 * BLOCK]
 
         @pl.when(active != 0)
         def _():
@@ -179,13 +181,14 @@
                     top + start + 1,
                 )
                 if section == 0:
-                    out0[...] = value.astype(BF16)
+                    out0[0 : 2 * BLOCK] = value.astype(BF16)
                     spread(work, 0, value, rows - 2)
                 else:
+                    out0[2 * BLOCK : 3 * BLOCK] = value.astype(BF16)
                     out1[...] = value.astype(BF16)
 
-    def call(info, xs, skips, bias, weights, prev0, prev1):
-        operands = [info, *xs, *skips, bias, *weights, prev0, prev1]
+    def call(info, xs, skips, bias, weights, prev0):
+        operands = [info, *xs, *skips, bias, *weights, prev0]
         vmem = pl.BlockSpec(memory_space=pltpu.VMEM)
         specs = [pl.BlockSpec(memory_space=pltpu.SMEM)] + [vmem] * (len(operands) - 1)
         scratch = [pltpu.VMEM((3 * BLOCK, 3 * CH), BF16)]
@@ -194,7 +197,7 @@
         return pl.pallas_call(
             kernel,
             out_shape=(
-                jax.ShapeDtypeStruct((2 * BLOCK, CH), BF16),
+                jax.ShapeDtypeStruct((3 * BLOCK, CH), BF16),
                 jax.ShapeDtypeStruct((BLOCK, CH), BF16),
             ),
             in_specs=specs,
@@ -237,11 +240,10 @@
     image = images.reshape(2, BLOCK, CH)
     below = shift_in_section(image, 0, -1)
     above = shift_in_section(image, 0, 1)
-    other = partner(both, pairs_from)
+    other = partner(both)
     halves = [lax.dynamic_slice_in_dim(w, core * HALF, HALF, axis=0) for w in own]
     fetched = [
-        partner(halves[0], pairs_from),
-        partner(halves[1], pairs_from),
+        partner(jnp.concatenate(halves[:2], axis=0), pairs_from),
         partner(halves[2], decoders),
     ]
 
@@ -266,8 +268,11 @@
             )
     give = jnp.where(parity == 0, wide[1], jnp.concatenate([close[0], close[0]], axis=0))
     got = partner(give, range(2))
-    level0 = jnp.where(parity == 0, wide[0], got)
-    level1 = jnp.where(parity == 0, got[:BLOCK], close[1])
+    level = jnp.where(
+        parity == 0,
+        jnp.concatenate([wide[0], got[:BLOCK]], axis=0),
+        jnp.concatenate([got, close[1]], axis=0),
+    )
 
     swapped = [
         lax.ppermute(
@@ -275,7 +280,7 @@
             JOINT,
             [
                 (s * STRIPS + a, s * STRIPS + b)
-                for s in (decoders if index == 2 else pairs_from)
+                for s in (decoders if index == 1 else pairs_from)
                 for a, b in cores
             ],
         )
@@ -295,7 +300,11 @@
         )
         return jnp.where(parity == 0, mine, remote), jnp.where(parity == 0, remote, mine)
 
-    by_kind = [joined(*parts) for parts in zip(own, fetched, swapped)]
+    by_kind = [
+        joined(own[0], fetched[0][:HALF], swapped[0][:HALF]),
+        joined(own[1], fetched[0][HALF:], swapped[0][HALF:]),
+        joined(own[2], fetched[1], swapped[1]),
+    ]
     all_weights = [pair[0] for pair in by_kind] + [pair[1] for pair in by_kind]
     encode_weights = all_weights[0:2] + all_weights[3:5]
 
@@ -303,34 +312,38 @@
         active = (group == phase).astype(jnp.int32)
         return jnp.stack([active, strip * ROWS, micro]).astype(jnp.int32)
 
-    decode = phase_kernel(True)
-    out0 = jnp.zeros((2 * BLOCK, CH), BF16)
-    out1 = jnp.zeros((BLOCK, CH), BF16)
+    kept = jnp.zeros((3 * BLOCK, CH), BF16)
     middle = GROUPS // 2
 
-    def onward(block, phase):
-        pieces = {d: send(block, [(phase, phase + 1, d)]) for d in (1, -1, 0)}
-        return (pieces[1], pieces[0], pieces[-1])
+    def onward(last, phase, centre=None):
+        down = send(last, [(phase, phase + 1, 1)])
+        up = send(last, [(phase, phase + 1, -1)])
+        straight = send(last if centre is None else centre, [(phase, phase + 1, 0)])
+        return (down, straight, up)
 
     for phase in range(1, middle):
-        encode = phase_kernel(False, phase == 1)
-        out0, out1 = encode(info_of(phase), xs, (), bias, encode_weights, out0, out1)
-        xs = onward(out1, phase)
+        encode = phase_kernel(False, doubled=phase == 1)
+        kept, last = encode(info_of(phase), xs, (), bias, encode_weights, kept)
+        xs = onward(last, phase, kept if phase + 1 == middle else None)
     mirror = [(g, GROUPS - 1 - g) for g in range(middle - 1)]
-    narrow = send(out0, [(middle - 1, middle, 0)])
-    out0 = jnp.where(group == 0, level0, out0)
-    out1 = jnp.where(group == 0, level1, out1)
-    late_wide = tuple(send(out1, [(a, b, shift) for a, b in mirror]) for shift in (1, 0, -1))
-    late_narrow = send(out0, [(a, b, 0) for a, b in mirror])
+    kept = jnp.where(group == 0, level, kept)
+    last = jnp.where(group == 0, level[2 * BLOCK :], last)
+    late = tuple(
+        send(kept if shift == 0 else last, [(a, b, shift) for a, b in mirror])
+        for shift in (1, 0, -1)
+    )
     for phase in range(middle, GROUPS):
-        skips = (*xs, narrow) if phase == middle else (*late_wide, late_narrow)
-        out0, out1 = decode(info_of(phase), xs, skips, bias, all_weights, out0, out1)
+        shared = phase == middle
+        decode = phase_kernel(True, shared=shared)
+        kept, last = decode(
+            info_of(phase), xs, () if shared else late, bias, all_weights, kept
+        )
         if phase + 1 < GROUPS:
-            xs = onward(out1, phase)
-
-    inner = out0[BLOCK // 2 : BLOCK // 2 + BLOCK]
-    mine = jnp.where(parity == 0, inner, out1)
-    theirs = partner(jnp.where(parity == 0, out1, inner))
+            xs = onward(last, phase)
+
+    inner = kept[BLOCK // 2 : BLOCK // 2 + BLOCK]
+    mine = jnp.where(parity == 0, inner, last)
+    theirs = partner(jnp.where(parity == 0, last, inner))
     result = jnp.where(
         micro == 0, jnp.stack([mine, theirs]), jnp.stack([theirs, mine])
     )

time: 204 us -> 149 us (0.73)
  the two profiles are of different devices: /device:TPU:2 before, /device:TPU:253 now
where the time goes in v1:
time: 149 us; the launch traced here: 148 us
  waiting for transfers between devices  86.3 us (58%)
  starting transfers between devices  41.3 us (28%)
  Pallas kernels  8.72 us (6%)
  other arithmetic  5.83 us (4%)
  local copies, waits for them, and re-layouts  5.01 us (3%)
    ppermute x21, waiting for transfers between devices, send(): return lax.ppermute(block, JOINT, route(moves))  64.5 us
    ppermute x5, waiting for transfers between devices, partner(): return lax.ppermute(block, 'section', [(i, i ^ 1) for i in sections])  21.8 us
    ppermute x21, starting transfers between devices, send(): return lax.ppermute(block, JOINT, route(moves))  18 us
    ppermute x5, starting transfers between devices, partner(): return lax.ppermute(block, 'section', [(i, i ^ 1) for i in sections])  10.8 us
    pallas_call x7, Pallas kernels, call(): pl.pallas_call(kernel, out_shape=(jax.ShapeDtypeStruct((3 * BLOCK, CH), B...  7.58 us
    ppermute x2, starting transfers between devices, body(): lax.ppermute(half, JOINT, [(s * STRIPS + a, s * STRIPS + b) for s in (dec...  6.48 us
    ppermute x6, starting transfers between devices, body(): lax.ppermute(close[to], JOINT, [(STRIPS + p, place(1, to) * STRIPS + p +...  3.99 us
    select_n x3, other arithmetic, joined(): jnp.where(parity == 0, remote, mine)  3.17 us
  transfers between devices with their start and end apart: 37, of which 6 were waited for; matrix products, arithmetic and copies ran while one was open for 5% of the time, Pallas kernels for 2%

profile of v1, /device:TPU:253, one launch (start us, length us, event | category | flops | bytes accessed | tf_op | source)
XLA Modules:
  0.0 147.9 jit_solution(17784797460618291947)
XLA Ops:
  0.0 1.4 constant_dynamic-slice_fusion.1
  1.5 1.1 pad_maximum_fusion
  2.6 2.9 %collective-permute-start.10 = (bf16[2304,256]{1,0:T(8,128)(2,1)}, bf16[2304,256]{1,0:T(8,128)(2,1)}, u32[]{:S(2)}, u32[]{:S(2)}) collective-permute-start(bf16[2304,256]{1,0:T(8,128)(2,1)} %pad_maximum_fusion), channel_id=1, source_target_pairs={{64,96},{96,64},{128,160},{160,128},{192,224},{224,192},{256,288},... | collective-permute-start | bytes 3538952 | tf_op jit(solution)/shard_map/ppermute | solution.py:237
  5.5 0.7 collective-permute-start
  6.9 2.5 %collective-permute-start.9 = (f32[2,256]{1,0:T(2,128)S(1)}, f32[2,256]{1,0:T(2,128)S(1)}, u32[]{:S(2)}, u32[]{:S(2)}) collective-permute-start(f32[2,256]{1,0:T(2,128)S(1)} %pad_maximum_fusion.1.refs_3_.refs_1_), channel_id=1, source_target_pairs={{0,32},{32,0},{64,96},{96,64},{128,160},{160,128},{192,224},{224,1... | collective-permute-start | bytes 6152 | tf_op jit(solution)/shard_map/ppermute | solution.py:237
  9.4 0.9 constant_dynamic-slice_fusion
  10.3 2.8 %collective-permute-start.21 = (bf16[1152,256]{1,0:T(8,128)(2,1)}, bf16[1152,256]{1,0:T(8,128)(2,1)}, u32[]{:S(2)}, u32[]{:S(2)}) collective-permute-start(bf16[1152,256]{1,0:T(8,128)(2,1)} %constant_dynamic-slice_fusion), channel_id=1, source_target_pairs={{256,288},{288,256},{320,352},{352,320},{384,416},{416,384},{448,4... | collective-permute-start | bytes 1769480 | tf_op jit(solution)/shard_map/ppermute | solution.py:237
  13.4 18.4 %collective-permute-done.10 = bf16[2304,256]{1,0:T(8,128)(2,1)} collective-permute-done((bf16[2304,256]{1,0:T(8,128)(2,1)}, bf16[2304,256]{1,0:T(8,128)(2,1)}, u32[]{:S(2)}, u32[]{:S(2)}) %collective-permute-start.10) | collective-permute-done | bytes 1179680 | tf_op jit(solution)/shard_map/ppermute | solution.py:237
  31.8 4.6 %collective-permute-start.11 = (bf16[2304,256]{1,0:T(8,128)(2,1)}, bf16[2304,256]{1,0:T(8,128)(2,1)}, u32[]{:S(2)}, u32[]{:S(2)}) collective-permute-start(bf16[2304,256]{1,0:T(8,128)(2,1)} %collective-permute-done.10), channel_id=1, source_target_pairs={{64,65},{65,64},{66,67},{67,66},{68,69},{69,68},{70,71},{71,70},{7... | collective-permute-start | bytes 3538952 | tf_op jit(solution)/shard_map/ppermute | solution.py:278
  37.0 0.7 collective-permute-start.2
  40.5 1.3 fusion.2
  42.5 1.3 fusion.1
  43.8 0.7 broadcast_select_fusion.2
  45.9 0.7 broadcast_select_fusion.3
  49.9 1.9 %collective-permute-start.22 = (bf16[1152,256]{1,0:T(8,128)(2,1)}, bf16[1152,256]{1,0:T(8,128)(2,1)S(1)}, u32[]{:S(2)}, u32[]{:S(2)}) collective-permute-start(bf16[1152,256]{1,0:T(8,128)(2,1)} %collective-permute-done.21), channel_id=1, source_target_pairs={{256,257},{257,256},{258,259},{259,258},{260,261},{261,260},{262,2... | collective-permute-start | bytes 1769480 | tf_op jit(solution)/shard_map/ppermute | solution.py:278
  55.2 0.8 collective-permute-start.18
  56.6 0.9 collective-permute-start.19
  57.6 1.3 collective-permute-start.27
  58.9 1.3 collective-permute-start.28
  60.2 1.8 %broadcast_select_fusion = (bf16[2304,256]{1,0:T(8,128)(2,1)S(1)}, bf16[2304,256]{1,0:T(8,128)(2,1)S(1)}) fusion(pred[]{:T(512)S(6)} %eq.61, bf16[1152,256]{1,0:T(8,128)(2,1)} %collective-permute-done.21, bf16[1152,256]{1,0:T(8,128)(2,1)S(1)} %collective-permute-done.22, pred[]{:T(512)S(6)} %eq.71, bf16[1,9,256,256]{3,2,1,0:T(8,128)(2,1)S(1)} %copy-done.4), kind=kLoop, calls=%fused_computation.4 | loop fusion | flops 6488064 | bytes 4718594 | tf_op jit(solution)/shard_map/jit(_where)/select_n | solution.py:301
  62.1 1.3 collective-permute-start.29
  65.3 4.5 %collective-permute-done.27.refs_4_ = bf16[128,256]{1,0:T(8,128)(2,1)S(1)} collective-permute-done((bf16[128,256]{1,0:T(8,128)(2,1)S(1)}, bf16[128,256]{1,0:T(8,128)(2,1)S(1)}, u32[]{:S(2)}, u32[]{:S(2)}) %collective-permute-start.27) | collective-permute-done | bytes 65568 | tf_op jit(solution)/shard_map/ppermute | solution.py:45
  70.5 14.0 %collective-permute-done.29.refs_6_ = bf16[128,256]{1,0:T(8,128)(2,1)S(1)} collective-permute-done((bf16[128,256]{1,0:T(8,128)(2,1)S(1)}, bf16[128,256]{1,0:T(8,128)(2,1)S(1)}, u32[]{:S(2)}, u32[]{:S(2)}) %collective-permute-start.29) | collective-permute-done | bytes 65568 | tf_op jit(solution)/shard_map/ppermute | solution.py:45
  87.8 1.3 collective-permute-start.33
  89.1 1.3 collective-permute-start.34
  90.4 1.3 collective-permute-start.35
  91.8 43.3 %collective-permute-done.33.refs_1_ = bf16[128,256]{1,0:T(8,128)(2,1)S(1)} collective-permute-done((bf16[128,256]{1,0:T(8,128)(2,1)S(1)}, bf16[128,256]{1,0:T(8,128)(2,1)S(1)}, u32[]{:S(2)}, u32[]{:S(2)}) %collective-permute-start.33) | collective-permute-done | bytes 65568 | tf_op jit(solution)/shard_map/ppermute | solution.py:45
  135.1 2.7 %collective-permute-done.35.refs_3_ = bf16[128,256]{1,0:T(8,128)(2,1)S(1)} collective-permute-done((bf16[128,256]{1,0:T(8,128)(2,1)S(1)}, bf16[128,256]{1,0:T(8,128)(2,1)S(1)}, u32[]{:S(2)}, u32[]{:S(2)}) %collective-permute-start.35) | collective-permute-done | bytes 65568 | tf_op jit(solution)/shard_map/ppermute | solution.py:45
  137.8 4.2 %decode.7 = (bf16[384,256]{1,0:T(8,128)(2,1)S(1)}, bf16[128,256]{1,0:T(8,128)(2,1)S(1)}) custom-call(s32[3]{0:T(128)S(1)} %add_add_fusion.refs_0_, bf16[128,256]{1,0:T(8,128)(2,1)S(1)} %collective-permute-done.33.refs_1_, bf16[128,256]{1,0:T(8,128)(2,1)S(1)} %collective-permute-done.34.refs_2_, bf16[128,256]{1,0:T(8,128)(2,1)S(1)} %collective-permute-done.35.refs_3_, ...), custom_call_target="tpu_custom_call" | custom-call | tf_op jit(solution)/shard_map/decode/pallas_call | solution.py:197
  141.9 1.9 %collective-permute-start.36 = (bf16[128,256]{1,0:T(8,128)(2,1)S(1)}, bf16[128,256]{1,0:T(8,128)(2,1)S(1)}, u32[]{:S(2)}, u32[]{:S(2)}) collective-permute-start(bf16[128,256]{1,0:T(8,128)(2,1)S(1)} %get-tuple-element.46), channel_id=1, source_target_pairs={{0,32},{32,0},{64,96},{96,64},{128,160},{160,128},{192,224},{224,1... | collective-permute-start | bytes 196616 | tf_op jit(solution)/shard_map/ppermute | solution.py:237
  143.9 3.4 %collective-permute-done.36 = bf16[128,256]{1,0:T(8,128)(2,1)S(1)} collective-permute-done((bf16[128,256]{1,0:T(8,128)(2,1)S(1)}, bf16[128,256]{1,0:T(8,128)(2,1)S(1)}, u32[]{:S(2)}, u32[]{:S(2)}) %collective-permute-start.36) | collective-permute-done | bytes 65568 | tf_op jit(solution)/shard_map/ppermute | solution.py:237
  147.2 0.7 maximum_select_fusion.4
  (93 shorter events, 19.6 us)
Async XLA Ops:
  2.6 29.2 %collective-permute-start.10 = (bf16[2304,256]{1,0:T(8,128)(2,1)}, bf16[2304,256]{1,0:T(8,128)(2,1)}, u32[]{:S(2)}, u32[]{:S(2)}) collective-permute-start(bf16[2304,256]{1,0:T(8,128)(2,1)} %pad_maximum_fusion), channel_id=1, source_target_pairs={{64,96},{96,64},{128,160},{160,128},{192,224},{224,192},{256,288},... | collective-permute-start | bytes 3538952 | tf_op jit(solution)/shard_map/ppermute | solution.py:237
  5.5 30.9 %collective-permute-start = (bf16[2,128,256]{2,1,0:T(8,128)(2,1)S(1)}, bf16[2,128,256]{2,1,0:T(8,128)(2,1)S(1)}, u32[]{:S(2)}, u32[]{:S(2)}) collective-permute-start(bf16[2,128,256]{2,1,0:T(8,128)(2,1)S(1)} %bitcast.39), channel_id=1, source_target_pairs={{0,1},{1,2},{2,3},{3,4},{4,5},{5,6},{6,7},{7,8},{8,9},{9,10},{10,1... | collective-permute-start | bytes 393224 | tf_op jit(solution)/shard_map/ppermute | solution.py:226
  6.2 30.2 %collective-permute-start.1 = (bf16[2,128,256]{2,1,0:T(8,128)(2,1)S(1)}, bf16[2,128,256]{2,1,0:T(8,128)(2,1)S(1)}, u32[]{:S(2)}, u32[]{:S(2)}) collective-permute-start(bf16[2,128,256]{2,1,0:T(8,128)(2,1)S(1)} %bitcast.40), channel_id=1, source_target_pairs={{1,0},{2,1},{3,2},{4,3},{5,4},{6,5},{7,6},{8,7},{9,8},{10,9},{11,1... | collective-permute-start | bytes 393224 | tf_op jit(solution)/shard_map/ppermute | solution.py:226
  6.9 30.9 %collective-permute-start.9 = (f32[2,256]{1,0:T(2,128)S(1)}, f32[2,256]{1,0:T(2,128)S(1)}, u32[]{:S(2)}, u32[]{:S(2)}) collective-permute-start(f32[2,256]{1,0:T(2,128)S(1)} %pad_maximum_fusion.1.refs_3_.refs_1_), channel_id=1, source_target_pairs={{0,32},{32,0},{64,96},{96,64},{128,160},{160,128},{192,224},{224,1... | collective-permute-start | bytes 6152 | tf_op jit(solution)/shard_map/ppermute | solution.py:237
  10.3 39.7 %collective-permute-start.21 = (bf16[1152,256]{1,0:T(8,128)(2,1)}, bf16[1152,256]{1,0:T(8,128)(2,1)}, u32[]{:S(2)}, u32[]{:S(2)}) collective-permute-start(bf16[1152,256]{1,0:T(8,128)(2,1)} %constant_dynamic-slice_fusion), channel_id=1, source_target_pairs={{256,288},{288,256},{320,352},{352,320},{384,416},{416,384},{448,4... | collective-permute-start | bytes 1769480 | tf_op jit(solution)/shard_map/ppermute | solution.py:237
  31.8 10.1 %collective-permute-start.11 = (bf16[2304,256]{1,0:T(8,128)(2,1)}, bf16[2304,256]{1,0:T(8,128)(2,1)}, u32[]{:S(2)}, u32[]{:S(2)}) collective-permute-start(bf16[2304,256]{1,0:T(8,128)(2,1)} %collective-permute-done.10), channel_id=1, source_target_pairs={{64,65},{65,64},{66,67},{67,66},{68,69},{69,68},{70,71},{71,70},{7... | collective-permute-start | bytes 3538952 | tf_op jit(solution)/shard_map/ppermute | solution.py:278
  38.5 6.0 %collective-permute-start.3 = (bf16[128,256]{1,0:T(8,128)(2,1)S(1)}, bf16[128,256]{1,0:T(8,128)(2,1)S(1)}, u32[]{:S(2)}, u32[]{:S(2)}) collective-permute-start(bf16[128,256]{1,0:T(8,128)(2,1)S(1)} %get-tuple-element.48), channel_id=1, source_target_pairs={{32,97},{33,98},{34,99},{35,100},{36,101},{37,102},{38,103},{39,10... | collective-permute-start | bytes 196616 | tf_op jit(solution)/shard_map/ppermute | solution.py:260
  39.1 6.0 %collective-permute-start.4 = (bf16[128,256]{1,0:T(8,128)(2,1)S(1)}, bf16[128,256]{1,0:T(8,128)(2,1)S(1)}, u32[]{:S(2)}, u32[]{:S(2)}) collective-permute-start(bf16[128,256]{1,0:T(8,128)(2,1)S(1)} %get-tuple-element.48), channel_id=1, source_target_pairs={{32,96},{33,97},{34,98},{35,99},{36,100},{37,101},{38,102},{39,103... | collective-permute-start | bytes 196616 | tf_op jit(solution)/shard_map/ppermute | solution.py:260
  39.8 6.7 %collective-permute-start.5 = (bf16[128,256]{1,0:T(8,128)(2,1)S(1)}, bf16[128,256]{1,0:T(8,128)(2,1)S(1)}, u32[]{:S(2)}, u32[]{:S(2)}) collective-permute-start(bf16[128,256]{1,0:T(8,128)(2,1)S(1)} %get-tuple-element.48), channel_id=1, source_target_pairs={{33,96},{34,97},{35,98},{36,99},{37,100},{38,101},{39,102},{40,103... | collective-permute-start | bytes 196616 | tf_op jit(solution)/shard_map/ppermute | solution.py:260
  41.8 4.7 %collective-permute-start.6 = (bf16[128,256]{1,0:T(8,128)(2,1)S(1)}, bf16[128,256]{1,0:T(8,128)(2,1)S(1)}, u32[]{:S(2)}, u32[]{:S(2)}) collective-permute-start(bf16[128,256]{1,0:T(8,128)(2,1)S(1)} %get-tuple-element.47), channel_id=1, source_target_pairs={{32,65},{33,66},{34,67},{35,68},{36,69},{37,70},{38,71},{39,72},{4... | collective-permute-start | bytes 196616 | tf_op jit(solution)/shard_map/ppermute | solution.py:260
  44.5 2.1 %collective-permute-start.7 = (bf16[128,256]{1,0:T(8,128)(2,1)S(1)}, bf16[128,256]{1,0:T(8,128)(2,1)S(1)}, u32[]{:S(2)}, u32[]{:S(2)}) collective-permute-start(bf16[128,256]{1,0:T(8,128)(2,1)S(1)} %get-tuple-element.47), channel_id=1, source_target_pairs={{32,64},{33,65},{34,66},{35,67},{36,68},{37,69},{38,70},{39,71},{4... | collective-permute-start | bytes 196616 | tf_op jit(solution)/shard_map/ppermute | solution.py:260
  47.2 4.7 %collective-permute-start.12 = (bf16[128,256]{1,0:T(8,128)(2,1)S(1)}, bf16[128,256]{1,0:T(8,128)(2,1)S(1)}, u32[]{:S(2)}, u32[]{:S(2)}) collective-permute-start(bf16[128,256]{1,0:T(8,128)(2,1)S(1)} %get-tuple-element.19), channel_id=1, source_target_pairs={{96,129},{97,130},{98,131},{99,132},{100,133},{101,134},{102,135},... | collective-permute-start | bytes 196616 | tf_op jit(solution)/shard_map/ppermute | solution.py:45
  47.9 4.0 %collective-permute-start.13 = (bf16[128,256]{1,0:T(8,128)(2,1)S(1)}, bf16[128,256]{1,0:T(8,128)(2,1)S(1)}, u32[]{:S(2)}, u32[]{:S(2)}) collective-permute-start(bf16[128,256]{1,0:T(8,128)(2,1)S(1)} %get-tuple-element.19), channel_id=1, source_target_pairs={{96,128},{97,129},{98,130},{99,131},{100,132},{101,133},{102,134},... | collective-permute-start | bytes 196616 | tf_op jit(solution)/shard_map/ppermute | solution.py:45
  48.5 3.4 %collective-permute-start.14 = (bf16[128,256]{1,0:T(8,128)(2,1)S(1)}, bf16[128,256]{1,0:T(8,128)(2,1)S(1)}, u32[]{:S(2)}, u32[]{:S(2)}) collective-permute-start(bf16[128,256]{1,0:T(8,128)(2,1)S(1)} %get-tuple-element.19), channel_id=1, source_target_pairs={{97,128},{98,129},{99,130},{100,131},{101,132},{102,133},{103,134}... | collective-permute-start | bytes 196616 | tf_op jit(solution)/shard_map/ppermute | solution.py:45
  49.3 5.3 %collective-permute-start.23 = (bf16[256,256]{1,0:T(8,128)(2,1)S(1)}, bf16[256,256]{1,0:T(8,128)(2,1)S(1)}, u32[]{:S(2)}, u32[]{:S(2)}) collective-permute-start(bf16[256,256]{1,0:T(8,128)(2,1)S(1)} %fusion), channel_id=1, source_target_pairs={{0,32},{32,0},{1,33},{33,1},{2,34},{34,2},{3,35},{35,3},{4,36},{36... | collective-permute-start | bytes 393224 | tf_op jit(solution)/shard_map/ppermute | solution.py:237
  49.9 9.0 %collective-permute-start.22 = (bf16[1152,256]{1,0:T(8,128)(2,1)}, bf16[1152,256]{1,0:T(8,128)(2,1)S(1)}, u32[]{:S(2)}, u32[]{:S(2)}) collective-permute-start(bf16[1152,256]{1,0:T(8,128)(2,1)} %collective-permute-done.21), channel_id=1, source_target_pairs={{256,257},{257,256},{258,259},{259,258},{260,261},{261,260},{262,2... | collective-permute-start | bytes 1769480 | tf_op jit(solution)/shard_map/ppermute | solution.py:278
  52.5 2.1 %collective-permute-start.15 = (bf16[128,256]{1,0:T(8,128)(2,1)S(1)}, bf16[128,256]{1,0:T(8,128)(2,1)S(1)}, u32[]{:S(2)}, u32[]{:S(2)}) collective-permute-start(bf16[128,256]{1,0:T(8,128)(2,1)S(1)} %get-tuple-element.21), channel_id=1, source_target_pairs={{128,225},{129,226},{130,227},{131,228},{132,229},{133,230},{134,2... | collective-permute-start | bytes 196616 | tf_op jit(solution)/shard_map/ppermute | solution.py:45
  55.2 6.9 %collective-permute-start.18 = (bf16[128,256]{1,0:T(8,128)(2,1)S(1)}, bf16[128,256]{1,0:T(8,128)(2,1)S(1)}, u32[]{:S(2)}, u32[]{:S(2)}) collective-permute-start(bf16[128,256]{1,0:T(8,128)(2,1)S(1)} %get-tuple-element.23), channel_id=1, source_target_pairs={{224,257},{225,258},{226,259},{227,260},{228,261},{229,262},{230,2... | collective-permute-start | bytes 196616 | tf_op jit(solution)/shard_map/ppermute | solution.py:45
  56.0 7.4 %collective-permute-start.20 = (bf16[128,256]{1,0:T(8,128)(2,1)S(1)}, bf16[128,256]{1,0:T(8,128)(2,1)S(1)}, u32[]{:S(2)}, u32[]{:S(2)}) collective-permute-start(bf16[128,256]{1,0:T(8,128)(2,1)S(1)} %get-tuple-element.23), channel_id=1, source_target_pairs={{225,256},{226,257},{227,258},{228,259},{229,260},{230,261},{231,2... | collective-permute-start | bytes 196616 | tf_op jit(solution)/shard_map/ppermute | solution.py:45
  56.6 6.7 %collective-permute-start.19 = (bf16[384,256]{1,0:T(8,128)(2,1)S(1)}, bf16[384,256]{1,0:T(8,128)(2,1)S(1)}, u32[]{:S(2)}, u32[]{:S(2)}) collective-permute-start(bf16[384,256]{1,0:T(8,128)(2,1)S(1)} %get-tuple-element.24), channel_id=1, source_target_pairs={{224,256},{225,257},{226,258},{227,259},{228,260},{229,261},{230,2... | collective-permute-start | bytes 589832 | tf_op jit(solution)/shard_map/ppermute | solution.py:45
  57.6 12.2 %collective-permute-start.27 = (bf16[128,256]{1,0:T(8,128)(2,1)S(1)}, bf16[128,256]{1,0:T(8,128)(2,1)S(1)}, u32[]{:S(2)}, u32[]{:S(2)}) collective-permute-start(bf16[128,256]{1,0:T(8,128)(2,1)S(1)} %slice_select_fusion), channel_id=1, source_target_pairs={{0,481},{1,482},{2,483},{3,484},{4,485},{5,486},{6,487},{7,488},{8... | collective-permute-start | bytes 196616 | tf_op jit(solution)/shard_map/ppermute | solution.py:45
  58.9 25.6 %collective-permute-start.28 = (bf16[384,256]{1,0:T(8,128)(2,1)S(1)}, bf16[384,256]{1,0:T(8,128)(2,1)S(1)}, u32[]{:S(2)}, u32[]{:S(2)}) collective-permute-start(bf16[384,256]{1,0:T(8,128)(2,1)S(1)} %get-tuple-element.33.refs_11_), channel_id=1, source_target_pairs={{0,480},{1,481},{2,482},{3,483},{4,484},{5,485},{6,486},{7,487},{8... | collective-permute-start | bytes 589832 | tf_op jit(solution)/shard_map/ppermute | solution.py:45
  62.1 22.4 %collective-permute-start.29 = (bf16[128,256]{1,0:T(8,128)(2,1)S(1)}, bf16[128,256]{1,0:T(8,128)(2,1)S(1)}, u32[]{:S(2)}, u32[]{:S(2)}) collective-permute-start(bf16[128,256]{1,0:T(8,128)(2,1)S(1)} %slice_select_fusion), channel_id=1, source_target_pairs={{1,480},{2,481},{3,482},{4,483},{5,484},{6,485},{7,486},{8,487},{9... | collective-permute-start | bytes 196616 | tf_op jit(solution)/shard_map/ppermute | solution.py:45
  64.0 20.5 %collective-permute-start.24 = (bf16[128,256]{1,0:T(8,128)(2,1)S(1)}, bf16[128,256]{1,0:T(8,128)(2,1)S(1)}, u32[]{:S(2)}, u32[]{:S(2)}) collective-permute-start(bf16[128,256]{1,0:T(8,128)(2,1)S(1)} %get-tuple-element.25), channel_id=1, source_target_pairs={{256,353},{257,354},{258,355},{259,356},{260,357},{261,358},{262,3... | collective-permute-start | bytes 196616 | tf_op jit(solution)/shard_map/ppermute | solution.py:45
  64.6 19.9 %collective-permute-start.25 = (bf16[128,256]{1,0:T(8,128)(2,1)S(1)}, bf16[128,256]{1,0:T(8,128)(2,1)S(1)}, u32[]{:S(2)}, u32[]{:S(2)}) collective-permute-start(bf16[128,256]{1,0:T(8,128)(2,1)S(1)} %get-tuple-element.25), channel_id=1, source_target_pairs={{256,352},{257,353},{258,354},{259,355},{260,356},{261,357},{262,3... | collective-permute-start | bytes 196616 | tf_op jit(solution)/shard_map/ppermute | solution.py:45
  69.8 14.7 %collective-permute-start.26 = (bf16[128,256]{1,0:T(8,128)(2,1)S(1)}, bf16[128,256]{1,0:T(8,128)(2,1)S(1)}, u32[]{:S(2)}, u32[]{:S(2)}) collective-permute-start(bf16[128,256]{1,0:T(8,128)(2,1)S(1)} %get-tuple-element.25), channel_id=1, source_target_pairs={{257,352},{258,353},{259,354},{260,355},{261,356},{262,357},{263,3... | collective-permute-start | bytes 196616 | tf_op jit(solution)/shard_map/ppermute | solution.py:45
  85.1 2.1 %collective-permute-start.30 = (bf16[128,256]{1,0:T(8,128)(2,1)S(1)}, bf16[128,256]{1,0:T(8,128)(2,1)S(1)}, u32[]{:S(2)}, u32[]{:S(2)}) collective-permute-start(bf16[128,256]{1,0:T(8,128)(2,1)S(1)} %get-tuple-element.27), channel_id=1, source_target_pairs={{352,385},{353,386},{354,387},{355,388},{356,389},{357,390},{358,3... | collective-permute-start | bytes 196616 | tf_op jit(solution)/shard_map/ppermute | solution.py:45
  85.8 1.4 collective-permute-start.31
  87.8 47.3 %collective-permute-start.33 = (bf16[128,256]{1,0:T(8,128)(2,1)S(1)}, bf16[128,256]{1,0:T(8,128)(2,1)S(1)}, u32[]{:S(2)}, u32[]{:S(2)}) collective-permute-start(bf16[128,256]{1,0:T(8,128)(2,1)S(1)} %get-tuple-element.29), channel_id=1, source_target_pairs={{384,481},{385,482},{386,483},{387,484},{388,485},{389,486},{390,4... | collective-permute-start | bytes 196616 | tf_op jit(solution)/shard_map/ppermute | solution.py:45
  89.1 46.0 %collective-permute-start.34 = (bf16[128,256]{1,0:T(8,128)(2,1)S(1)}, bf16[128,256]{1,0:T(8,128)(2,1)S(1)}, u32[]{:S(2)}, u32[]{:S(2)}) collective-permute-start(bf16[128,256]{1,0:T(8,128)(2,1)S(1)} %get-tuple-element.29), channel_id=1, source_target_pairs={{384,480},{385,481},{386,482},{387,483},{388,484},{389,485},{390,4... | collective-permute-start | bytes 196616 | tf_op jit(solution)/shard_map/ppermute | solution.py:45
  90.4 47.4 %collective-permute-start.35 = (bf16[128,256]{1,0:T(8,128)(2,1)S(1)}, bf16[128,256]{1,0:T(8,128)(2,1)S(1)}, u32[]{:S(2)}, u32[]{:S(2)}) collective-permute-start(bf16[128,256]{1,0:T(8,128)(2,1)S(1)} %get-tuple-element.29), channel_id=1, source_target_pairs={{385,480},{386,481},{387,482},{388,483},{389,484},{390,485},{391,4... | collective-permute-start | bytes 196616 | tf_op jit(solution)/shard_map/ppermute | solution.py:45
  141.9 5.3 %collective-permute-start.36 = (bf16[128,256]{1,0:T(8,128)(2,1)S(1)}, bf16[128,256]{1,0:T(8,128)(2,1)S(1)}, u32[]{:S(2)}, u32[]{:S(2)}) collective-permute-start(bf16[128,256]{1,0:T(8,128)(2,1)S(1)} %get-tuple-element.46), channel_id=1, source_target_pairs={{0,32},{32,0},{64,96},{96,64},{128,160},{160,128},{192,224},{224,1... | collective-permute-start | bytes 196616 | tf_op jit(solution)/shard_map/ppermute | solution.py:237
  (12 other events, 103.5 us)

commit v2 on v1

--- a/solution.py
+++ b/solution.py
@@ -123,19 +123,25 @@
     return call
 
 
-def phase_kernel(decoder, doubled=False, shared=False):
+def phase_kernel(decoder, doubled=False, mated=False, shared=False):
     kinds = 3 if decoder else 2
 
     def kernel(*refs):
         refs = list(refs)
         info = refs.pop(0)
         xs = [refs.pop(0) for _ in range(6 if doubled else 3)]
+        if mated:
+            straight, mate, far = xs
+            if shared:
+                mate = mate.at[2 * BLOCK : 3 * BLOCK]
+            own_rows = straight.at[2 * BLOCK : 3 * BLOCK] if shared else straight
         if decoder:
-            skips = xs if shared else [refs.pop(0) for _ in range(3)]
-            skip_narrow = skips[1].at[0 : 2 * BLOCK]
-            skip_wide = [skips[0], skips[1].at[2 * BLOCK : 3 * BLOCK], skips[2]]
-        if shared:
-            xs = skip_wide
+            if shared:
+                skip_narrow = straight.at[0 : 2 * BLOCK]
+            else:
+                skips = [refs.pop(0) for _ in range(3)]
+                skip_narrow = skips[1].at[0 : 2 * BLOCK]
+                skip_wide = [skips[0], skips[1].at[2 * BLOCK : 3 * BLOCK], skips[2]]
         bias = refs.pop(0)
         weights = [refs.pop(0) for _ in range(2 * kinds)]
         prev0 = refs.pop(0)
@@ -155,12 +161,25 @@
 
         @pl.when(active != 0)
         def _():
-            for index in range(3):
+            def piece(index):
+                if mated:
+                    if index == 1:
+                        return own_rows[...].astype(F32)
+                    sides = (far, mate) if index == 0 else (mate, far)
+                    return jnp.where(
+                        info[3] == 0, sides[0][...].astype(F32), sides[1][...].astype(F32)
+                    )
                 value = xs[index][...].astype(F32)
                 if doubled:
                     value = jnp.where(info[2] == 0, value, xs[index + 3][...].astype(F32))
+                return value
+
+            for index in range(3):
+                value = piece(index)
                 spread(work, index * BLOCK, value, ROWS)
-            if decoder:
+                if shared:
+                    spread(skip_work, index * BLOCK, value, ROWS)
+            if decoder and not shared:
                 for index, ref in enumerate(skip_wide):
                     spread(skip_work, index * BLOCK, ref[...].astype(F32), ROWS)
             for section in range(2):
@@ -240,11 +259,9 @@
     image = images.reshape(2, BLOCK, CH)
     below = shift_in_section(image, 0, -1)
     above = shift_in_section(image, 0, 1)
-    other = partner(both)
-    halves = [lax.dynamic_slice_in_dim(w, core * HALF, HALF, axis=0) for w in own]
     fetched = [
-        partner(jnp.concatenate(halves[:2], axis=0), pairs_from),
-        partner(halves[2], decoders),
+        partner(jnp.where(core == 0, own[0], own[1]), pairs_from),
+        partner(lax.dynamic_slice_in_dim(own[2], core * HALF, HALF, axis=0), decoders),
     ]
 
     def solo_info(which):
@@ -266,6 +283,7 @@
                     if 0 <= p + shift < STRIPS
                 ],
             )
+    other = partner(both)
     give = jnp.where(parity == 0, wide[1], jnp.concatenate([close[0], close[0]], axis=0))
     got = partner(give, range(2))
     level = jnp.where(
@@ -292,37 +310,65 @@
         jnp.concatenate([other, both], axis=0),
     )
 
-    def joined(mine, half, other_half):
-        remote = jnp.where(
-            core == 0,
-            jnp.concatenate([half, other_half], axis=0),
-            jnp.concatenate([other_half, half], axis=0),
-        )
+    def in_order(mine, remote):
         return jnp.where(parity == 0, mine, remote), jnp.where(parity == 0, remote, mine)
 
+    def by_core(at_zero, at_one):
+        return jnp.where(core == 0, at_zero, at_one)
+
+    skip_halves = jnp.where(
+        core == 0,
+        jnp.concatenate([fetched[1], swapped[1]], axis=0),
+        jnp.concatenate([swapped[1], fetched[1]], axis=0),
+    )
     by_kind = [
-        joined(own[0], fetched[0][:HALF], swapped[0][:HALF]),
-        joined(own[1], fetched[0][HALF:], swapped[0][HALF:]),
-        joined(own[2], fetched[1], swapped[1]),
+        in_order(own[0], by_core(fetched[0], swapped[0])),
+        in_order(own[1], by_core(swapped[0], fetched[0])),
+        in_order(own[2], skip_halves),
     ]
     all_weights = [pair[0] for pair in by_kind] + [pair[1] for pair in by_kind]
     encode_weights = all_weights[0:2] + all_weights[3:5]
 
     def info_of(phase):
         active = (group == phase).astype(jnp.int32)
-        return jnp.stack([active, strip * ROWS, micro]).astype(jnp.int32)
+        return jnp.stack([active, strip * ROWS, micro, core]).astype(jnp.int32)
 
     kept = jnp.zeros((3 * BLOCK, CH), BF16)
     middle = GROUPS // 2
 
     def onward(last, phase, centre=None):
-        down = send(last, [(phase, phase + 1, 1)])
-        up = send(last, [(phase, phase + 1, -1)])
-        straight = send(last if centre is None else centre, [(phase, phase + 1, 0)])
-        return (down, straight, up)
+        following = phase + 1
+        if phase % 2:
+            straight = send(last if centre is None else centre, [(phase, following, 0)])
+            far = lax.ppermute(
+                last,
+                JOINT,
+                [
+                    (
+                        place(phase, m) * STRIPS + p + (1 if p % 2 else -1),
+                        place(following, m) * STRIPS + p,
+                    )
+                    for m in range(2)
+                    for p in range(1, STRIPS - 1)
+                ],
+            )
+        else:
+            down = send(last, [(phase, following, 1)])
+            up = send(last, [(phase, following, -1)])
+            return (down, send(last, [(phase, following, 0)]), up)
+        mate = lax.ppermute(
+            straight,
+            JOINT,
+            [
+                (place(following, m) * STRIPS + a, place(following, m) * STRIPS + b)
+                for m in range(2)
+                for a, b in cores
+            ],
+        )
+        return (straight, mate, far)
 
     for phase in range(1, middle):
-        encode = phase_kernel(False, doubled=phase == 1)
+        encode = phase_kernel(False, doubled=phase == 1, mated=phase % 2 == 0)
         kept, last = encode(info_of(phase), xs, (), bias, encode_weights, kept)
         xs = onward(last, phase, kept if phase + 1 == middle else None)
     mirror = [(g, GROUPS - 1 - g) for g in range(middle - 1)]
@@ -334,7 +380,7 @@
     )
     for phase in range(middle, GROUPS):
         shared = phase == middle
-        decode = phase_kernel(True, shared=shared)
+        decode = phase_kernel(True, mated=phase % 2 == 0, shared=shared)
         kept, last = decode(
             info_of(phase), xs, () if shared else late, bias, all_weights, kept
         )

time: 149 us -> 165 us (1.11)
  the two profiles are of different devices: /device:TPU:253 before, /device:TPU:382 now
where the time goes in v2:
time: 165 us; the launch traced here: 164 us
  waiting for transfers between devices  95.9 us (58%)
  starting transfers between devices  39.9 us (24%)
  local copies, waits for them, and re-layouts  10.1 us (6%)
  Pallas kernels  9.64 us (6%)
  other arithmetic  7.17 us (4%)
    ppermute x15, waiting for transfers between devices, send(): return lax.ppermute(block, JOINT, route(moves))  63.5 us
    ppermute x5, waiting for transfers between devices, partner(): return lax.ppermute(block, 'section', [(i, i ^ 1) for i in sections])  32.4 us
    ppermute x15, starting transfers between devices, send(): return lax.ppermute(block, JOINT, route(moves))  14.7 us
    ppermute x5, starting transfers between devices, partner(): return lax.ppermute(block, 'section', [(i, i ^ 1) for i in sections])  11.3 us
    pallas_call x7, Pallas kernels, call(): pl.pallas_call(kernel, out_shape=(jax.ShapeDtypeStruct((3 * BLOCK, CH), B...  8.5 us
    unnamed x48, local copies, waits for them, and re-layouts  8.09 us
    ppermute x6, starting transfers between devices, body(): lax.ppermute(close[to], JOINT, [(STRIPS + p, place(1, to) * STRIPS + p +...  4.12 us
    ppermute x2, starting transfers between devices, body(): lax.ppermute(half, JOINT, [(s * STRIPS + a, s * STRIPS + b) for s in (dec...  3.82 us
  transfers between devices with their start and end apart: 37, of which 8 were waited for; matrix products, arithmetic and copies ran while one was open for 4% of the time, Pallas kernels for 2%

profile of v2, /device:TPU:382, one launch (start us, length us, event | category | flops | bytes accessed | tf_op | source)
XLA Modules:
  0.0 163.5 jit_solution(14851988392869625630)
XLA Ops:
  0.0 1.9 %broadcast_select_fusion.2 = bf16[2304,256]{1,0:T(8,128)(2,1)S(1)} fusion(pred[]{:T(512)S(6)} %eq.72, bf16[1,9,256,256]{3,2,1,0:T(8,128)(2,1)} %param.9, bf16[1,9,256,256]{3,2,1,0:T(8,128)(2,1)} %param.7), kind=kLoop, calls=%fused_computation.3 | loop fusion | flops 589824 | bytes 3538945 | tf_op jit(solution)/shard_map/jit(_where)/select_n | solution.py:263
  1.9 2.9 %collective-permute-start.10 = (bf16[2304,256]{1,0:T(8,128)(2,1)S(1)}, bf16[2304,256]{1,0:T(8,128)(2,1)}, u32[]{:S(2)}, u32[]{:S(2)}) collective-permute-start(bf16[2304,256]{1,0:T(8,128)(2,1)S(1)} %broadcast_select_fusion.2), channel_id=1, source_target_pairs={{64,96},{96,64},{128,160},{160,128},{192,224},{224,192},{256,288},... | collective-permute-start | bytes 3538952 | tf_op jit(solution)/shard_map/ppermute | solution.py:256
  6.1 25.6 %collective-permute-done.10 = bf16[2304,256]{1,0:T(8,128)(2,1)} collective-permute-done((bf16[2304,256]{1,0:T(8,128)(2,1)S(1)}, bf16[2304,256]{1,0:T(8,128)(2,1)}, u32[]{:S(2)}, u32[]{:S(2)}) %collective-permute-start.10) | collective-permute-done | bytes 1179680 | tf_op jit(solution)/shard_map/ppermute | solution.py:256
  31.7 1.9 %collective-permute-start.11 = (bf16[2304,256]{1,0:T(8,128)(2,1)}, bf16[2304,256]{1,0:T(8,128)(2,1)}, u32[]{:S(2)}, u32[]{:S(2)}) collective-permute-start(bf16[2304,256]{1,0:T(8,128)(2,1)} %collective-permute-done.10), channel_id=1, source_target_pairs={{64,65},{65,64},{66,67},{67,66},{68,69},{69,68},{70,71},{71,70},{7... | collective-permute-start | bytes 3538952 | tf_op jit(solution)/shard_map/ppermute | solution.py:296
  33.7 2.7 %collective-permute-start.9 = (f32[2,256]{1,0:T(2,128)S(1)}, f32[2,256]{1,0:T(2,128)S(1)}, u32[]{:S(2)}, u32[]{:S(2)}) collective-permute-start(f32[2,256]{1,0:T(2,128)S(1)} %pad_maximum_fusion.refs_3_.refs_1_), channel_id=1, source_target_pairs={{0,32},{32,0},{64,96},{96,64},{128,160},{160,128},{192,224},{224,1... | collective-permute-start | bytes 6152 | tf_op jit(solution)/shard_map/ppermute | solution.py:256
  36.4 1.9 %constant_dynamic-slice_fusion = bf16[1152,256]{1,0:T(8,128)(2,1)} fusion(bf16[2304,256]{1,0:T(8,128)(2,1)} %bitcast.43, s32[]{:T(128)S(6)} %select_n.152), kind=kLoop, calls=%fused_computation.32 | loop fusion | bytes 1179652 | tf_op jit(solution)/shard_map/dynamic_slice | solution.py:264
  38.4 3.1 %collective-permute-start.21 = (bf16[1152,256]{1,0:T(8,128)(2,1)}, bf16[1152,256]{1,0:T(8,128)(2,1)}, u32[]{:S(2)}, u32[]{:S(2)}) collective-permute-start(bf16[1152,256]{1,0:T(8,128)(2,1)} %constant_dynamic-slice_fusion), channel_id=1, source_target_pairs={{256,288},{288,256},{320,352},{352,320},{384,416},{416,384},{448,4... | collective-permute-start | bytes 1769480 | tf_op jit(solution)/shard_map/ppermute | solution.py:256
  48.0 1.9 %broadcast_select_fusion.5 = (bf16[2304,256]{1,0:T(8,128)(2,1)S(1)}, bf16[2304,256]{1,0:T(8,128)(2,1)S(1)}, bf16[2304,256]{1,0:T(8,128)(2,1)S(1)}, bf16[2304,256]{1,0:T(8,128)(2,1)S(1)}) fusion(pred[]{:T(512)S(6)} %eq.62, bf16[2304,256]{1,0:T(8,128)(2,1)} %collective-permute-done.11, bf16[2304,256]{1,0:T(8,128)(2,1)} %collective-permute-done.10, pred[]{:T(512)S(6)} %eq.72, ...), kind=kLoop, calls=%fused_computation.6 | loop fusion | flops 3538944 | bytes 9437186 | tf_op jit(solution)/shard_map/jit(_where)/select_n | solution.py:314
  53.5 2.6 %collective-permute-done.21 = bf16[1152,256]{1,0:T(8,128)(2,1)} collective-permute-done((bf16[1152,256]{1,0:T(8,128)(2,1)}, bf16[1152,256]{1,0:T(8,128)(2,1)}, u32[]{:S(2)}, u32[]{:S(2)}) %collective-permute-start.21) | collective-permute-done | bytes 589856 | tf_op jit(solution)/shard_map/ppermute | solution.py:256
  56.0 1.9 %collective-permute-start.22 = (bf16[1152,256]{1,0:T(8,128)(2,1)}, bf16[1152,256]{1,0:T(8,128)(2,1)S(1)}, u32[]{:S(2)}, u32[]{:S(2)}) collective-permute-start(bf16[1152,256]{1,0:T(8,128)(2,1)} %collective-permute-done.21), channel_id=1, source_target_pairs={{256,257},{257,256},{258,259},{259,258},{260,261},{261,260},{262,2... | collective-permute-start | bytes 1769480 | tf_op jit(solution)/shard_map/ppermute | solution.py:296
  62.8 1.3 collective-permute-start.27
  64.1 1.3 collective-permute-start.28
  66.1 1.8 %broadcast_select_fusion.3 = (bf16[2304,256]{1,0:T(8,128)(2,1)S(1)}, bf16[2304,256]{1,0:T(8,128)(2,1)S(1)}) fusion(pred[]{:T(512)S(6)} %eq.62, bf16[1152,256]{1,0:T(8,128)(2,1)} %collective-permute-done.21, bf16[1152,256]{1,0:T(8,128)(2,1)S(1)} %collective-permute-done.22, pred[]{:T(512)S(6)} %eq.72, bf16[1,9,256,256]{3,2,1,0:T(8,128)(2,1)S(1)} %copy-done.21), kind=kLoop, calls=%fused_computation.4 | loop fusion | flops 6488064 | bytes 4718594 | tf_op jit(solution)/shard_map/jit(_where)/select_n | solution.py:314
  68.0 1.5 collective-permute-start.29
  72.5 7.5 %collective-permute-done.29.refs_6_ = bf16[128,256]{1,0:T(8,128)(2,1)S(1)} collective-permute-done((bf16[128,256]{1,0:T(8,128)(2,1)S(1)}, bf16[128,256]{1,0:T(8,128)(2,1)S(1)}, u32[]{:S(2)}, u32[]{:S(2)}) %collective-permute-start.29) | collective-permute-done | bytes 65568 | tf_op jit(solution)/shard_map/ppermute | solution.py:45
  80.0 1.2 decode.5
  81.9 1.3 collective-permute-start.30
  84.6 1.3 copy-done.1
  85.9 1.3 copy-done.3
  87.2 1.3 copy-done.5
  88.4 0.9 copy-done.11
  89.4 0.8 copy-done.15
  91.1 0.9 copy-done.19
  92.0 0.9 decode.6
  92.9 1.3 collective-permute-start.33
  94.2 1.3 collective-permute-start.34
  95.5 1.3 collective-permute-start.35
  96.8 49.3 %collective-permute-done.33.refs_1_ = bf16[128,256]{1,0:T(8,128)(2,1)S(1)} collective-permute-done((bf16[128,256]{1,0:T(8,128)(2,1)S(1)}, bf16[128,256]{1,0:T(8,128)(2,1)S(1)}, u32[]{:S(2)}, u32[]{:S(2)}) %collective-permute-start.33) | collective-permute-done | bytes 65568 | tf_op jit(solution)/shard_map/ppermute | solution.py:45
  146.1 6.1 %collective-permute-done.34.refs_2_ = bf16[128,256]{1,0:T(8,128)(2,1)S(1)} collective-permute-done((bf16[128,256]{1,0:T(8,128)(2,1)S(1)}, bf16[128,256]{1,0:T(8,128)(2,1)S(1)}, u32[]{:S(2)}, u32[]{:S(2)}) %collective-permute-start.34) | collective-permute-done | bytes 65568 | tf_op jit(solution)/shard_map/ppermute | solution.py:45
  152.5 4.1 %decode.7 = (bf16[384,256]{1,0:T(8,128)(2,1)S(1)}, bf16[128,256]{1,0:T(8,128)(2,1)S(1)}) custom-call(s32[4]{0:T(128)S(1)} %add_add_fusion.refs_0_, bf16[128,256]{1,0:T(8,128)(2,1)S(1)} %collective-permute-done.33.refs_1_, bf16[128,256]{1,0:T(8,128)(2,1)S(1)} %collective-permute-done.34.refs_2_, bf16[128,256]{1,0:T(8,128)(2,1)S(1)} %collective-permute-done.35.refs_3_, ...), custom_call_target="tpu_custom_call" | custom-call | tf_op jit(solution)/shard_map/decode/pallas_call | solution.py:216
  156.7 1.9 %collective-permute-start.36 = (bf16[128,256]{1,0:T(8,128)(2,1)S(1)}, bf16[128,256]{1,0:T(8,128)(2,1)S(1)}, u32[]{:S(2)}, u32[]{:S(2)}) collective-permute-start(bf16[128,256]{1,0:T(8,128)(2,1)S(1)} %get-tuple-element.44), channel_id=1, source_target_pairs={{0,32},{32,0},{64,96},{96,64},{128,160},{160,128},{192,224},{224,1... | collective-permute-start | bytes 196616 | tf_op jit(solution)/shard_map/ppermute | solution.py:256
  158.6 4.2 %collective-permute-done.36 = bf16[128,256]{1,0:T(8,128)(2,1)S(1)} collective-permute-done((bf16[128,256]{1,0:T(8,128)(2,1)S(1)}, bf16[128,256]{1,0:T(8,128)(2,1)S(1)}, u32[]{:S(2)}, u32[]{:S(2)}) %collective-permute-start.36) | collective-permute-done | bytes 65568 | tf_op jit(solution)/shard_map/ppermute | solution.py:256
  (123 shorter events, 23.6 us)
Async XLA Ops:
  1.9 29.8 %collective-permute-start.10 = (bf16[2304,256]{1,0:T(8,128)(2,1)S(1)}, bf16[2304,256]{1,0:T(8,128)(2,1)}, u32[]{:S(2)}, u32[]{:S(2)}) collective-permute-start(bf16[2304,256]{1,0:T(8,128)(2,1)S(1)} %broadcast_select_fusion.2), channel_id=1, source_target_pairs={{64,96},{96,64},{128,160},{160,128},{192,224},{224,192},{256,288},... | collective-permute-start | bytes 3538952 | tf_op jit(solution)/shard_map/ppermute | solution.py:256
  4.8 36.9 %collective-permute-start = (bf16[2,128,256]{2,1,0:T(8,128)(2,1)S(1)}, bf16[2,128,256]{2,1,0:T(8,128)(2,1)S(1)}, u32[]{:S(2)}, u32[]{:S(2)}) collective-permute-start(bf16[2,128,256]{2,1,0:T(8,128)(2,1)S(1)} %bitcast.40), channel_id=1, source_target_pairs={{0,1},{1,2},{2,3},{3,4},{4,5},{5,6},{6,7},{7,8},{8,9},{9,10},{10,1... | collective-permute-start | bytes 393224 | tf_op jit(solution)/shard_map/ppermute | solution.py:245
  5.5 36.2 %collective-permute-start.1 = (bf16[2,128,256]{2,1,0:T(8,128)(2,1)S(1)}, bf16[2,128,256]{2,1,0:T(8,128)(2,1)S(1)}, u32[]{:S(2)}, u32[]{:S(2)}) collective-permute-start(bf16[2,128,256]{2,1,0:T(8,128)(2,1)S(1)} %bitcast.41), channel_id=1, source_target_pairs={{1,0},{2,1},{3,2},{4,3},{5,4},{6,5},{7,6},{8,7},{9,8},{10,9},{11,1... | collective-permute-start | bytes 393224 | tf_op jit(solution)/shard_map/ppermute | solution.py:245
  31.7 15.6 %collective-permute-start.11 = (bf16[2304,256]{1,0:T(8,128)(2,1)}, bf16[2304,256]{1,0:T(8,128)(2,1)}, u32[]{:S(2)}, u32[]{:S(2)}) collective-permute-start(bf16[2304,256]{1,0:T(8,128)(2,1)} %collective-permute-done.10), channel_id=1, source_target_pairs={{64,65},{65,64},{66,67},{67,66},{68,69},{69,68},{70,71},{71,70},{7... | collective-permute-start | bytes 3538952 | tf_op jit(solution)/shard_map/ppermute | solution.py:296
  33.7 11.6 %collective-permute-start.9 = (f32[2,256]{1,0:T(2,128)S(1)}, f32[2,256]{1,0:T(2,128)S(1)}, u32[]{:S(2)}, u32[]{:S(2)}) collective-permute-start(f32[2,256]{1,0:T(2,128)S(1)} %pad_maximum_fusion.refs_3_.refs_1_), channel_id=1, source_target_pairs={{0,32},{32,0},{64,96},{96,64},{128,160},{160,128},{192,224},{224,1... | collective-permute-start | bytes 6152 | tf_op jit(solution)/shard_map/ppermute | solution.py:256
  38.4 17.6 %collective-permute-start.21 = (bf16[1152,256]{1,0:T(8,128)(2,1)}, bf16[1152,256]{1,0:T(8,128)(2,1)}, u32[]{:S(2)}, u32[]{:S(2)}) collective-permute-start(bf16[1152,256]{1,0:T(8,128)(2,1)} %constant_dynamic-slice_fusion), channel_id=1, source_target_pairs={{256,288},{288,256},{320,352},{352,320},{384,416},{416,384},{448,4... | collective-permute-start | bytes 1769480 | tf_op jit(solution)/shard_map/ppermute | solution.py:256
  43.8 2.2 %collective-permute-start.3 = (bf16[128,256]{1,0:T(8,128)(2,1)S(1)}, bf16[128,256]{1,0:T(8,128)(2,1)S(1)}, u32[]{:S(2)}, u32[]{:S(2)}) collective-permute-start(bf16[128,256]{1,0:T(8,128)(2,1)S(1)} %get-tuple-element.46), channel_id=1, source_target_pairs={{32,97},{33,98},{34,99},{35,100},{36,101},{37,102},{38,103},{39,10... | collective-permute-start | bytes 196616 | tf_op jit(solution)/shard_map/ppermute | solution.py:277
  44.6 2.1 %collective-permute-start.4 = (bf16[128,256]{1,0:T(8,128)(2,1)S(1)}, bf16[128,256]{1,0:T(8,128)(2,1)S(1)}, u32[]{:S(2)}, u32[]{:S(2)}) collective-permute-start(bf16[128,256]{1,0:T(8,128)(2,1)S(1)} %get-tuple-element.46), channel_id=1, source_target_pairs={{32,96},{33,97},{34,98},{35,99},{36,100},{37,101},{38,102},{39,103... | collective-permute-start | bytes 196616 | tf_op jit(solution)/shard_map/ppermute | solution.py:277
  45.3 4.7 %collective-permute-start.5 = (bf16[128,256]{1,0:T(8,128)(2,1)S(1)}, bf16[128,256]{1,0:T(8,128)(2,1)S(1)}, u32[]{:S(2)}, u32[]{:S(2)}) collective-permute-start(bf16[128,256]{1,0:T(8,128)(2,1)S(1)} %get-tuple-element.46), channel_id=1, source_target_pairs={{33,96},{34,97},{35,98},{36,99},{37,100},{38,101},{39,102},{40,103... | collective-permute-start | bytes 196616 | tf_op jit(solution)/shard_map/ppermute | solution.py:277
  46.0 4.0 %collective-permute-start.6 = (bf16[128,256]{1,0:T(8,128)(2,1)S(1)}, bf16[128,256]{1,0:T(8,128)(2,1)S(1)}, u32[]{:S(2)}, u32[]{:S(2)}) collective-permute-start(bf16[128,256]{1,0:T(8,128)(2,1)S(1)} %get-tuple-element.45), channel_id=1, source_target_pairs={{32,65},{33,66},{34,67},{35,68},{36,69},{37,70},{38,71},{39,72},{4... | collective-permute-start | bytes 196616 | tf_op jit(solution)/shard_map/ppermute | solution.py:277
  46.7 3.4 %collective-permute-start.7 = (bf16[128,256]{1,0:T(8,128)(2,1)S(1)}, bf16[128,256]{1,0:T(8,128)(2,1)S(1)}, u32[]{:S(2)}, u32[]{:S(2)}) collective-permute-start(bf16[128,256]{1,0:T(8,128)(2,1)S(1)} %get-tuple-element.45), channel_id=1, source_target_pairs={{32,64},{33,65},{34,66},{35,67},{36,68},{37,69},{38,70},{39,71},{4... | collective-permute-start | bytes 196616 | tf_op jit(solution)/shard_map/ppermute | solution.py:277
  47.3 2.7 %collective-permute-start.8 = (bf16[128,256]{1,0:T(8,128)(2,1)S(1)}, bf16[128,256]{1,0:T(8,128)(2,1)S(1)}, u32[]{:S(2)}, u32[]{:S(2)}) collective-permute-start(bf16[128,256]{1,0:T(8,128)(2,1)S(1)} %get-tuple-element.45), channel_id=1, source_target_pairs={{33,64},{34,65},{35,66},{36,67},{37,68},{38,69},{39,70},{40,71},{4... | collective-permute-start | bytes 196616 | tf_op jit(solution)/shard_map/ppermute | solution.py:277
  51.4 6.6 %collective-permute-start.14 = (bf16[128,256]{1,0:T(8,128)(2,1)S(1)}, bf16[128,256]{1,0:T(8,128)(2,1)S(1)}, u32[]{:S(2)}, u32[]{:S(2)}) collective-permute-start(bf16[128,256]{1,0:T(8,128)(2,1)S(1)} %get-tuple-element.19), channel_id=1, source_target_pairs={{98,129},{97,130},{100,131},{99,132},{102,133},{101,134},{104,135}... | collective-permute-start | bytes 196616 | tf_op jit(solution)/shard_map/ppermute | solution.py:343
  52.1 5.9 %collective-permute-start.13 = (bf16[128,256]{1,0:T(8,128)(2,1)S(1)}, bf16[128,256]{1,0:T(8,128)(2,1)S(1)}, u32[]{:S(2)}, u32[]{:S(2)}) collective-permute-start(bf16[128,256]{1,0:T(8,128)(2,1)S(1)} %collective-permute-done.12.refs_1_), channel_id=1, source_target_pairs={{128,129},{129,128},{130,131},{131,130},{132,133},{133,132},{134,1... | collective-permute-start | bytes 196616 | tf_op jit(solution)/shard_map/ppermute | solution.py:359
  52.8 7.8 %collective-permute-start.23 = (bf16[256,256]{1,0:T(8,128)(2,1)S(1)}, bf16[256,256]{1,0:T(8,128)(2,1)S(1)}, u32[]{:S(2)}, u32[]{:S(2)}) collective-permute-start(bf16[256,256]{1,0:T(8,128)(2,1)S(1)} %fusion), channel_id=1, source_target_pairs={{0,32},{32,0},{1,33},{33,1},{2,34},{34,2},{3,35},{35,3},{4,36},{36... | collective-permute-start | bytes 393224 | tf_op jit(solution)/shard_map/ppermute | solution.py:256
  56.0 10.1 %collective-permute-start.22 = (bf16[1152,256]{1,0:T(8,128)(2,1)}, bf16[1152,256]{1,0:T(8,128)(2,1)S(1)}, u32[]{:S(2)}, u32[]{:S(2)}) collective-permute-start(bf16[1152,256]{1,0:T(8,128)(2,1)} %collective-permute-done.21), channel_id=1, source_target_pairs={{256,257},{257,256},{258,259},{259,258},{260,261},{261,260},{262,2... | collective-permute-start | bytes 1769480 | tf_op jit(solution)/shard_map/ppermute | solution.py:296
  58.5 2.1 %collective-permute-start.15 = (bf16[128,256]{1,0:T(8,128)(2,1)S(1)}, bf16[128,256]{1,0:T(8,128)(2,1)S(1)}, u32[]{:S(2)}, u32[]{:S(2)}) collective-permute-start(bf16[128,256]{1,0:T(8,128)(2,1)S(1)} %get-tuple-element.21), channel_id=1, source_target_pairs={{128,225},{129,226},{130,227},{131,228},{132,229},{133,230},{134,2... | collective-permute-start | bytes 196616 | tf_op jit(solution)/shard_map/ppermute | solution.py:45
  61.2 4.2 %collective-permute-start.18 = (bf16[384,256]{1,0:T(8,128)(2,1)S(1)}, bf16[384,256]{1,0:T(8,128)(2,1)S(1)}, u32[]{:S(2)}, u32[]{:S(2)}) collective-permute-start(bf16[384,256]{1,0:T(8,128)(2,1)S(1)} %get-tuple-element.23), channel_id=1, source_target_pairs={{224,256},{225,257},{226,258},{227,259},{228,260},{229,261},{230,2... | collective-permute-start | bytes 589832 | tf_op jit(solution)/shard_map/ppermute | solution.py:45
  62.0 7.4 %collective-permute-start.20 = (bf16[128,256]{1,0:T(8,128)(2,1)S(1)}, bf16[128,256]{1,0:T(8,128)(2,1)S(1)}, u32[]{:S(2)}, u32[]{:S(2)}) collective-permute-start(bf16[128,256]{1,0:T(8,128)(2,1)S(1)} %get-tuple-element.24), channel_id=1, source_target_pairs={{226,257},{225,258},{228,259},{227,260},{230,261},{229,262},{232,2... | collective-permute-start | bytes 196616 | tf_op jit(solution)/shard_map/ppermute | solution.py:343
  62.8 8.9 %collective-permute-start.27 = (bf16[128,256]{1,0:T(8,128)(2,1)S(1)}, bf16[128,256]{1,0:T(8,128)(2,1)S(1)}, u32[]{:S(2)}, u32[]{:S(2)}) collective-permute-start(bf16[128,256]{1,0:T(8,128)(2,1)S(1)} %slice_select_fusion), channel_id=1, source_target_pairs={{0,481},{1,482},{2,483},{3,484},{4,485},{5,486},{6,487},{7,488},{8... | collective-permute-start | bytes 196616 | tf_op jit(solution)/shard_map/ppermute | solution.py:45
  64.1 15.8 %collective-permute-start.28 = (bf16[384,256]{1,0:T(8,128)(2,1)S(1)}, bf16[384,256]{1,0:T(8,128)(2,1)S(1)}, u32[]{:S(2)}, u32[]{:S(2)}) collective-permute-start(bf16[384,256]{1,0:T(8,128)(2,1)S(1)} %get-tuple-element.33.refs_11_), channel_id=1, source_target_pairs={{0,480},{1,481},{2,482},{3,483},{4,484},{5,485},{6,486},{7,487},{8... | collective-permute-start | bytes 589832 | tf_op jit(solution)/shard_map/ppermute | solution.py:45
  65.4 4.0 %collective-permute-start.19 = (bf16[384,256]{1,0:T(8,128)(2,1)S(1)}, bf16[384,256]{1,0:T(8,128)(2,1)S(1)}, u32[]{:S(2)}, u32[]{:S(2)}) collective-permute-start(bf16[384,256]{1,0:T(8,128)(2,1)S(1)} %collective-permute-done.18.refs_1_), channel_id=1, source_target_pairs={{256,257},{257,256},{258,259},{259,258},{260,261},{261,260},{262,2... | collective-permute-start | bytes 589832 | tf_op jit(solution)/shard_map/ppermute | solution.py:359
  68.0 12.0 %collective-permute-start.29 = (bf16[128,256]{1,0:T(8,128)(2,1)S(1)}, bf16[128,256]{1,0:T(8,128)(2,1)S(1)}, u32[]{:S(2)}, u32[]{:S(2)}) collective-permute-start(bf16[128,256]{1,0:T(8,128)(2,1)S(1)} %slice_select_fusion), channel_id=1, source_target_pairs={{1,480},{2,481},{3,482},{4,483},{5,484},{6,485},{7,486},{8,487},{9... | collective-permute-start | bytes 196616 | tf_op jit(solution)/shard_map/ppermute | solution.py:45
  70.1 9.9 %collective-permute-start.24 = (bf16[128,256]{1,0:T(8,128)(2,1)S(1)}, bf16[128,256]{1,0:T(8,128)(2,1)S(1)}, u32[]{:S(2)}, u32[]{:S(2)}) collective-permute-start(bf16[128,256]{1,0:T(8,128)(2,1)S(1)} %get-tuple-element.25), channel_id=1, source_target_pairs={{256,353},{257,354},{258,355},{259,356},{260,357},{261,358},{262,3... | collective-permute-start | bytes 196616 | tf_op jit(solution)/shard_map/ppermute | solution.py:45
  70.7 9.2 %collective-permute-start.25 = (bf16[128,256]{1,0:T(8,128)(2,1)S(1)}, bf16[128,256]{1,0:T(8,128)(2,1)S(1)}, u32[]{:S(2)}, u32[]{:S(2)}) collective-permute-start(bf16[128,256]{1,0:T(8,128)(2,1)S(1)} %get-tuple-element.25), channel_id=1, source_target_pairs={{256,352},{257,353},{258,354},{259,355},{260,356},{261,357},{262,3... | collective-permute-start | bytes 196616 | tf_op jit(solution)/shard_map/ppermute | solution.py:45
  71.7 8.2 %collective-permute-start.26 = (bf16[128,256]{1,0:T(8,128)(2,1)S(1)}, bf16[128,256]{1,0:T(8,128)(2,1)S(1)}, u32[]{:S(2)}, u32[]{:S(2)}) collective-permute-start(bf16[128,256]{1,0:T(8,128)(2,1)S(1)} %get-tuple-element.25), channel_id=1, source_target_pairs={{257,352},{258,353},{259,354},{260,355},{261,356},{262,357},{263,3... | collective-permute-start | bytes 196616 | tf_op jit(solution)/shard_map/ppermute | solution.py:45
  81.9 1.9 %collective-permute-start.30 = (bf16[128,256]{1,0:T(8,128)(2,1)}, bf16[128,256]{1,0:T(8,128)(2,1)}, u32[]{:S(2)}, u32[]{:S(2)}) collective-permute-start(bf16[128,256]{1,0:T(8,128)(2,1)} %get-tuple-element.27), channel_id=1, source_target_pairs={{352,384},{353,385},{354,386},{355,387},{356,388},{357,389},{358,3... | collective-permute-start | bytes 196616 | tf_op jit(solution)/shard_map/ppermute | solution.py:45
  83.2 1.4 collective-permute-start.32
  92.9 53.3 %collective-permute-start.33 = (bf16[128,256]{1,0:T(8,128)(2,1)S(1)}, bf16[128,256]{1,0:T(8,128)(2,1)S(1)}, u32[]{:S(2)}, u32[]{:S(2)}) collective-permute-start(bf16[128,256]{1,0:T(8,128)(2,1)S(1)} %get-tuple-element.29), channel_id=1, source_target_pairs={{384,481},{385,482},{386,483},{387,484},{388,485},{389,486},{390,4... | collective-permute-start | bytes 196616 | tf_op jit(solution)/shard_map/ppermute | solution.py:45
  94.2 58.0 %collective-permute-start.34 = (bf16[128,256]{1,0:T(8,128)(2,1)S(1)}, bf16[128,256]{1,0:T(8,128)(2,1)S(1)}, u32[]{:S(2)}, u32[]{:S(2)}) collective-permute-start(bf16[128,256]{1,0:T(8,128)(2,1)S(1)} %get-tuple-element.29), channel_id=1, source_target_pairs={{384,480},{385,481},{386,482},{387,483},{388,484},{389,485},{390,4... | collective-permute-start | bytes 196616 | tf_op jit(solution)/shard_map/ppermute | solution.py:45
  95.5 57.1 %collective-permute-start.35 = (bf16[128,256]{1,0:T(8,128)(2,1)S(1)}, bf16[128,256]{1,0:T(8,128)(2,1)S(1)}, u32[]{:S(2)}, u32[]{:S(2)}) collective-permute-start(bf16[128,256]{1,0:T(8,128)(2,1)S(1)} %get-tuple-element.29), channel_id=1, source_target_pairs={{385,480},{386,481},{387,482},{388,483},{389,484},{390,485},{391,4... | collective-permute-start | bytes 196616 | tf_op jit(solution)/shard_map/ppermute | solution.py:45
  156.7 6.2 %collective-permute-start.36 = (bf16[128,256]{1,0:T(8,128)(2,1)S(1)}, bf16[128,256]{1,0:T(8,128)(2,1)S(1)}, u32[]{:S(2)}, u32[]{:S(2)}) collective-permute-start(bf16[128,256]{1,0:T(8,128)(2,1)S(1)} %get-tuple-element.44), channel_id=1, source_target_pairs={{0,32},{32,0},{64,96},{96,64},{128,160},{160,128},{192,224},{224,1... | collective-permute-start | bytes 196616 | tf_op jit(solution)/shard_map/ppermute | solution.py:256
  (29 other events, 251.7 us)

commit v3 on v2

--- a/solution.py
+++ b/solution.py
@@ -19,6 +19,7 @@
 HEIGHT = ROWS * STRIPS
 GROUPS = SECTIONS // 2
 JOINT = ("section", "strip")
+VMEM_LIMIT = 16 * 1024 * 1024
 
 
 def place(group, micro):
@@ -79,7 +80,7 @@
     return value.astype(BF16).astype(F32)
 
 
-def single_kernel(halo):
+def single_kernel(which, halo):
     tall = ROWS + 2 * halo
     out_rows = tall - 4
 
@@ -87,11 +88,11 @@
         blocks = refs[:-5]
         bias, first, second, out, work = refs[-5:]
 
-        @pl.when(info[0] == 0)
+        @pl.when(info[4] != which)
         def _():
             out[...] = jnp.zeros(out.shape, BF16)
 
-        @pl.when(info[0] != 0)
+        @pl.when(info[4] == which)
         def _():
             for micro in range(2):
                 at = micro * tall * COLS
@@ -117,13 +118,13 @@
             in_specs=[pl.BlockSpec(memory_space=pltpu.SMEM)] + [vmem] * (len(operands) - 1),
             out_specs=vmem,
             scratch_shapes=[pltpu.VMEM((2 * tall * COLS, 3 * CH), BF16)],
-            compiler_params=pltpu.CompilerParams(vmem_limit_bytes=40 * 1024 * 1024),
+            compiler_params=pltpu.CompilerParams(vmem_limit_bytes=VMEM_LIMIT),
         )(*operands)
 
     return call
 
 
-def phase_kernel(decoder, doubled=False, mated=False, shared=False):
+def phase_kernel(phase, decoder, doubled=False, mated=False, shared=False):
     kinds = 3 if decoder else 2
 
     def kernel(*refs):
@@ -151,7 +152,7 @@
         if decoder:
             skip_work = refs.pop(0)
 
-        active = info[0]
+        active = (info[0] == phase).astype(jnp.int32)
         top = info[1]
 
         @pl.when(active == 0)
@@ -222,7 +223,7 @@
             in_specs=specs,
             out_specs=(vmem, vmem),
             scratch_shapes=scratch,
-            compiler_params=pltpu.CompilerParams(vmem_limit_bytes=40 * 1024 * 1024),
+            compiler_params=pltpu.CompilerParams(vmem_limit_bytes=VMEM_LIMIT),
             name="decode" if decoder else "encode",
         )(*operands)
 
@@ -236,6 +237,10 @@
     parity = section % 2
     group = section // 2
     micro = jnp.where(group % 2 == 0, parity, 1 - parity)
+    info = jnp.stack([group, strip * ROWS, micro, core, section]).astype(jnp.int32)
+    images, info, core_zero, even, group_zero, micro_zero = lax.optimization_barrier(
+        (images, info, core == 0, parity == 0, group == 0, micro == 0)
+    )
     own = [w.reshape(TAPS, CH) for w in (conv_first[0], conv_second[0], conv_skip[0])]
     decoders = range(SECTIONS // 2, SECTIONS)
     pairs_from = range(2, SECTIONS)
@@ -260,17 +265,13 @@
     below = shift_in_section(image, 0, -1)
     above = shift_in_section(image, 0, 1)
     fetched = [
-        partner(jnp.where(core == 0, own[0], own[1]), pairs_from),
+        partner(jnp.where(core_zero, own[0], own[1]), pairs_from),
         partner(lax.dynamic_slice_in_dim(own[2], core * HALF, HALF, axis=0), decoders),
     ]
 
-    def solo_info(which):
-        active = (section == which).astype(jnp.int32)
-        return jnp.stack([active, strip * ROWS]).astype(jnp.int32)
-
-    wide = single_kernel(4)(solo_info(0), (above, image, below), both, own[0], own[1])
+    wide = single_kernel(0, 4)(info, (above, image, below), both, own[0], own[1])
     handed = lax.ppermute(wide, JOINT, [(p, STRIPS + p) for p in range(STRIPS)])
-    close = single_kernel(2)(solo_info(1), (handed,), both, own[0], own[1])
+    close = single_kernel(1, 2)(info, (handed,), both, own[0], own[1])
     xs = [None] * 6
     for shift in (1, -1, 0):
         for to in range(2):
@@ -284,10 +285,10 @@
                 ],
             )
     other = partner(both)
-    give = jnp.where(parity == 0, wide[1], jnp.concatenate([close[0], close[0]], axis=0))
+    give = jnp.where(even, wide[1], jnp.concatenate([close[0], close[0]], axis=0))
     got = partner(give, range(2))
     level = jnp.where(
-        parity == 0,
+        even,
         jnp.concatenate([wide[0], got[:BLOCK]], axis=0),
         jnp.concatenate([got, close[1]], axis=0),
     )
@@ -305,19 +306,19 @@
         for index, half in enumerate(fetched)
     ]
     bias = jnp.where(
-        parity == 0,
+        even,
         jnp.concatenate([both, other], axis=0),
         jnp.concatenate([other, both], axis=0),
     )
 
     def in_order(mine, remote):
-        return jnp.where(parity == 0, mine, remote), jnp.where(parity == 0, remote, mine)
+        return jnp.where(even, mine, remote), jnp.where(even, remote, mine)
 
     def by_core(at_zero, at_one):
-        return jnp.where(core == 0, at_zero, at_one)
+        return jnp.where(core_zero, at_zero, at_one)
 
     skip_halves = jnp.where(
-        core == 0,
+        core_zero,
         jnp.concatenate([fetched[1], swapped[1]], axis=0),
         jnp.concatenate([swapped[1], fetched[1]], axis=0),
     )
@@ -328,10 +329,6 @@
     ]
     all_weights = [pair[0] for pair in by_kind] + [pair[1] for pair in by_kind]
     encode_weights = all_weights[0:2] + all_weights[3:5]
-
-    def info_of(phase):
-        active = (group == phase).astype(jnp.int32)
-        return jnp.stack([active, strip * ROWS, micro, core]).astype(jnp.int32)
 
     kept = jnp.zeros((3 * BLOCK, CH), BF16)
     middle = GROUPS // 2
@@ -368,30 +365,30 @@
         return (straight, mate, far)
 
     for phase in range(1, middle):
-        encode = phase_kernel(False, doubled=phase == 1, mated=phase % 2 == 0)
-        kept, last = encode(info_of(phase), xs, (), bias, encode_weights, kept)
+        encode = phase_kernel(phase, False, doubled=phase == 1, mated=phase % 2 == 0)
+        kept, last = encode(info, xs, (), bias, encode_weights, kept)
         xs = onward(last, phase, kept if phase + 1 == middle else None)
     mirror = [(g, GROUPS - 1 - g) for g in range(middle - 1)]
-    kept = jnp.where(group == 0, level, kept)
-    last = jnp.where(group == 0, level[2 * BLOCK :], last)
+    kept = jnp.where(group_zero, level, kept)
+    last = jnp.where(group_zero, level[2 * BLOCK :], last)
     late = tuple(
         send(kept if shift == 0 else last, [(a, b, shift) for a, b in mirror])
         for shift in (1, 0, -1)
     )
     for phase in range(middle, GROUPS):
         shared = phase == middle
-        decode = phase_kernel(True, mated=phase % 2 == 0, shared=shared)
+        decode = phase_kernel(phase, True, mated=phase % 2 == 0, shared=shared)
         kept, last = decode(
-            info_of(phase), xs, () if shared else late, bias, all_weights, kept
+            info, xs, () if shared else late, bias, all_weights, kept
         )
         if phase + 1 < GROUPS:
             xs = onward(last, phase)
 
     inner = kept[BLOCK // 2 : BLOCK // 2 + BLOCK]
-    mine = jnp.where(parity == 0, inner, last)
-    theirs = partner(jnp.where(parity == 0, last, inner))
+    mine = jnp.where(even, inner, last)
+    theirs = partner(jnp.where(even, last, inner))
     result = jnp.where(
-        micro == 0, jnp.stack([mine, theirs]), jnp.stack([theirs, mine])
+        micro_zero, jnp.stack([mine, theirs]), jnp.stack([theirs, mine])
     )
     return result.reshape(1, 2, ROWS, COLS, CH)
 

time: 165 us -> 153 us (0.927)
  the two profiles are of different devices: /device:TPU:382 before, /device:TPU:318 now
where the time goes in v3:
time: 153 us; the launch traced here: 152 us
  waiting for transfers between devices  97.2 us (64%)
  starting transfers between devices  38.9 us (25%)
  Pallas kernels  8.89 us (6%)
  other arithmetic  5.33 us (3%)
    ppermute x15, waiting for transfers between devices, send(): return lax.ppermute(block, JOINT, route(moves))  61.8 us
    ppermute x5, waiting for transfers between devices, partner(): return lax.ppermute(block, 'section', [(i, i ^ 1) for i in sections])  35.4 us
    ppermute x15, starting transfers between devices, send(): return lax.ppermute(block, JOINT, route(moves))  13.9 us
    ppermute x5, starting transfers between devices, partner(): return lax.ppermute(block, 'section', [(i, i ^ 1) for i in sections])  11.2 us
    pallas_call x7, Pallas kernels, call(): pl.pallas_call(kernel, out_shape=(jax.ShapeDtypeStruct((3 * BLOCK, CH), B...  7.75 us
    ppermute x6, starting transfers between devices, body(): lax.ppermute(close[to], JOINT, [(STRIPS + p, place(1, to) * STRIPS + p +...  3.99 us
    ppermute x2, starting transfers between devices, body(): lax.ppermute(half, JOINT, [(s * STRIPS + a, s * STRIPS + b) for s in (dec...  3.82 us
  transfers between devices with their start and end apart: 37, of which 8 were waited for; matrix products, arithmetic and copies ran while one was open for 3% of the time, Pallas kernels for 2%

profile of v3, /device:TPU:318, one launch (start us, length us, event | category | flops | bytes accessed | tf_op | source)
XLA Modules:
  0.0 152.3 jit_solution(1146830916215933500)
XLA Ops:
  0.1 1.9 %broadcast_select_fusion.2 = bf16[2304,256]{1,0:T(8,128)(2,1)S(1)} fusion(pred[]{:T(512)S(6)} %eq.20, bf16[1,9,256,256]{3,2,1,0:T(8,128)(2,1)} %param.9, bf16[1,9,256,256]{3,2,1,0:T(8,128)(2,1)} %param.7), kind=kLoop, calls=%fused_computation.3 | loop fusion | flops 589824 | bytes 3538945 | tf_op jit(solution)/shard_map/jit(_where)/select_n | solution.py:268
  2.0 2.7 %collective-permute-start.10 = (bf16[2304,256]{1,0:T(8,128)(2,1)S(1)}, bf16[2304,256]{1,0:T(8,128)(2,1)}, u32[]{:S(2)}, u32[]{:S(2)}) collective-permute-start(bf16[2304,256]{1,0:T(8,128)(2,1)S(1)} %broadcast_select_fusion.2), channel_id=1, source_target_pairs={{64,96},{96,64},{128,160},{160,128},{192,224},{224,192},{256,288},... | collective-permute-start | bytes 3538952 | tf_op jit(solution)/shard_map/ppermute | solution.py:261
  4.8 27.0 %collective-permute-done.10 = bf16[2304,256]{1,0:T(8,128)(2,1)} collective-permute-done((bf16[2304,256]{1,0:T(8,128)(2,1)S(1)}, bf16[2304,256]{1,0:T(8,128)(2,1)}, u32[]{:S(2)}, u32[]{:S(2)}) %collective-permute-start.10) | collective-permute-done | bytes 1179680 | tf_op jit(solution)/shard_map/ppermute | solution.py:261
  31.7 1.9 %collective-permute-start.11 = (bf16[2304,256]{1,0:T(8,128)(2,1)}, bf16[2304,256]{1,0:T(8,128)(2,1)}, u32[]{:S(2)}, u32[]{:S(2)}) collective-permute-start(bf16[2304,256]{1,0:T(8,128)(2,1)} %collective-permute-done.10), channel_id=1, source_target_pairs={{64,65},{65,64},{66,67},{67,66},{68,69},{69,68},{70,71},{71,70},{7... | collective-permute-start | bytes 3538952 | tf_op jit(solution)/shard_map/ppermute | solution.py:297
  33.7 0.7 collective-permute-start
  34.3 0.7 collective-permute-start.1
  35.7 0.7 collective-permute-start.2
  36.3 2.7 %collective-permute-start.9 = (f32[2,256]{1,0:T(2,128)S(1)}, f32[2,256]{1,0:T(2,128)S(1)}, u32[]{:S(2)}, u32[]{:S(2)}) collective-permute-start(f32[2,256]{1,0:T(2,128)S(1)} %pad_maximum_fusion.refs_3_.refs_1_), channel_id=1, source_target_pairs={{0,32},{32,0},{64,96},{96,64},{128,160},{160,128},{192,224},{224,1... | collective-permute-start | bytes 6152 | tf_op jit(solution)/shard_map/ppermute | solution.py:261
  39.1 1.1 constant_dynamic-slice_fusion
  40.2 3.1 %collective-permute-start.21 = (bf16[1152,256]{1,0:T(8,128)(2,1)S(1)}, bf16[1152,256]{1,0:T(8,128)(2,1)S(1)}, u32[]{:S(2)}, u32[]{:S(2)}) collective-permute-start(bf16[1152,256]{1,0:T(8,128)(2,1)S(1)} %constant_dynamic-slice_fusion), channel_id=1, source_target_pairs={{256,288},{288,256},{320,352},{352,320},{384,416},{416,384},{448,4... | collective-permute-start | bytes 1769480 | tf_op jit(solution)/shard_map/ppermute | solution.py:261
  43.9 0.7 collective-permute-start.3
  48.0 1.9 %broadcast_select_fusion.5 = (bf16[2304,256]{1,0:T(8,128)(2,1)S(1)}, bf16[2304,256]{1,0:T(8,128)(2,1)S(1)}, bf16[2304,256]{1,0:T(8,128)(2,1)S(1)}, bf16[2304,256]{1,0:T(8,128)(2,1)S(1)}) fusion(pred[]{:T(512)S(6)} %eq.21, bf16[2304,256]{1,0:T(8,128)(2,1)} %collective-permute-done.11, bf16[2304,256]{1,0:T(8,128)(2,1)} %collective-permute-done.10, pred[]{:T(512)S(6)} %eq.20, ...), kind=kLoop, calls=%fused_computation.6 | loop fusion | flops 3538944 | bytes 9437186 | tf_op jit(solution)/shard_map/jit(_where)/select_n | solution.py:315
  52.7 0.7 collective-permute-start.23
  53.4 4.2 %collective-permute-done.21 = bf16[1152,256]{1,0:T(8,128)(2,1)S(1)} collective-permute-done((bf16[1152,256]{1,0:T(8,128)(2,1)S(1)}, bf16[1152,256]{1,0:T(8,128)(2,1)S(1)}, u32[]{:S(2)}, u32[]{:S(2)}) %collective-permute-start.21) | collective-permute-done | bytes 589856 | tf_op jit(solution)/shard_map/ppermute | solution.py:261
  57.6 1.9 %collective-permute-start.22 = (bf16[1152,256]{1,0:T(8,128)(2,1)S(1)}, bf16[1152,256]{1,0:T(8,128)(2,1)S(1)}, u32[]{:S(2)}, u32[]{:S(2)}) collective-permute-start(bf16[1152,256]{1,0:T(8,128)(2,1)S(1)} %collective-permute-done.21), channel_id=1, source_target_pairs={{256,257},{257,256},{258,259},{259,258},{260,261},{261,260},{262,2... | collective-permute-start | bytes 1769480 | tf_op jit(solution)/shard_map/ppermute | solution.py:297
  62.8 0.8 collective-permute-start.18
  64.4 1.3 collective-permute-start.27
  65.7 1.3 collective-permute-start.28
  67.0 0.7 collective-permute-start.19
  68.3 1.3 collective-permute-start.29
  69.6 0.8 decode.4
  71.7 1.5 collective-permute-done.27.refs_4_
  73.9 7.6 %collective-permute-done.29.refs_6_ = bf16[128,256]{1,0:T(8,128)(2,1)S(1)} collective-permute-done((bf16[128,256]{1,0:T(8,128)(2,1)S(1)}, bf16[128,256]{1,0:T(8,128)(2,1)S(1)}, u32[]{:S(2)}, u32[]{:S(2)}) %collective-permute-start.29) | collective-permute-done | bytes 65568 | tf_op jit(solution)/shard_map/ppermute | solution.py:46
  84.7 1.3 collective-permute-start.33
  86.0 1.3 collective-permute-start.34
  87.3 1.3 collective-permute-start.35
  88.6 47.2 %collective-permute-done.33.refs_1_ = bf16[128,256]{1,0:T(8,128)(2,1)S(1)} collective-permute-done((bf16[128,256]{1,0:T(8,128)(2,1)S(1)}, bf16[128,256]{1,0:T(8,128)(2,1)S(1)}, u32[]{:S(2)}, u32[]{:S(2)}) %collective-permute-start.33) | collective-permute-done | bytes 65568 | tf_op jit(solution)/shard_map/ppermute | solution.py:46
  135.8 5.0 %collective-permute-done.34.refs_2_ = bf16[128,256]{1,0:T(8,128)(2,1)S(1)} collective-permute-done((bf16[128,256]{1,0:T(8,128)(2,1)S(1)}, bf16[128,256]{1,0:T(8,128)(2,1)S(1)}, u32[]{:S(2)}, u32[]{:S(2)}) %collective-permute-start.34) | collective-permute-done | bytes 65568 | tf_op jit(solution)/shard_map/ppermute | solution.py:46
  141.3 4.1 %decode.7 = (bf16[384,256]{1,0:T(8,128)(2,1)S(1)}, bf16[128,256]{1,0:T(8,128)(2,1)S(1)}) custom-call(s32[5]{0:T(128)S(1)} %stack.37.info.refs_0_, bf16[128,256]{1,0:T(8,128)(2,1)S(1)} %collective-permute-done.33.refs_1_, bf16[128,256]{1,0:T(8,128)(2,1)S(1)} %collective-permute-done.34.refs_2_, bf16[128,256]{1,0:T(8,128)(2,1)S(1)} %collective-permute-done.35.refs_3_, ...), custom_call_target="tpu_custom_call" | custom-call | tf_op jit(solution)/shard_map/decode/pallas_call | solution.py:217
  145.4 1.9 %collective-permute-start.36 = (bf16[128,256]{1,0:T(8,128)(2,1)S(1)}, bf16[128,256]{1,0:T(8,128)(2,1)S(1)}, u32[]{:S(2)}, u32[]{:S(2)}) collective-permute-start(bf16[128,256]{1,0:T(8,128)(2,1)S(1)} %get-tuple-element.56), channel_id=1, source_target_pairs={{0,32},{32,0},{64,96},{96,64},{128,160},{160,128},{192,224},{224,1... | collective-permute-start | bytes 196616 | tf_op jit(solution)/shard_map/ppermute | solution.py:261
  147.4 4.2 %collective-permute-done.36 = bf16[128,256]{1,0:T(8,128)(2,1)S(1)} collective-permute-done((bf16[128,256]{1,0:T(8,128)(2,1)S(1)}, bf16[128,256]{1,0:T(8,128)(2,1)S(1)}, u32[]{:S(2)}, u32[]{:S(2)}) %collective-permute-start.36) | collective-permute-done | bytes 65568 | tf_op jit(solution)/shard_map/ppermute | solution.py:261
  151.6 0.7 maximum_select_fusion.2
  (79 shorter events, 17.5 us)
Async XLA Ops:
  2.0 29.7 %collective-permute-start.10 = (bf16[2304,256]{1,0:T(8,128)(2,1)S(1)}, bf16[2304,256]{1,0:T(8,128)(2,1)}, u32[]{:S(2)}, u32[]{:S(2)}) collective-permute-start(bf16[2304,256]{1,0:T(8,128)(2,1)S(1)} %broadcast_select_fusion.2), channel_id=1, source_target_pairs={{64,96},{96,64},{128,160},{160,128},{192,224},{224,192},{256,288},... | collective-permute-start | bytes 3538952 | tf_op jit(solution)/shard_map/ppermute | solution.py:261
  31.7 15.6 %collective-permute-start.11 = (bf16[2304,256]{1,0:T(8,128)(2,1)}, bf16[2304,256]{1,0:T(8,128)(2,1)}, u32[]{:S(2)}, u32[]{:S(2)}) collective-permute-start(bf16[2304,256]{1,0:T(8,128)(2,1)} %collective-permute-done.10), channel_id=1, source_target_pairs={{64,65},{65,64},{66,67},{67,66},{68,69},{69,68},{70,71},{71,70},{7... | collective-permute-start | bytes 3538952 | tf_op jit(solution)/shard_map/ppermute | solution.py:297
  33.7 1.4 collective-permute-start
  35.7 7.7 %collective-permute-start.2 = (bf16[2,256,256]{2,1,0:T(8,128)(2,1)S(1)}, bf16[2,256,256]{2,1,0:T(8,128)(2,1)S(1)}, u32[]{:S(2)}, u32[]{:S(2)}) collective-permute-start(bf16[2,256,256]{2,1,0:T(8,128)(2,1)S(1)} %shard_map.64), channel_id=1, source_target_pairs={{0,32},{1,33},{2,34},{3,35},{4,36},{5,37},{6,38},{7,39},{8,40},{9,... | collective-permute-start | bytes 786440 | tf_op jit(solution)/shard_map/ppermute | solution.py:273
  36.3 8.9 %collective-permute-start.9 = (f32[2,256]{1,0:T(2,128)S(1)}, f32[2,256]{1,0:T(2,128)S(1)}, u32[]{:S(2)}, u32[]{:S(2)}) collective-permute-start(f32[2,256]{1,0:T(2,128)S(1)} %pad_maximum_fusion.refs_3_.refs_1_), channel_id=1, source_target_pairs={{0,32},{32,0},{64,96},{96,64},{128,160},{160,128},{192,224},{224,1... | collective-permute-start | bytes 6152 | tf_op jit(solution)/shard_map/ppermute | solution.py:261
  40.2 17.3 %collective-permute-start.21 = (bf16[1152,256]{1,0:T(8,128)(2,1)S(1)}, bf16[1152,256]{1,0:T(8,128)(2,1)S(1)}, u32[]{:S(2)}, u32[]{:S(2)}) collective-permute-start(bf16[1152,256]{1,0:T(8,128)(2,1)S(1)} %constant_dynamic-slice_fusion), channel_id=1, source_target_pairs={{256,288},{288,256},{320,352},{352,320},{384,416},{416,384},{448,4... | collective-permute-start | bytes 1769480 | tf_op jit(solution)/shard_map/ppermute | solution.py:261
  43.9 2.1 %collective-permute-start.3 = (bf16[128,256]{1,0:T(8,128)(2,1)S(1)}, bf16[128,256]{1,0:T(8,128)(2,1)S(1)}, u32[]{:S(2)}, u32[]{:S(2)}) collective-permute-start(bf16[128,256]{1,0:T(8,128)(2,1)S(1)} %get-tuple-element.58), channel_id=1, source_target_pairs={{32,97},{33,98},{34,99},{35,100},{36,101},{37,102},{38,103},{39,10... | collective-permute-start | bytes 196616 | tf_op jit(solution)/shard_map/ppermute | solution.py:278
  44.6 2.1 %collective-permute-start.4 = (bf16[128,256]{1,0:T(8,128)(2,1)S(1)}, bf16[128,256]{1,0:T(8,128)(2,1)S(1)}, u32[]{:S(2)}, u32[]{:S(2)}) collective-permute-start(bf16[128,256]{1,0:T(8,128)(2,1)S(1)} %get-tuple-element.58), channel_id=1, source_target_pairs={{32,96},{33,97},{34,98},{35,99},{36,100},{37,101},{38,102},{39,103... | collective-permute-start | bytes 196616 | tf_op jit(solution)/shard_map/ppermute | solution.py:278
  45.3 4.7 %collective-permute-start.5 = (bf16[128,256]{1,0:T(8,128)(2,1)S(1)}, bf16[128,256]{1,0:T(8,128)(2,1)S(1)}, u32[]{:S(2)}, u32[]{:S(2)}) collective-permute-start(bf16[128,256]{1,0:T(8,128)(2,1)S(1)} %get-tuple-element.58), channel_id=1, source_target_pairs={{33,96},{34,97},{35,98},{36,99},{37,100},{38,101},{39,102},{40,103... | collective-permute-start | bytes 196616 | tf_op jit(solution)/shard_map/ppermute | solution.py:278
  46.0 4.0 %collective-permute-start.6 = (bf16[128,256]{1,0:T(8,128)(2,1)S(1)}, bf16[128,256]{1,0:T(8,128)(2,1)S(1)}, u32[]{:S(2)}, u32[]{:S(2)}) collective-permute-start(bf16[128,256]{1,0:T(8,128)(2,1)S(1)} %get-tuple-element.57), channel_id=1, source_target_pairs={{32,65},{33,66},{34,67},{35,68},{36,69},{37,70},{38,71},{39,72},{4... | collective-permute-start | bytes 196616 | tf_op jit(solution)/shard_map/ppermute | solution.py:278
  46.7 3.3 %collective-permute-start.7 = (bf16[128,256]{1,0:T(8,128)(2,1)S(1)}, bf16[128,256]{1,0:T(8,128)(2,1)S(1)}, u32[]{:S(2)}, u32[]{:S(2)}) collective-permute-start(bf16[128,256]{1,0:T(8,128)(2,1)S(1)} %get-tuple-element.57), channel_id=1, source_target_pairs={{32,64},{33,65},{34,66},{35,67},{36,68},{37,69},{38,70},{39,71},{4... | collective-permute-start | bytes 196616 | tf_op jit(solution)/shard_map/ppermute | solution.py:278
  47.4 2.6 %collective-permute-start.8 = (bf16[128,256]{1,0:T(8,128)(2,1)S(1)}, bf16[128,256]{1,0:T(8,128)(2,1)S(1)}, u32[]{:S(2)}, u32[]{:S(2)}) collective-permute-start(bf16[128,256]{1,0:T(8,128)(2,1)S(1)} %get-tuple-element.57), channel_id=1, source_target_pairs={{33,64},{34,65},{35,66},{36,67},{37,68},{38,69},{39,70},{40,71},{4... | collective-permute-start | bytes 196616 | tf_op jit(solution)/shard_map/ppermute | solution.py:278
  51.3 8.2 %collective-permute-start.14 = (bf16[128,256]{1,0:T(8,128)(2,1)S(1)}, bf16[128,256]{1,0:T(8,128)(2,1)S(1)}, u32[]{:S(2)}, u32[]{:S(2)}) collective-permute-start(bf16[128,256]{1,0:T(8,128)(2,1)S(1)} %get-tuple-element.30), channel_id=1, source_target_pairs={{98,129},{97,130},{100,131},{99,132},{102,133},{101,134},{104,135}... | collective-permute-start | bytes 196616 | tf_op jit(solution)/shard_map/ppermute | solution.py:340
  52.0 7.5 %collective-permute-start.13 = (bf16[128,256]{1,0:T(8,128)(2,1)S(1)}, bf16[128,256]{1,0:T(8,128)(2,1)S(1)}, u32[]{:S(2)}, u32[]{:S(2)}) collective-permute-start(bf16[128,256]{1,0:T(8,128)(2,1)S(1)} %collective-permute-done.12.refs_1_), channel_id=1, source_target_pairs={{128,129},{129,128},{130,131},{131,130},{132,133},{133,132},{134,1... | collective-permute-start | bytes 196616 | tf_op jit(solution)/shard_map/ppermute | solution.py:356
  52.7 9.4 %collective-permute-start.23 = (bf16[256,256]{1,0:T(8,128)(2,1)S(1)}, bf16[256,256]{1,0:T(8,128)(2,1)S(1)}, u32[]{:S(2)}, u32[]{:S(2)}) collective-permute-start(bf16[256,256]{1,0:T(8,128)(2,1)S(1)} %fusion), channel_id=1, source_target_pairs={{0,32},{32,0},{1,33},{33,1},{2,34},{34,2},{3,35},{35,3},{4,36},{36... | collective-permute-start | bytes 393224 | tf_op jit(solution)/shard_map/ppermute | solution.py:261
  57.6 10.1 %collective-permute-start.22 = (bf16[1152,256]{1,0:T(8,128)(2,1)S(1)}, bf16[1152,256]{1,0:T(8,128)(2,1)S(1)}, u32[]{:S(2)}, u32[]{:S(2)}) collective-permute-start(bf16[1152,256]{1,0:T(8,128)(2,1)S(1)} %collective-permute-done.21), channel_id=1, source_target_pairs={{256,257},{257,256},{258,259},{259,258},{260,261},{261,260},{262,2... | collective-permute-start | bytes 1769480 | tf_op jit(solution)/shard_map/ppermute | solution.py:297
  60.1 2.1 %collective-permute-start.15 = (bf16[128,256]{1,0:T(8,128)(2,1)S(1)}, bf16[128,256]{1,0:T(8,128)(2,1)S(1)}, u32[]{:S(2)}, u32[]{:S(2)}) collective-permute-start(bf16[128,256]{1,0:T(8,128)(2,1)S(1)} %get-tuple-element.32), channel_id=1, source_target_pairs={{128,225},{129,226},{130,227},{131,228},{132,229},{133,230},{134,2... | collective-permute-start | bytes 196616 | tf_op jit(solution)/shard_map/ppermute | solution.py:46
  60.7 1.4 collective-permute-start.16
  62.8 4.2 %collective-permute-start.18 = (bf16[384,256]{1,0:T(8,128)(2,1)S(1)}, bf16[384,256]{1,0:T(8,128)(2,1)S(1)}, u32[]{:S(2)}, u32[]{:S(2)}) collective-permute-start(bf16[384,256]{1,0:T(8,128)(2,1)S(1)} %get-tuple-element.34), channel_id=1, source_target_pairs={{224,256},{225,257},{226,258},{227,259},{228,260},{229,261},{230,2... | collective-permute-start | bytes 589832 | tf_op jit(solution)/shard_map/ppermute | solution.py:46
  63.6 6.0 %collective-permute-start.20 = (bf16[128,256]{1,0:T(8,128)(2,1)S(1)}, bf16[128,256]{1,0:T(8,128)(2,1)S(1)}, u32[]{:S(2)}, u32[]{:S(2)}) collective-permute-start(bf16[128,256]{1,0:T(8,128)(2,1)S(1)} %get-tuple-element.35), channel_id=1, source_target_pairs={{226,257},{225,258},{228,259},{227,260},{230,261},{229,262},{232,2... | collective-permute-start | bytes 196616 | tf_op jit(solution)/shard_map/ppermute | solution.py:340
  64.4 8.9 %collective-permute-start.27 = (bf16[128,256]{1,0:T(8,128)(2,1)S(1)}, bf16[128,256]{1,0:T(8,128)(2,1)S(1)}, u32[]{:S(2)}, u32[]{:S(2)}) collective-permute-start(bf16[128,256]{1,0:T(8,128)(2,1)S(1)} %slice_select_fusion), channel_id=1, source_target_pairs={{0,481},{1,482},{2,483},{3,484},{4,485},{5,486},{6,487},{7,488},{8... | collective-permute-start | bytes 196616 | tf_op jit(solution)/shard_map/ppermute | solution.py:46
  65.7 15.8 %collective-permute-start.28 = (bf16[384,256]{1,0:T(8,128)(2,1)S(1)}, bf16[384,256]{1,0:T(8,128)(2,1)S(1)}, u32[]{:S(2)}, u32[]{:S(2)}) collective-permute-start(bf16[384,256]{1,0:T(8,128)(2,1)S(1)} %get-tuple-element.45.refs_11_), channel_id=1, source_target_pairs={{0,480},{1,481},{2,482},{3,483},{4,484},{5,485},{6,486},{7,487},{8... | collective-permute-start | bytes 589832 | tf_op jit(solution)/shard_map/ppermute | solution.py:46
  67.0 2.7 %collective-permute-start.19 = (bf16[384,256]{1,0:T(8,128)(2,1)S(1)}, bf16[384,256]{1,0:T(8,128)(2,1)S(1)}, u32[]{:S(2)}, u32[]{:S(2)}) collective-permute-start(bf16[384,256]{1,0:T(8,128)(2,1)S(1)} %collective-permute-done.18.refs_1_), channel_id=1, source_target_pairs={{256,257},{257,256},{258,259},{259,258},{260,261},{261,260},{262,2... | collective-permute-start | bytes 589832 | tf_op jit(solution)/shard_map/ppermute | solution.py:356
  68.3 13.2 %collective-permute-start.29 = (bf16[128,256]{1,0:T(8,128)(2,1)S(1)}, bf16[128,256]{1,0:T(8,128)(2,1)S(1)}, u32[]{:S(2)}, u32[]{:S(2)}) collective-permute-start(bf16[128,256]{1,0:T(8,128)(2,1)S(1)} %slice_select_fusion), channel_id=1, source_target_pairs={{1,480},{2,481},{3,482},{4,483},{5,484},{6,485},{7,486},{8,487},{9... | collective-permute-start | bytes 196616 | tf_op jit(solution)/shard_map/ppermute | solution.py:46
  70.4 11.1 %collective-permute-start.24 = (bf16[128,256]{1,0:T(8,128)(2,1)S(1)}, bf16[128,256]{1,0:T(8,128)(2,1)S(1)}, u32[]{:S(2)}, u32[]{:S(2)}) collective-permute-start(bf16[128,256]{1,0:T(8,128)(2,1)S(1)} %get-tuple-element.37), channel_id=1, source_target_pairs={{256,353},{257,354},{258,355},{259,356},{260,357},{261,358},{262,3... | collective-permute-start | bytes 196616 | tf_op jit(solution)/shard_map/ppermute | solution.py:46
  71.1 10.4 %collective-permute-start.25 = (bf16[128,256]{1,0:T(8,128)(2,1)S(1)}, bf16[128,256]{1,0:T(8,128)(2,1)S(1)}, u32[]{:S(2)}, u32[]{:S(2)}) collective-permute-start(bf16[128,256]{1,0:T(8,128)(2,1)S(1)} %get-tuple-element.37), channel_id=1, source_target_pairs={{256,352},{257,353},{258,354},{259,355},{260,356},{261,357},{262,3... | collective-permute-start | bytes 196616 | tf_op jit(solution)/shard_map/ppermute | solution.py:46
  73.3 8.2 %collective-permute-start.26 = (bf16[128,256]{1,0:T(8,128)(2,1)S(1)}, bf16[128,256]{1,0:T(8,128)(2,1)S(1)}, u32[]{:S(2)}, u32[]{:S(2)}) collective-permute-start(bf16[128,256]{1,0:T(8,128)(2,1)S(1)} %get-tuple-element.37), channel_id=1, source_target_pairs={{257,352},{258,353},{259,354},{260,355},{261,356},{262,357},{263,3... | collective-permute-start | bytes 196616 | tf_op jit(solution)/shard_map/ppermute | solution.py:46
  82.8 1.4 collective-permute-start.32
  84.7 51.1 %collective-permute-start.33 = (bf16[128,256]{1,0:T(8,128)(2,1)S(1)}, bf16[128,256]{1,0:T(8,128)(2,1)S(1)}, u32[]{:S(2)}, u32[]{:S(2)}) collective-permute-start(bf16[128,256]{1,0:T(8,128)(2,1)S(1)} %get-tuple-element.41), channel_id=1, source_target_pairs={{384,481},{385,482},{386,483},{387,484},{388,485},{389,486},{390,4... | collective-permute-start | bytes 196616 | tf_op jit(solution)/shard_map/ppermute | solution.py:46
  86.0 54.8 %collective-permute-start.34 = (bf16[128,256]{1,0:T(8,128)(2,1)S(1)}, bf16[128,256]{1,0:T(8,128)(2,1)S(1)}, u32[]{:S(2)}, u32[]{:S(2)}) collective-permute-start(bf16[128,256]{1,0:T(8,128)(2,1)S(1)} %get-tuple-element.41), channel_id=1, source_target_pairs={{384,480},{385,481},{386,482},{387,483},{388,484},{389,485},{390,4... | collective-permute-start | bytes 196616 | tf_op jit(solution)/shard_map/ppermute | solution.py:46
  87.3 54.0 %collective-permute-start.35 = (bf16[128,256]{1,0:T(8,128)(2,1)S(1)}, bf16[128,256]{1,0:T(8,128)(2,1)S(1)}, u32[]{:S(2)}, u32[]{:S(2)}) collective-permute-start(bf16[128,256]{1,0:T(8,128)(2,1)S(1)} %get-tuple-element.41), channel_id=1, source_target_pairs={{385,480},{386,481},{387,482},{388,483},{389,484},{390,485},{391,4... | collective-permute-start | bytes 196616 | tf_op jit(solution)/shard_map/ppermute | solution.py:46
  145.4 6.2 %collective-permute-start.36 = (bf16[128,256]{1,0:T(8,128)(2,1)S(1)}, bf16[128,256]{1,0:T(8,128)(2,1)S(1)}, u32[]{:S(2)}, u32[]{:S(2)}) collective-permute-start(bf16[128,256]{1,0:T(8,128)(2,1)S(1)} %get-tuple-element.56), channel_id=1, source_target_pairs={{0,32},{32,0},{64,96},{96,64},{128,160},{160,128},{192,224},{224,1... | collective-permute-start | bytes 196616 | tf_op jit(solution)/shard_map/ppermute | solution.py:261
  (11 other events, 183.1 us)

commit v4 on v3

--- a/solution.py
+++ b/solution.py
@@ -13,7 +13,6 @@
 CH = 256
 BLOCK = ROWS * COLS
 TAPS = 9 * CH
-HALF = TAPS // 2
 SECTIONS = 16
 STRIPS = 32
 HEIGHT = ROWS * STRIPS
@@ -144,7 +143,7 @@
                 skip_narrow = skips[1].at[0 : 2 * BLOCK]
                 skip_wide = [skips[0], skips[1].at[2 * BLOCK : 3 * BLOCK], skips[2]]
         bias = refs.pop(0)
-        weights = [refs.pop(0) for _ in range(2 * kinds)]
+        weights = [refs.pop(0) for _ in range(6 if doubled else 2 * kinds)]
         prev0 = refs.pop(0)
         out0 = refs.pop(0)
         out1 = refs.pop(0)
@@ -160,8 +159,7 @@
             out0[...] = prev0[...]
             out1[...] = prev0[2 * BLOCK : 3 * BLOCK]
 
-        @pl.when(active != 0)
-        def _():
+        def compute(weights):
             def piece(index):
                 if mated:
                     if index == 1:
@@ -207,6 +205,23 @@
                     out0[2 * BLOCK : 3 * BLOCK] = value.astype(BF16)
                     out1[...] = value.astype(BF16)
 
+        if doubled:
+            mine, taken, passed = weights[0:2], weights[2:4], weights[4:6]
+            for parity in range(2):
+                for core in range(2):
+                    remote = (
+                        [taken[0], passed[1]] if core == 0 else [passed[0], taken[1]]
+                    )
+
+                    @pl.when((active != 0) & (info[5] == parity) & (info[3] == core))
+                    def _():
+                        compute(mine + remote if parity == 0 else remote + mine)
+        else:
+
+            @pl.when(active != 0)
+            def _():
+                compute(weights)
+
     def call(info, xs, skips, bias, weights, prev0):
         operands = [info, *xs, *skips, bias, *weights, prev0]
         vmem = pl.BlockSpec(memory_space=pltpu.VMEM)
@@ -237,7 +252,7 @@
     parity = section % 2
     group = section // 2
     micro = jnp.where(group % 2 == 0, parity, 1 - parity)
-    info = jnp.stack([group, strip * ROWS, micro, core, section]).astype(jnp.int32)
+    info = jnp.stack([group, strip * ROWS, micro, core, section, parity]).astype(jnp.int32)
     images, info, core_zero, even, group_zero, micro_zero = lax.optimization_barrier(
         (images, info, core == 0, parity == 0, group == 0, micro == 0)
     )
@@ -264,9 +279,17 @@
     image = images.reshape(2, BLOCK, CH)
     below = shift_in_section(image, 0, -1)
     above = shift_in_section(image, 0, 1)
-    fetched = [
-        partner(jnp.where(core_zero, own[0], own[1]), pairs_from),
-        partner(lax.dynamic_slice_in_dim(own[2], core * HALF, HALF, axis=0), decoders),
+    taken = [
+        lax.ppermute(
+            own[c],
+            JOINT,
+            [
+                (i * STRIPS + p, (i ^ 1) * STRIPS + p)
+                for i in pairs_from
+                for p in range(c, STRIPS, 2)
+            ],
+        )
+        for c in range(2)
     ]
 
     wide = single_kernel(0, 4)(info, (above, image, below), both, own[0], own[1])
@@ -285,6 +308,7 @@
                 ],
             )
     other = partner(both)
+    skip_weight = partner(own[2], decoders)
     give = jnp.where(even, wide[1], jnp.concatenate([close[0], close[0]], axis=0))
     got = partner(give, range(2))
     level = jnp.where(
@@ -293,17 +317,17 @@
         jnp.concatenate([got, close[1]], axis=0),
     )
 
-    swapped = [
+    passed = [
         lax.ppermute(
-            half,
+            taken[c],
             JOINT,
             [
-                (s * STRIPS + a, s * STRIPS + b)
-                for s in (decoders if index == 1 else pairs_from)
-                for a, b in cores
+                (i * STRIPS + p, i * STRIPS + (p ^ 1))
+                for i in pairs_from
+                for p in range(c, STRIPS, 2)
             ],
         )
-        for index, half in enumerate(fetched)
+        for c in range(2)
     ]
     bias = jnp.where(
         even,
@@ -317,15 +341,10 @@
     def by_core(at_zero, at_one):
         return jnp.where(core_zero, at_zero, at_one)
 
-    skip_halves = jnp.where(
-        core_zero,
-        jnp.concatenate([fetched[1], swapped[1]], axis=0),
-        jnp.concatenate([swapped[1], fetched[1]], axis=0),
-    )
     by_kind = [
-        in_order(own[0], by_core(fetched[0], swapped[0])),
-        in_order(own[1], by_core(swapped[0], fetched[0])),
-        in_order(own[2], skip_halves),
+        in_order(own[0], by_core(taken[0], passed[0])),
+        in_order(own[1], by_core(passed[1], taken[1])),
+        in_order(own[2], skip_weight),
     ]
     all_weights = [pair[0] for pair in by_kind] + [pair[1] for pair in by_kind]
     encode_weights = all_weights[0:2] + all_weights[3:5]
@@ -357,7 +376,8 @@
             straight,
             JOINT,
             [
-                (place(following, m) * STRIPS + a, place(following, m) * STRIPS + b)
+                (place(g, m) * STRIPS + a, place(g, m) * STRIPS + b)
+                for g in range(2, GROUPS, 2)
                 for m in range(2)
                 for a, b in cores
             ],
@@ -366,15 +386,23 @@
 
     for phase in range(1, middle):
         encode = phase_kernel(phase, False, doubled=phase == 1, mated=phase % 2 == 0)
-        kept, last = encode(info, xs, (), bias, encode_weights, kept)
+        kept, last = encode(
+            info,
+            xs,
+            (),
+            bias,
+            [*own[:2], *taken, *passed] if phase == 1 else encode_weights,
+            kept,
+        )
         xs = onward(last, phase, kept if phase + 1 == middle else None)
-    mirror = [(g, GROUPS - 1 - g) for g in range(middle - 1)]
-    kept = jnp.where(group_zero, level, kept)
-    last = jnp.where(group_zero, level[2 * BLOCK :], last)
-    late = tuple(
-        send(kept if shift == 0 else last, [(a, b, shift) for a, b in mirror])
-        for shift in (1, 0, -1)
-    )
+        if phase == middle - 2:
+            mirror = [(g, GROUPS - 1 - g) for g in range(middle - 1)]
+            kept = jnp.where(group_zero, level, kept)
+            last = jnp.where(group_zero, level[2 * BLOCK :], last)
+            late = tuple(
+                send(kept if shift == 0 else last, [(a, b, shift) for a, b in mirror])
+                for shift in (1, 0, -1)
+            )
     for phase in range(middle, GROUPS):
         shared = phase == middle
         decode = phase_kernel(phase, True, mated=phase % 2 == 0, shared=shared)

time: 153 us -> 159 us (1.039)
  the two profiles are of different devices: /device:TPU:318 before, /device:TPU:254 now
where the time goes in v4:
time: 159 us; the launch traced here: 158 us
  waiting for transfers between devices  104 us (65%)
  starting transfers between devices  38.3 us (24%)
  Pallas kernels  8.76 us (6%)
  local copies, waits for them, and re-layouts  3.61 us (2%)
  other arithmetic  2.4 us (2%)
    ppermute x15, waiting for transfers between devices, send(): return lax.ppermute(block, JOINT, route(moves))  55.8 us
    ppermute x2, waiting for transfers between devices, body(): lax.ppermute(own[c], JOINT, [(i * STRIPS + p, (i ^ 1) * STRIPS + p) for i...  25.6 us
    ppermute x4, waiting for transfers between devices, partner(): return lax.ppermute(block, 'section', [(i, i ^ 1) for i in sections])  22.4 us
    ppermute x15, starting transfers between devices, send(): return lax.ppermute(block, JOINT, route(moves))  13.9 us
    ppermute x4, starting transfers between devices, partner(): return lax.ppermute(block, 'section', [(i, i ^ 1) for i in sections])  8.06 us
    pallas_call x7, Pallas kernels, call(): pl.pallas_call(kernel, out_shape=(jax.ShapeDtypeStruct((3 * BLOCK, CH), B...  7.62 us
    ppermute x6, starting transfers between devices, body(): lax.ppermute(close[to], JOINT, [(STRIPS + p, place(1, to) * STRIPS + p +...  3.98 us
    unnamed x20, local copies, waits for them, and re-layouts  3.48 us
  transfers between devices with their start and end apart: 38, of which 8 were waited for; matrix products, arithmetic and copies ran while one was open for 1% of the time, Pallas kernels for 2%

profile of v4, /device:TPU:254, one launch (start us, length us, event | category | flops | bytes accessed | tf_op | source)
XLA Modules:
  0.0 157.8 jit_solution(16572477122171241159)
XLA Ops:
  0.0 2.7 %collective-permute-start.10 = (bf16[2304,256]{1,0:T(8,128)(2,1)}, bf16[2304,256]{1,0:T(8,128)(2,1)S(1)}, u32[]{:S(2)}, u32[]{:S(2)}) collective-permute-start(bf16[2304,256]{1,0:T(8,128)(2,1)} %bitcast.32), channel_id=1, source_target_pairs={{64,96},{66,98},{68,100},{70,102},{72,104},{74,106},{76,108},{78,1... | collective-permute-start | bytes 3538952 | tf_op jit(solution)/shard_map/ppermute | solution.py:283
  2.7 0.7 collective-permute-start.11
  5.0 25.6 %collective-permute-done.10.refs_10_ = bf16[2304,256]{1,0:T(8,128)(2,1)S(1)} collective-permute-done((bf16[2304,256]{1,0:T(8,128)(2,1)}, bf16[2304,256]{1,0:T(8,128)(2,1)S(1)}, u32[]{:S(2)}, u32[]{:S(2)}) %collective-permute-start.10) | collective-permute-done | bytes 1179680 | tf_op jit(solution)/shard_map/ppermute | solution.py:283
  30.5 1.4 collective-permute-start.12
  31.9 1.3 collective-permute-start.13
  33.2 0.7 pad_maximum_fusion.refs_3_.refs_1_
  34.0 1.3 copy-done
  35.2 1.3 copy-done.2
  36.5 0.9 copy-done.4
  38.0 0.8 collective-permute-start.2
  40.8 2.7 %collective-permute-start.9 = (f32[2,256]{1,0:T(2,128)S(1)}, f32[2,256]{1,0:T(2,128)S(1)}, u32[]{:S(2)}, u32[]{:S(2)}) collective-permute-start(f32[2,256]{1,0:T(2,128)S(1)} %pad_maximum_fusion.refs_3_.refs_1_), channel_id=1, source_target_pairs={{0,32},{32,0},{64,96},{96,64},{128,160},{160,128},{192,224},{224,1... | collective-permute-start | bytes 6152 | tf_op jit(solution)/shard_map/ppermute | solution.py:276
  43.6 2.7 %collective-permute-done.9 = f32[2,256]{1,0:T(2,128)S(1)} collective-permute-done((f32[2,256]{1,0:T(2,128)S(1)}, f32[2,256]{1,0:T(2,128)S(1)}, u32[]{:S(2)}, u32[]{:S(2)}) %collective-permute-start.9) | collective-permute-done | bytes 2080 | tf_op jit(solution)/shard_map/ppermute | solution.py:276
  49.8 2.7 %collective-permute-start.24 = (bf16[2304,256]{1,0:T(8,128)(2,1)S(1)}, bf16[2304,256]{1,0:T(8,128)(2,1)S(1)}, u32[]{:S(2)}, u32[]{:S(2)}) collective-permute-start(bf16[2304,256]{1,0:T(8,128)(2,1)S(1)} %bitcast.39), channel_id=1, source_target_pairs={{256,288},{288,256},{320,352},{352,320},{384,416},{416,384},{448,4... | collective-permute-start | bytes 3538952 | tf_op jit(solution)/shard_map/ppermute | solution.py:276
  53.2 0.8 collective-permute-start.14
  55.0 0.8 collective-permute-start.15
  59.0 1.3 collective-permute-start.29
  60.9 0.7 collective-permute-start.21
  61.6 1.3 collective-permute-start.28
  63.6 0.7 collective-permute-start.22
  64.2 15.4 %collective-permute-done.24 = bf16[2304,256]{1,0:T(8,128)(2,1)S(1)} collective-permute-done((bf16[2304,256]{1,0:T(8,128)(2,1)S(1)}, bf16[2304,256]{1,0:T(8,128)(2,1)S(1)}, u32[]{:S(2)}, u32[]{:S(2)}) %collective-permute-start.24) | collective-permute-done | bytes 1179680 | tf_op jit(solution)/shard_map/ppermute | solution.py:276
  79.9 1.3 collective-permute-start.30
  83.8 6.7 %collective-permute-done.30.refs_6_ = bf16[128,256]{1,0:T(8,128)(2,1)S(1)} collective-permute-done((bf16[128,256]{1,0:T(8,128)(2,1)S(1)}, bf16[128,256]{1,0:T(8,128)(2,1)S(1)}, u32[]{:S(2)}, u32[]{:S(2)}) %collective-permute-start.30) | collective-permute-done | bytes 65568 | tf_op jit(solution)/shard_map/ppermute | solution.py:45
  93.8 1.3 collective-permute-start.34
  95.1 1.3 collective-permute-start.35
  96.4 1.3 collective-permute-start.36
  97.7 43.1 %collective-permute-done.34.refs_1_ = bf16[128,256]{1,0:T(8,128)(2,1)S(1)} collective-permute-done((bf16[128,256]{1,0:T(8,128)(2,1)S(1)}, bf16[128,256]{1,0:T(8,128)(2,1)S(1)}, u32[]{:S(2)}, u32[]{:S(2)}) %collective-permute-start.34) | collective-permute-done | bytes 65568 | tf_op jit(solution)/shard_map/ppermute | solution.py:45
  140.8 4.7 %collective-permute-done.35.refs_2_ = bf16[128,256]{1,0:T(8,128)(2,1)S(1)} collective-permute-done((bf16[128,256]{1,0:T(8,128)(2,1)S(1)}, bf16[128,256]{1,0:T(8,128)(2,1)S(1)}, u32[]{:S(2)}, u32[]{:S(2)}) %collective-permute-start.35) | collective-permute-done | bytes 65568 | tf_op jit(solution)/shard_map/ppermute | solution.py:45
  145.5 1.3 collective-permute-done.36.refs_3_
  146.8 4.2 %decode.7 = (bf16[384,256]{1,0:T(8,128)(2,1)S(1)}, bf16[128,256]{1,0:T(8,128)(2,1)S(1)}) custom-call(s32[6]{0:T(128)S(1)} %stack.41.info.refs_0_, bf16[128,256]{1,0:T(8,128)(2,1)S(1)} %collective-permute-done.34.refs_1_, bf16[128,256]{1,0:T(8,128)(2,1)S(1)} %collective-permute-done.35.refs_2_, bf16[128,256]{1,0:T(8,128)(2,1)S(1)} %collective-permute-done.36.refs_3_, ...), custom_call_target="tpu_custom_call" | custom-call | tf_op jit(solution)/shard_map/decode/pallas_call | solution.py:232
  151.0 1.9 %collective-permute-start.37 = (bf16[128,256]{1,0:T(8,128)(2,1)S(1)}, bf16[128,256]{1,0:T(8,128)(2,1)S(1)}, u32[]{:S(2)}, u32[]{:S(2)}) collective-permute-start(bf16[128,256]{1,0:T(8,128)(2,1)S(1)} %get-tuple-element.54), channel_id=1, source_target_pairs={{0,32},{32,0},{64,96},{96,64},{128,160},{160,128},{192,224},{224,1... | collective-permute-start | bytes 196616 | tf_op jit(solution)/shard_map/ppermute | solution.py:276
  152.9 4.2 %collective-permute-done.37 = bf16[128,256]{1,0:T(8,128)(2,1)S(1)} collective-permute-done((bf16[128,256]{1,0:T(8,128)(2,1)S(1)}, bf16[128,256]{1,0:T(8,128)(2,1)S(1)}, u32[]{:S(2)}, u32[]{:S(2)}) %collective-permute-start.37) | collective-permute-done | bytes 65568 | tf_op jit(solution)/shard_map/ppermute | solution.py:276
  157.1 0.7 maximum_select_fusion.1
  (89 shorter events, 19.2 us)
Async XLA Ops:
  0.0 30.5 %collective-permute-start.10 = (bf16[2304,256]{1,0:T(8,128)(2,1)}, bf16[2304,256]{1,0:T(8,128)(2,1)S(1)}, u32[]{:S(2)}, u32[]{:S(2)}) collective-permute-start(bf16[2304,256]{1,0:T(8,128)(2,1)} %bitcast.32), channel_id=1, source_target_pairs={{64,96},{66,98},{68,100},{70,102},{72,104},{74,106},{76,108},{78,1... | collective-permute-start | bytes 3538952 | tf_op jit(solution)/shard_map/ppermute | solution.py:283
  2.7 29.2 %collective-permute-start.11 = (bf16[2304,256]{1,0:T(8,128)(2,1)}, bf16[2304,256]{1,0:T(8,128)(2,1)S(1)}, u32[]{:S(2)}, u32[]{:S(2)}) collective-permute-start(bf16[2304,256]{1,0:T(8,128)(2,1)} %bitcast.28), channel_id=1, source_target_pairs={{65,97},{67,99},{69,101},{71,103},{73,105},{75,107},{77,109},{79,1... | collective-permute-start | bytes 3538952 | tf_op jit(solution)/shard_map/ppermute | solution.py:283
  3.6 30.3 %collective-permute-start = (bf16[2,128,256]{2,1,0:T(8,128)(2,1)}, bf16[2,128,256]{2,1,0:T(8,128)(2,1)S(1)}, u32[]{:S(2)}, u32[]{:S(2)}) collective-permute-start(bf16[2,128,256]{2,1,0:T(8,128)(2,1)} %bitcast.36), channel_id=1, source_target_pairs={{0,1},{1,2},{2,3},{3,4},{4,5},{5,6},{6,7},{7,8},{8,9},{9,10},{10,1... | collective-permute-start | bytes 393224 | tf_op jit(solution)/shard_map/ppermute | solution.py:265
  4.3 29.6 %collective-permute-start.1 = (bf16[2,128,256]{2,1,0:T(8,128)(2,1)}, bf16[2,128,256]{2,1,0:T(8,128)(2,1)S(1)}, u32[]{:S(2)}, u32[]{:S(2)}) collective-permute-start(bf16[2,128,256]{2,1,0:T(8,128)(2,1)} %bitcast.37), channel_id=1, source_target_pairs={{1,0},{2,1},{3,2},{4,3},{5,4},{6,5},{7,6},{8,7},{9,8},{10,9},{11,1... | collective-permute-start | bytes 393224 | tf_op jit(solution)/shard_map/ppermute | solution.py:265
  30.5 22.0 %collective-permute-start.12 = (bf16[2304,256]{1,0:T(8,128)(2,1)S(1)}, bf16[2304,256]{1,0:T(8,128)(2,1)S(1)}, u32[]{:S(2)}, u32[]{:S(2)}) collective-permute-start(bf16[2304,256]{1,0:T(8,128)(2,1)S(1)} %collective-permute-done.10.refs_10_), channel_id=1, source_target_pairs={{64,65},{66,67},{68,69},{70,71},{72,73},{74,75},{76,77},{78,79},{8... | collective-permute-start | bytes 3538952 | tf_op jit(solution)/shard_map/ppermute | solution.py:321
  31.9 20.6 %collective-permute-start.13 = (bf16[2304,256]{1,0:T(8,128)(2,1)S(1)}, bf16[2304,256]{1,0:T(8,128)(2,1)S(1)}, u32[]{:S(2)}, u32[]{:S(2)}) collective-permute-start(bf16[2304,256]{1,0:T(8,128)(2,1)S(1)} %collective-permute-done.11.refs_11_), channel_id=1, source_target_pairs={{65,64},{67,66},{69,68},{71,70},{73,72},{75,74},{77,76},{79,78},{8... | collective-permute-start | bytes 3538952 | tf_op jit(solution)/shard_map/ppermute | solution.py:321
  39.4 7.5 %collective-permute-start.3 = (bf16[128,256]{1,0:T(8,128)(2,1)S(1)}, bf16[128,256]{1,0:T(8,128)(2,1)S(1)}, u32[]{:S(2)}, u32[]{:S(2)}) collective-permute-start(bf16[128,256]{1,0:T(8,128)(2,1)S(1)} %get-tuple-element.56), channel_id=1, source_target_pairs={{32,97},{33,98},{34,99},{35,100},{36,101},{37,102},{38,103},{39,10... | collective-permute-start | bytes 196616 | tf_op jit(solution)/shard_map/ppermute | solution.py:301
  40.1 8.9 %collective-permute-start.20 = (bf16[256,256]{1,0:T(8,128)(2,1)S(1)}, bf16[256,256]{1,0:T(8,128)(2,1)S(1)}, u32[]{:S(2)}, u32[]{:S(2)}) collective-permute-start(bf16[256,256]{1,0:T(8,128)(2,1)S(1)} %fusion), channel_id=1, source_target_pairs={{0,32},{32,0},{1,33},{33,1},{2,34},{34,2},{3,35},{35,3},{4,36},{36... | collective-permute-start | bytes 393224 | tf_op jit(solution)/shard_map/ppermute | solution.py:276
  40.8 5.5 %collective-permute-start.9 = (f32[2,256]{1,0:T(2,128)S(1)}, f32[2,256]{1,0:T(2,128)S(1)}, u32[]{:S(2)}, u32[]{:S(2)}) collective-permute-start(f32[2,256]{1,0:T(2,128)S(1)} %pad_maximum_fusion.refs_3_.refs_1_), channel_id=1, source_target_pairs={{0,32},{32,0},{64,96},{96,64},{128,160},{160,128},{192,224},{224,1... | collective-permute-start | bytes 6152 | tf_op jit(solution)/shard_map/ppermute | solution.py:276
  47.0 1.4 collective-permute-start.5
  47.7 2.1 %collective-permute-start.6 = (bf16[128,256]{1,0:T(8,128)(2,1)S(1)}, bf16[128,256]{1,0:T(8,128)(2,1)S(1)}, u32[]{:S(2)}, u32[]{:S(2)}) collective-permute-start(bf16[128,256]{1,0:T(8,128)(2,1)S(1)} %get-tuple-element.55), channel_id=1, source_target_pairs={{32,65},{33,66},{34,67},{35,68},{36,69},{37,70},{38,71},{39,72},{4... | collective-permute-start | bytes 196616 | tf_op jit(solution)/shard_map/ppermute | solution.py:301
  48.4 4.2 %collective-permute-start.7 = (bf16[128,256]{1,0:T(8,128)(2,1)S(1)}, bf16[128,256]{1,0:T(8,128)(2,1)S(1)}, u32[]{:S(2)}, u32[]{:S(2)}) collective-permute-start(bf16[128,256]{1,0:T(8,128)(2,1)S(1)} %get-tuple-element.55), channel_id=1, source_target_pairs={{32,64},{33,65},{34,66},{35,67},{36,68},{37,69},{38,70},{39,71},{4... | collective-permute-start | bytes 196616 | tf_op jit(solution)/shard_map/ppermute | solution.py:301
  49.1 3.5 %collective-permute-start.8 = (bf16[128,256]{1,0:T(8,128)(2,1)S(1)}, bf16[128,256]{1,0:T(8,128)(2,1)S(1)}, u32[]{:S(2)}, u32[]{:S(2)}) collective-permute-start(bf16[128,256]{1,0:T(8,128)(2,1)S(1)} %get-tuple-element.55), channel_id=1, source_target_pairs={{33,64},{34,65},{35,66},{36,67},{37,68},{38,69},{39,70},{40,71},{4... | collective-permute-start | bytes 196616 | tf_op jit(solution)/shard_map/ppermute | solution.py:301
  49.8 29.9 %collective-permute-start.24 = (bf16[2304,256]{1,0:T(8,128)(2,1)S(1)}, bf16[2304,256]{1,0:T(8,128)(2,1)S(1)}, u32[]{:S(2)}, u32[]{:S(2)}) collective-permute-start(bf16[2304,256]{1,0:T(8,128)(2,1)S(1)} %bitcast.39), channel_id=1, source_target_pairs={{256,288},{288,256},{320,352},{352,320},{384,416},{416,384},{448,4... | collective-permute-start | bytes 3538952 | tf_op jit(solution)/shard_map/ppermute | solution.py:276
  53.2 1.8 %collective-permute-start.14 = (bf16[128,256]{1,0:T(8,128)(2,1)S(1)}, bf16[128,256]{1,0:T(8,128)(2,1)S(1)}, u32[]{:S(2)}, u32[]{:S(2)}) collective-permute-start(bf16[128,256]{1,0:T(8,128)(2,1)S(1)} %get-tuple-element.29), channel_id=1, source_target_pairs={{96,128},{97,129},{98,130},{99,131},{100,132},{101,133},{102,134},... | collective-permute-start | bytes 196616 | tf_op jit(solution)/shard_map/ppermute | solution.py:45
  54.0 2.2 %collective-permute-start.16 = (bf16[128,256]{1,0:T(8,128)(2,1)S(1)}, bf16[128,256]{1,0:T(8,128)(2,1)S(1)}, u32[]{:S(2)}, u32[]{:S(2)}) collective-permute-start(bf16[128,256]{1,0:T(8,128)(2,1)S(1)} %get-tuple-element.29), channel_id=1, source_target_pairs={{98,129},{97,130},{100,131},{99,132},{102,133},{101,134},{104,135}... | collective-permute-start | bytes 196616 | tf_op jit(solution)/shard_map/ppermute | solution.py:359
  56.8 3.4 %collective-permute-start.17 = (bf16[128,256]{1,0:T(8,128)(2,1)S(1)}, bf16[128,256]{1,0:T(8,128)(2,1)S(1)}, u32[]{:S(2)}, u32[]{:S(2)}) collective-permute-start(bf16[128,256]{1,0:T(8,128)(2,1)S(1)} %get-tuple-element.32), channel_id=1, source_target_pairs={{128,225},{129,226},{130,227},{131,228},{132,229},{133,230},{134,2... | collective-permute-start | bytes 196616 | tf_op jit(solution)/shard_map/ppermute | solution.py:45
  57.5 2.8 %collective-permute-start.18 = (bf16[128,256]{1,0:T(8,128)(2,1)S(1)}, bf16[128,256]{1,0:T(8,128)(2,1)S(1)}, u32[]{:S(2)}, u32[]{:S(2)}) collective-permute-start(bf16[128,256]{1,0:T(8,128)(2,1)S(1)} %get-tuple-element.32), channel_id=1, source_target_pairs={{128,224},{129,225},{130,226},{131,227},{132,228},{133,229},{134,2... | collective-permute-start | bytes 196616 | tf_op jit(solution)/shard_map/ppermute | solution.py:45
  58.2 2.1 %collective-permute-start.19 = (bf16[128,256]{1,0:T(8,128)(2,1)S(1)}, bf16[128,256]{1,0:T(8,128)(2,1)S(1)}, u32[]{:S(2)}, u32[]{:S(2)}) collective-permute-start(bf16[128,256]{1,0:T(8,128)(2,1)S(1)} %get-tuple-element.32), channel_id=1, source_target_pairs={{129,224},{130,225},{131,226},{132,227},{133,228},{134,229},{135,2... | collective-permute-start | bytes 196616 | tf_op jit(solution)/shard_map/ppermute | solution.py:45
  59.0 31.6 %collective-permute-start.29 = (bf16[384,256]{1,0:T(8,128)(2,1)S(1)}, bf16[384,256]{1,0:T(8,128)(2,1)S(1)}, u32[]{:S(2)}, u32[]{:S(2)}) collective-permute-start(bf16[384,256]{1,0:T(8,128)(2,1)S(1)} %get-tuple-element.45.refs_9_), channel_id=1, source_target_pairs={{0,480},{1,481},{2,482},{3,483},{4,484},{5,485},{6,486},{7,487},{8... | collective-permute-start | bytes 589832 | tf_op jit(solution)/shard_map/ppermute | solution.py:45
  60.9 2.7 %collective-permute-start.21 = (bf16[384,256]{1,0:T(8,128)(2,1)S(1)}, bf16[384,256]{1,0:T(8,128)(2,1)S(1)}, u32[]{:S(2)}, u32[]{:S(2)}) collective-permute-start(bf16[384,256]{1,0:T(8,128)(2,1)S(1)} %get-tuple-element.35.refs_11_), channel_id=1, source_target_pairs={{224,256},{225,257},{226,258},{227,259},{228,260},{229,261},{230,2... | collective-permute-start | bytes 589832 | tf_op jit(solution)/shard_map/ppermute | solution.py:45
  61.6 21.6 %collective-permute-start.28 = (bf16[128,256]{1,0:T(8,128)(2,1)S(1)}, bf16[128,256]{1,0:T(8,128)(2,1)S(1)}, u32[]{:S(2)}, u32[]{:S(2)}) collective-permute-start(bf16[128,256]{1,0:T(8,128)(2,1)S(1)} %slice_select_fusion), channel_id=1, source_target_pairs={{0,481},{1,482},{2,483},{3,484},{4,485},{5,486},{6,487},{7,488},{8... | collective-permute-start | bytes 196616 | tf_op jit(solution)/shard_map/ppermute | solution.py:45
  62.9 18.3 %collective-permute-start.23 = (bf16[128,256]{1,0:T(8,128)(2,1)S(1)}, bf16[128,256]{1,0:T(8,128)(2,1)S(1)}, u32[]{:S(2)}, u32[]{:S(2)}) collective-permute-start(bf16[128,256]{1,0:T(8,128)(2,1)S(1)} %get-tuple-element.36), channel_id=1, source_target_pairs={{226,257},{225,258},{228,259},{227,260},{230,261},{229,262},{232,2... | collective-permute-start | bytes 196616 | tf_op jit(solution)/shard_map/ppermute | solution.py:359
  63.6 17.7 %collective-permute-start.22 = (bf16[384,256]{1,0:T(8,128)(2,1)S(1)}, bf16[384,256]{1,0:T(8,128)(2,1)S(1)}, u32[]{:S(2)}, u32[]{:S(2)}) collective-permute-start(bf16[384,256]{1,0:T(8,128)(2,1)S(1)} %collective-permute-done.21.refs_1_), channel_id=1, source_target_pairs={{128,129},{129,128},{130,131},{131,130},{132,133},{133,132},{134,1... | collective-permute-start | bytes 589832 | tf_op jit(solution)/shard_map/ppermute | solution.py:375
  79.9 10.7 %collective-permute-start.30 = (bf16[128,256]{1,0:T(8,128)(2,1)S(1)}, bf16[128,256]{1,0:T(8,128)(2,1)S(1)}, u32[]{:S(2)}, u32[]{:S(2)}) collective-permute-start(bf16[128,256]{1,0:T(8,128)(2,1)S(1)} %slice_select_fusion), channel_id=1, source_target_pairs={{1,480},{2,481},{3,482},{4,483},{5,484},{6,485},{7,486},{8,487},{9... | collective-permute-start | bytes 196616 | tf_op jit(solution)/shard_map/ppermute | solution.py:45
  81.8 8.8 %collective-permute-start.25 = (bf16[128,256]{1,0:T(8,128)(2,1)S(1)}, bf16[128,256]{1,0:T(8,128)(2,1)S(1)}, u32[]{:S(2)}, u32[]{:S(2)}) collective-permute-start(bf16[128,256]{1,0:T(8,128)(2,1)S(1)} %get-tuple-element.37), channel_id=1, source_target_pairs={{256,353},{257,354},{258,355},{259,356},{260,357},{261,358},{262,3... | collective-permute-start | bytes 196616 | tf_op jit(solution)/shard_map/ppermute | solution.py:45
  82.5 8.1 %collective-permute-start.26 = (bf16[128,256]{1,0:T(8,128)(2,1)S(1)}, bf16[128,256]{1,0:T(8,128)(2,1)S(1)}, u32[]{:S(2)}, u32[]{:S(2)}) collective-permute-start(bf16[128,256]{1,0:T(8,128)(2,1)S(1)} %get-tuple-element.37), channel_id=1, source_target_pairs={{256,352},{257,353},{258,354},{259,355},{260,356},{261,357},{262,3... | collective-permute-start | bytes 196616 | tf_op jit(solution)/shard_map/ppermute | solution.py:45
  83.2 7.4 %collective-permute-start.27 = (bf16[128,256]{1,0:T(8,128)(2,1)S(1)}, bf16[128,256]{1,0:T(8,128)(2,1)S(1)}, u32[]{:S(2)}, u32[]{:S(2)}) collective-permute-start(bf16[128,256]{1,0:T(8,128)(2,1)S(1)} %get-tuple-element.37), channel_id=1, source_target_pairs={{257,352},{258,353},{259,354},{260,355},{261,356},{262,357},{263,3... | collective-permute-start | bytes 196616 | tf_op jit(solution)/shard_map/ppermute | solution.py:45
  93.8 47.0 %collective-permute-start.34 = (bf16[128,256]{1,0:T(8,128)(2,1)S(1)}, bf16[128,256]{1,0:T(8,128)(2,1)S(1)}, u32[]{:S(2)}, u32[]{:S(2)}) collective-permute-start(bf16[128,256]{1,0:T(8,128)(2,1)S(1)} %get-tuple-element.41), channel_id=1, source_target_pairs={{384,481},{385,482},{386,483},{387,484},{388,485},{389,486},{390,4... | collective-permute-start | bytes 196616 | tf_op jit(solution)/shard_map/ppermute | solution.py:45
  95.1 50.4 %collective-permute-start.35 = (bf16[128,256]{1,0:T(8,128)(2,1)S(1)}, bf16[128,256]{1,0:T(8,128)(2,1)S(1)}, u32[]{:S(2)}, u32[]{:S(2)}) collective-permute-start(bf16[128,256]{1,0:T(8,128)(2,1)S(1)} %get-tuple-element.41), channel_id=1, source_target_pairs={{384,480},{385,481},{386,482},{387,483},{388,484},{389,485},{390,4... | collective-permute-start | bytes 196616 | tf_op jit(solution)/shard_map/ppermute | solution.py:45
  96.4 50.4 %collective-permute-start.36 = (bf16[128,256]{1,0:T(8,128)(2,1)S(1)}, bf16[128,256]{1,0:T(8,128)(2,1)S(1)}, u32[]{:S(2)}, u32[]{:S(2)}) collective-permute-start(bf16[128,256]{1,0:T(8,128)(2,1)S(1)} %get-tuple-element.41), channel_id=1, source_target_pairs={{385,480},{386,481},{387,482},{388,483},{389,484},{390,485},{391,4... | collective-permute-start | bytes 196616 | tf_op jit(solution)/shard_map/ppermute | solution.py:45
  151.0 6.2 %collective-permute-start.37 = (bf16[128,256]{1,0:T(8,128)(2,1)S(1)}, bf16[128,256]{1,0:T(8,128)(2,1)S(1)}, u32[]{:S(2)}, u32[]{:S(2)}) collective-permute-start(bf16[128,256]{1,0:T(8,128)(2,1)S(1)} %get-tuple-element.54), channel_id=1, source_target_pairs={{0,32},{32,0},{64,96},{96,64},{128,160},{160,128},{192,224},{224,1... | collective-permute-start | bytes 196616 | tf_op jit(solution)/shard_map/ppermute | solution.py:276
  (17 other events, 54.9 us)

commit v5 on v4

--- a/solution.py
+++ b/solution.py
@@ -354,30 +354,25 @@
 
     def onward(last, phase, centre=None):
         following = phase + 1
-        if phase % 2:
-            straight = send(last if centre is None else centre, [(phase, following, 0)])
-            far = lax.ppermute(
-                last,
-                JOINT,
-                [
-                    (
-                        place(phase, m) * STRIPS + p + (1 if p % 2 else -1),
-                        place(following, m) * STRIPS + p,
-                    )
-                    for m in range(2)
-                    for p in range(1, STRIPS - 1)
-                ],
-            )
-        else:
-            down = send(last, [(phase, following, 1)])
-            up = send(last, [(phase, following, -1)])
-            return (down, send(last, [(phase, following, 0)]), up)
+        straight = send(last if centre is None else centre, [(phase, following, 0)])
+        far = lax.ppermute(
+            last,
+            JOINT,
+            [
+                (
+                    place(phase, m) * STRIPS + p + (1 if p % 2 else -1),
+                    place(following, m) * STRIPS + p,
+                )
+                for m in range(2)
+                for p in range(1, STRIPS - 1)
+            ],
+        )
         mate = lax.ppermute(
             straight,
             JOINT,
             [
                 (place(g, m) * STRIPS + a, place(g, m) * STRIPS + b)
-                for g in range(2, GROUPS, 2)
+                for g in range(2 + following % 2, GROUPS, 2)
                 for m in range(2)
                 for a, b in cores
             ],
@@ -385,7 +380,7 @@
         return (straight, mate, far)
 
     for phase in range(1, middle):
-        encode = phase_kernel(phase, False, doubled=phase == 1, mated=phase % 2 == 0)
+        encode = phase_kernel(phase, False, doubled=phase == 1, mated=phase > 1)
         kept, last = encode(
             info,
             xs,
@@ -405,7 +400,7 @@
             )
     for phase in range(middle, GROUPS):
         shared = phase == middle
-        decode = phase_kernel(phase, True, mated=phase % 2 == 0, shared=shared)
+        decode = phase_kernel(phase, True, mated=phase > 1, shared=shared)
         kept, last = decode(
             info, xs, () if shared else late, bias, all_weights, kept
         )

time: 159 us -> 160 us (level)
  the two profiles are of different devices: /device:TPU:254 before, /device:TPU:382 now
where the time goes in v5:
time: 160 us; the launch traced here: 159 us
  waiting for transfers between devices  100 us (62%)
  starting transfers between devices  41.6 us (26%)
  Pallas kernels  9.5 us (6%)
  local copies, waits for them, and re-layouts  3.6 us (2%)
  other arithmetic  3.55 us (2%)
    ppermute x9, waiting for transfers between devices, send(): return lax.ppermute(block, JOINT, route(moves))  52.1 us
    ppermute x2, waiting for transfers between devices, body(): lax.ppermute(own[c], JOINT, [(i * STRIPS + p, (i ^ 1) * STRIPS + p) for i...  27.1 us
    ppermute x4, waiting for transfers between devices, partner(): return lax.ppermute(block, 'section', [(i, i ^ 1) for i in sections])  18.9 us
    ppermute x9, starting transfers between devices, send(): return lax.ppermute(block, JOINT, route(moves))  8.63 us
    pallas_call x7, Pallas kernels, call(): pl.pallas_call(kernel, out_shape=(jax.ShapeDtypeStruct((3 * BLOCK, CH), B...  8.37 us
    ppermute x4, starting transfers between devices, partner(): return lax.ppermute(block, 'section', [(i, i ^ 1) for i in sections])  8.06 us
    ppermute x6, starting transfers between devices, onward(): lax.ppermute(straight, JOINT, [(place(g, m) * STRIPS + a, place(g, m) * S...  8.04 us
    ppermute x6, starting transfers between devices, onward(): lax.ppermute(last, JOINT, [(place(phase, m) * STRIPS + p + (1 if p % 2 el...  4.62 us
  transfers between devices with their start and end apart: 38, of which 8 were waited for; matrix products, arithmetic and copies ran while one was open for 2% of the time, Pallas kernels for 3%

profile of v5, /device:TPU:382, one launch (start us, length us, event | category | flops | bytes accessed | tf_op | source)
XLA Modules:
  0.0 159.5 jit_solution(4425691879309772113)
XLA Ops:
  0.0 2.7 %collective-permute-start.10 = (bf16[2304,256]{1,0:T(8,128)(2,1)}, bf16[2304,256]{1,0:T(8,128)(2,1)S(1)}, u32[]{:S(2)}, u32[]{:S(2)}) collective-permute-start(bf16[2304,256]{1,0:T(8,128)(2,1)} %bitcast.32), channel_id=1, source_target_pairs={{64,96},{66,98},{68,100},{70,102},{72,104},{74,106},{76,108},{78,1... | collective-permute-start | bytes 3538952 | tf_op jit(solution)/shard_map/ppermute | solution.py:283
  2.7 0.7 collective-permute-start.11
  3.5 27.1 %collective-permute-done.10.refs_10_ = bf16[2304,256]{1,0:T(8,128)(2,1)S(1)} collective-permute-done((bf16[2304,256]{1,0:T(8,128)(2,1)}, bf16[2304,256]{1,0:T(8,128)(2,1)S(1)}, u32[]{:S(2)}, u32[]{:S(2)}) %collective-permute-start.10) | collective-permute-done | bytes 1179680 | tf_op jit(solution)/shard_map/ppermute | solution.py:283
  30.5 1.4 collective-permute-start.12
  31.9 1.3 collective-permute-start.13
  35.4 1.3 copy-done
  36.7 1.3 copy-done.2
  38.0 0.9 copy-done.4
  39.5 0.8 collective-permute-start.2
  40.3 2.7 %collective-permute-start.9 = (f32[2,256]{1,0:T(2,128)S(1)}, f32[2,256]{1,0:T(2,128)S(1)}, u32[]{:S(2)}, u32[]{:S(2)}) collective-permute-start(f32[2,256]{1,0:T(2,128)S(1)} %pad_maximum_fusion.refs_3_.refs_1_), channel_id=1, source_target_pairs={{0,32},{32,0},{64,96},{96,64},{128,160},{160,128},{192,224},{224,1... | collective-permute-start | bytes 6152 | tf_op jit(solution)/shard_map/ppermute | solution.py:276
  45.0 0.8 collective-permute-done.9
  48.6 2.7 %collective-permute-start.24 = (bf16[2304,256]{1,0:T(8,128)(2,1)S(1)}, bf16[2304,256]{1,0:T(8,128)(2,1)S(1)}, u32[]{:S(2)}, u32[]{:S(2)}) collective-permute-start(bf16[2304,256]{1,0:T(8,128)(2,1)S(1)} %bitcast.39), channel_id=1, source_target_pairs={{256,288},{288,256},{320,352},{352,320},{384,416},{416,384},{448,4... | collective-permute-start | bytes 3538952 | tf_op jit(solution)/shard_map/ppermute | solution.py:276
  52.1 1.3 encode.3
  53.5 0.8 collective-permute-start.14
  54.9 1.5 broadcast_select_fusion.4
  56.4 0.8 collective-permute-start.15
  59.6 1.9 %collective-permute-start.18 = (bf16[128,256]{1,0:T(8,128)(2,1)S(1)}, bf16[128,256]{1,0:T(8,128)(2,1)S(1)}, u32[]{:S(2)}, u32[]{:S(2)}) collective-permute-start(bf16[128,256]{1,0:T(8,128)(2,1)S(1)} %collective-permute-done.17.refs_1_), channel_id=1, source_target_pairs={{224,225},{225,224},{226,227},{227,226},{228,229},{229,228},{230,2... | collective-permute-start | bytes 196616 | tf_op jit(solution)/shard_map/ppermute | solution.py:370
  61.6 1.1 collective-permute-done.18.refs_2_
  65.3 13.9 %collective-permute-done.24 = bf16[2304,256]{1,0:T(8,128)(2,1)S(1)} collective-permute-done((bf16[2304,256]{1,0:T(8,128)(2,1)S(1)}, bf16[2304,256]{1,0:T(8,128)(2,1)S(1)}, u32[]{:S(2)}, u32[]{:S(2)}) %collective-permute-start.24) | collective-permute-done | bytes 1179680 | tf_op jit(solution)/shard_map/ppermute | solution.py:276
  79.4 1.3 collective-permute-start.29
  82.0 1.3 collective-permute-start.28
  83.3 1.3 collective-permute-start.30
  85.3 2.0 %collective-permute-start.26 = (bf16[128,256]{1,0:T(8,128)(2,1)S(1)}, bf16[128,256]{1,0:T(8,128)(2,1)S(1)}, u32[]{:S(2)}, u32[]{:S(2)}) collective-permute-start(bf16[128,256]{1,0:T(8,128)(2,1)S(1)} %collective-permute-done.25.refs_1_), channel_id=1, source_target_pairs={{224,225},{225,224},{226,227},{227,226},{228,229},{229,228},{230,2... | collective-permute-start | bytes 196616 | tf_op jit(solution)/shard_map/ppermute | solution.py:370
  87.3 13.2 %collective-permute-done.28.refs_4_ = bf16[128,256]{1,0:T(8,128)(2,1)S(1)} collective-permute-done((bf16[128,256]{1,0:T(8,128)(2,1)S(1)}, bf16[128,256]{1,0:T(8,128)(2,1)S(1)}, u32[]{:S(2)}, u32[]{:S(2)}) %collective-permute-start.28) | collective-permute-done | bytes 65568 | tf_op jit(solution)/shard_map/ppermute | solution.py:45
  103.8 1.3 collective-permute-start.34
  105.1 1.3 collective-permute-start.36
  106.4 38.9 %collective-permute-done.34.refs_1_ = bf16[128,256]{1,0:T(8,128)(2,1)S(1)} collective-permute-done((bf16[128,256]{1,0:T(8,128)(2,1)S(1)}, bf16[128,256]{1,0:T(8,128)(2,1)S(1)}, u32[]{:S(2)}, u32[]{:S(2)}) %collective-permute-start.34) | collective-permute-done | bytes 65568 | tf_op jit(solution)/shard_map/ppermute | solution.py:45
  145.3 1.9 %collective-permute-start.35 = (bf16[128,256]{1,0:T(8,128)(2,1)S(1)}, bf16[128,256]{1,0:T(8,128)(2,1)S(1)}, u32[]{:S(2)}, u32[]{:S(2)}) collective-permute-start(bf16[128,256]{1,0:T(8,128)(2,1)S(1)} %collective-permute-done.34.refs_1_), channel_id=1, source_target_pairs={{224,225},{225,224},{226,227},{227,226},{228,229},{229,228},{230,2... | collective-permute-start | bytes 196616 | tf_op jit(solution)/shard_map/ppermute | solution.py:370
  147.2 1.2 collective-permute-done.35.refs_2_
  148.5 4.2 %decode.7 = (bf16[384,256]{1,0:T(8,128)(2,1)S(1)}, bf16[128,256]{1,0:T(8,128)(2,1)S(1)}) custom-call(s32[6]{0:T(128)S(1)} %stack.41.info.refs_0_, bf16[128,256]{1,0:T(8,128)(2,1)S(1)} %collective-permute-done.34.refs_1_, bf16[128,256]{1,0:T(8,128)(2,1)S(1)} %collective-permute-done.35.refs_2_, bf16[128,256]{1,0:T(8,128)(2,1)S(1)} %collective-permute-done.36.refs_3_, ...), custom_call_target="tpu_custom_call" | custom-call | tf_op jit(solution)/shard_map/decode/pallas_call | solution.py:232
  152.7 1.9 %collective-permute-start.37 = (bf16[128,256]{1,0:T(8,128)(2,1)S(1)}, bf16[128,256]{1,0:T(8,128)(2,1)S(1)}, u32[]{:S(2)}, u32[]{:S(2)}) collective-permute-start(bf16[128,256]{1,0:T(8,128)(2,1)S(1)} %get-tuple-element.54), channel_id=1, source_target_pairs={{0,32},{32,0},{64,96},{96,64},{128,160},{160,128},{192,224},{224,1... | collective-permute-start | bytes 196616 | tf_op jit(solution)/shard_map/ppermute | solution.py:276
  154.6 4.2 %collective-permute-done.37 = bf16[128,256]{1,0:T(8,128)(2,1)S(1)} collective-permute-done((bf16[128,256]{1,0:T(8,128)(2,1)S(1)}, bf16[128,256]{1,0:T(8,128)(2,1)S(1)}, u32[]{:S(2)}, u32[]{:S(2)}) %collective-permute-start.37) | collective-permute-done | bytes 65568 | tf_op jit(solution)/shard_map/ppermute | solution.py:276
  (84 shorter events, 19.6 us)
Async XLA Ops:
  0.0 30.5 %collective-permute-start.10 = (bf16[2304,256]{1,0:T(8,128)(2,1)}, bf16[2304,256]{1,0:T(8,128)(2,1)S(1)}, u32[]{:S(2)}, u32[]{:S(2)}) collective-permute-start(bf16[2304,256]{1,0:T(8,128)(2,1)} %bitcast.32), channel_id=1, source_target_pairs={{64,96},{66,98},{68,100},{70,102},{72,104},{74,106},{76,108},{78,1... | collective-permute-start | bytes 3538952 | tf_op jit(solution)/shard_map/ppermute | solution.py:283
  2.7 29.2 %collective-permute-start.11 = (bf16[2304,256]{1,0:T(8,128)(2,1)}, bf16[2304,256]{1,0:T(8,128)(2,1)S(1)}, u32[]{:S(2)}, u32[]{:S(2)}) collective-permute-start(bf16[2304,256]{1,0:T(8,128)(2,1)} %bitcast.28), channel_id=1, source_target_pairs={{65,97},{67,99},{69,101},{71,103},{73,105},{75,107},{77,109},{79,1... | collective-permute-start | bytes 3538952 | tf_op jit(solution)/shard_map/ppermute | solution.py:283
  30.5 21.5 %collective-permute-start.12 = (bf16[2304,256]{1,0:T(8,128)(2,1)S(1)}, bf16[2304,256]{1,0:T(8,128)(2,1)S(1)}, u32[]{:S(2)}, u32[]{:S(2)}) collective-permute-start(bf16[2304,256]{1,0:T(8,128)(2,1)S(1)} %collective-permute-done.10.refs_10_), channel_id=1, source_target_pairs={{64,65},{66,67},{68,69},{70,71},{72,73},{74,75},{76,77},{78,79},{8... | collective-permute-start | bytes 3538952 | tf_op jit(solution)/shard_map/ppermute | solution.py:321
  31.9 20.1 %collective-permute-start.13 = (bf16[2304,256]{1,0:T(8,128)(2,1)S(1)}, bf16[2304,256]{1,0:T(8,128)(2,1)}, u32[]{:S(2)}, u32[]{:S(2)}) collective-permute-start(bf16[2304,256]{1,0:T(8,128)(2,1)S(1)} %collective-permute-done.11.refs_11_), channel_id=1, source_target_pairs={{65,64},{67,66},{69,68},{71,70},{73,72},{75,74},{77,76},{79,78},{8... | collective-permute-start | bytes 3538952 | tf_op jit(solution)/shard_map/ppermute | solution.py:321
  33.4 2.1 %collective-permute-start = (bf16[2,128,256]{2,1,0:T(8,128)(2,1)}, bf16[2,128,256]{2,1,0:T(8,128)(2,1)S(1)}, u32[]{:S(2)}, u32[]{:S(2)}) collective-permute-start(bf16[2,128,256]{2,1,0:T(8,128)(2,1)} %bitcast.36), channel_id=1, source_target_pairs={{0,1},{1,2},{2,3},{3,4},{4,5},{5,6},{6,7},{7,8},{8,9},{9,10},{10,1... | collective-permute-start | bytes 393224 | tf_op jit(solution)/shard_map/ppermute | solution.py:265
  39.5 3.6 %collective-permute-start.2 = (bf16[2,256,256]{2,1,0:T(8,128)(2,1)S(1)}, bf16[2,256,256]{2,1,0:T(8,128)(2,1)S(1)}, u32[]{:S(2)}, u32[]{:S(2)}) collective-permute-start(bf16[2,256,256]{2,1,0:T(8,128)(2,1)S(1)} %shard_map.64), channel_id=1, source_target_pairs={{0,32},{1,33},{2,34},{3,35},{4,36},{5,37},{6,38},{7,39},{8,40},{9,... | collective-permute-start | bytes 786440 | tf_op jit(solution)/shard_map/ppermute | solution.py:296
  40.3 5.5 %collective-permute-start.9 = (f32[2,256]{1,0:T(2,128)S(1)}, f32[2,256]{1,0:T(2,128)S(1)}, u32[]{:S(2)}, u32[]{:S(2)}) collective-permute-start(f32[2,256]{1,0:T(2,128)S(1)} %pad_maximum_fusion.refs_3_.refs_1_), channel_id=1, source_target_pairs={{0,32},{32,0},{64,96},{96,64},{128,160},{160,128},{192,224},{224,1... | collective-permute-start | bytes 6152 | tf_op jit(solution)/shard_map/ppermute | solution.py:276
  43.7 2.8 %collective-permute-start.3 = (bf16[128,256]{1,0:T(8,128)(2,1)S(1)}, bf16[128,256]{1,0:T(8,128)(2,1)S(1)}, u32[]{:S(2)}, u32[]{:S(2)}) collective-permute-start(bf16[128,256]{1,0:T(8,128)(2,1)S(1)} %get-tuple-element.56), channel_id=1, source_target_pairs={{32,97},{33,98},{34,99},{35,100},{36,101},{37,102},{38,103},{39,10... | collective-permute-start | bytes 196616 | tf_op jit(solution)/shard_map/ppermute | solution.py:301
  44.3 2.8 %collective-permute-start.4 = (bf16[128,256]{1,0:T(8,128)(2,1)S(1)}, bf16[128,256]{1,0:T(8,128)(2,1)S(1)}, u32[]{:S(2)}, u32[]{:S(2)}) collective-permute-start(bf16[128,256]{1,0:T(8,128)(2,1)S(1)} %get-tuple-element.56), channel_id=1, source_target_pairs={{32,96},{33,97},{34,98},{35,99},{36,100},{37,101},{38,102},{39,103... | collective-permute-start | bytes 196616 | tf_op jit(solution)/shard_map/ppermute | solution.py:301
  45.8 2.1 %collective-permute-start.5 = (bf16[128,256]{1,0:T(8,128)(2,1)S(1)}, bf16[128,256]{1,0:T(8,128)(2,1)S(1)}, u32[]{:S(2)}, u32[]{:S(2)}) collective-permute-start(bf16[128,256]{1,0:T(8,128)(2,1)S(1)} %get-tuple-element.56), channel_id=1, source_target_pairs={{33,96},{34,97},{35,98},{36,99},{37,100},{38,101},{39,102},{40,103... | collective-permute-start | bytes 196616 | tf_op jit(solution)/shard_map/ppermute | solution.py:301
  46.5 2.1 %collective-permute-start.6 = (bf16[128,256]{1,0:T(8,128)(2,1)S(1)}, bf16[128,256]{1,0:T(8,128)(2,1)S(1)}, u32[]{:S(2)}, u32[]{:S(2)}) collective-permute-start(bf16[128,256]{1,0:T(8,128)(2,1)S(1)} %get-tuple-element.55), channel_id=1, source_target_pairs={{32,65},{33,66},{34,67},{35,68},{36,69},{37,70},{38,71},{39,72},{4... | collective-permute-start | bytes 196616 | tf_op jit(solution)/shard_map/ppermute | solution.py:301
  47.2 4.2 %collective-permute-start.7 = (bf16[128,256]{1,0:T(8,128)(2,1)S(1)}, bf16[128,256]{1,0:T(8,128)(2,1)S(1)}, u32[]{:S(2)}, u32[]{:S(2)}) collective-permute-start(bf16[128,256]{1,0:T(8,128)(2,1)S(1)} %get-tuple-element.55), channel_id=1, source_target_pairs={{32,64},{33,65},{34,66},{35,67},{36,68},{37,69},{38,70},{39,71},{4... | collective-permute-start | bytes 196616 | tf_op jit(solution)/shard_map/ppermute | solution.py:301
  47.9 4.2 %collective-permute-start.8 = (bf16[128,256]{1,0:T(8,128)(2,1)S(1)}, bf16[128,256]{1,0:T(8,128)(2,1)S(1)}, u32[]{:S(2)}, u32[]{:S(2)}) collective-permute-start(bf16[128,256]{1,0:T(8,128)(2,1)S(1)} %get-tuple-element.55), channel_id=1, source_target_pairs={{33,64},{34,65},{35,66},{36,67},{37,68},{38,69},{39,70},{40,71},{4... | collective-permute-start | bytes 196616 | tf_op jit(solution)/shard_map/ppermute | solution.py:301
  48.6 30.6 %collective-permute-start.24 = (bf16[2304,256]{1,0:T(8,128)(2,1)S(1)}, bf16[2304,256]{1,0:T(8,128)(2,1)S(1)}, u32[]{:S(2)}, u32[]{:S(2)}) collective-permute-start(bf16[2304,256]{1,0:T(8,128)(2,1)S(1)} %bitcast.39), channel_id=1, source_target_pairs={{256,288},{288,256},{320,352},{352,320},{384,416},{416,384},{448,4... | collective-permute-start | bytes 3538952 | tf_op jit(solution)/shard_map/ppermute | solution.py:276
  51.4 7.5 %collective-permute-start.20 = (bf16[256,256]{1,0:T(8,128)(2,1)S(1)}, bf16[256,256]{1,0:T(8,128)(2,1)S(1)}, u32[]{:S(2)}, u32[]{:S(2)}) collective-permute-start(bf16[256,256]{1,0:T(8,128)(2,1)S(1)} %fusion), channel_id=1, source_target_pairs={{0,32},{32,0},{1,33},{33,1},{2,34},{34,2},{3,35},{35,3},{4,36},{36... | collective-permute-start | bytes 393224 | tf_op jit(solution)/shard_map/ppermute | solution.py:276
  53.5 3.0 %collective-permute-start.14 = (bf16[128,256]{1,0:T(8,128)(2,1)S(1)}, bf16[128,256]{1,0:T(8,128)(2,1)S(1)}, u32[]{:S(2)}, u32[]{:S(2)}) collective-permute-start(bf16[128,256]{1,0:T(8,128)(2,1)S(1)} %get-tuple-element.29), channel_id=1, source_target_pairs={{96,128},{97,129},{98,130},{99,131},{100,132},{101,133},{102,134},... | collective-permute-start | bytes 196616 | tf_op jit(solution)/shard_map/ppermute | solution.py:45
  54.3 3.3 %collective-permute-start.16 = (bf16[128,256]{1,0:T(8,128)(2,1)S(1)}, bf16[128,256]{1,0:T(8,128)(2,1)S(1)}, u32[]{:S(2)}, u32[]{:S(2)}) collective-permute-start(bf16[128,256]{1,0:T(8,128)(2,1)S(1)} %get-tuple-element.29), channel_id=1, source_target_pairs={{98,129},{97,130},{100,131},{99,132},{102,133},{101,134},{104,135}... | collective-permute-start | bytes 196616 | tf_op jit(solution)/shard_map/ppermute | solution.py:358
  58.2 1.4 collective-permute-start.17
  58.9 2.7 %collective-permute-start.19 = (bf16[128,256]{1,0:T(8,128)(2,1)S(1)}, bf16[128,256]{1,0:T(8,128)(2,1)S(1)}, u32[]{:S(2)}, u32[]{:S(2)}) collective-permute-start(bf16[128,256]{1,0:T(8,128)(2,1)S(1)} %get-tuple-element.32), channel_id=1, source_target_pairs={{130,225},{129,226},{132,227},{131,228},{134,229},{133,230},{136,2... | collective-permute-start | bytes 196616 | tf_op jit(solution)/shard_map/ppermute | solution.py:358
  59.6 3.1 %collective-permute-start.18 = (bf16[128,256]{1,0:T(8,128)(2,1)S(1)}, bf16[128,256]{1,0:T(8,128)(2,1)S(1)}, u32[]{:S(2)}, u32[]{:S(2)}) collective-permute-start(bf16[128,256]{1,0:T(8,128)(2,1)S(1)} %collective-permute-done.17.refs_1_), channel_id=1, source_target_pairs={{224,225},{225,224},{226,227},{227,226},{228,229},{229,228},{230,2... | collective-permute-start | bytes 196616 | tf_op jit(solution)/shard_map/ppermute | solution.py:370
  64.0 16.8 %collective-permute-start.23 = (bf16[128,256]{1,0:T(8,128)(2,1)S(1)}, bf16[128,256]{1,0:T(8,128)(2,1)S(1)}, u32[]{:S(2)}, u32[]{:S(2)}) collective-permute-start(bf16[128,256]{1,0:T(8,128)(2,1)S(1)} %get-tuple-element.36), channel_id=1, source_target_pairs={{226,257},{225,258},{228,259},{227,260},{230,261},{229,262},{232,2... | collective-permute-start | bytes 196616 | tf_op jit(solution)/shard_map/ppermute | solution.py:358
  64.7 16.1 %collective-permute-start.22 = (bf16[384,256]{1,0:T(8,128)(2,1)S(1)}, bf16[384,256]{1,0:T(8,128)(2,1)S(1)}, u32[]{:S(2)}, u32[]{:S(2)}) collective-permute-start(bf16[384,256]{1,0:T(8,128)(2,1)S(1)} %collective-permute-done.21.refs_1_), channel_id=1, source_target_pairs={{128,129},{129,128},{130,131},{131,130},{132,133},{133,132},{134,1... | collective-permute-start | bytes 589832 | tf_op jit(solution)/shard_map/ppermute | solution.py:370
  79.4 21.1 %collective-permute-start.29 = (bf16[384,256]{1,0:T(8,128)(2,1)S(1)}, bf16[384,256]{1,0:T(8,128)(2,1)S(1)}, u32[]{:S(2)}, u32[]{:S(2)}) collective-permute-start(bf16[384,256]{1,0:T(8,128)(2,1)S(1)} %get-tuple-element.45.refs_9_), channel_id=1, source_target_pairs={{0,480},{1,481},{2,482},{3,483},{4,484},{5,485},{6,486},{7,487},{8... | collective-permute-start | bytes 589832 | tf_op jit(solution)/shard_map/ppermute | solution.py:45
  81.3 4.0 %collective-permute-start.25 = (bf16[128,256]{1,0:T(8,128)(2,1)S(1)}, bf16[128,256]{1,0:T(8,128)(2,1)S(1)}, u32[]{:S(2)}, u32[]{:S(2)}) collective-permute-start(bf16[128,256]{1,0:T(8,128)(2,1)S(1)} %get-tuple-element.37), channel_id=1, source_target_pairs={{256,352},{257,353},{258,354},{259,355},{260,356},{261,357},{262,3... | collective-permute-start | bytes 196616 | tf_op jit(solution)/shard_map/ppermute | solution.py:45
  82.0 18.5 %collective-permute-start.28 = (bf16[128,256]{1,0:T(8,128)(2,1)S(1)}, bf16[128,256]{1,0:T(8,128)(2,1)S(1)}, u32[]{:S(2)}, u32[]{:S(2)}) collective-permute-start(bf16[128,256]{1,0:T(8,128)(2,1)S(1)} %slice_select_fusion), channel_id=1, source_target_pairs={{0,481},{1,482},{2,483},{3,484},{4,485},{5,486},{6,487},{7,488},{8... | collective-permute-start | bytes 196616 | tf_op jit(solution)/shard_map/ppermute | solution.py:45
  83.3 17.2 %collective-permute-start.30 = (bf16[128,256]{1,0:T(8,128)(2,1)S(1)}, bf16[128,256]{1,0:T(8,128)(2,1)S(1)}, u32[]{:S(2)}, u32[]{:S(2)}) collective-permute-start(bf16[128,256]{1,0:T(8,128)(2,1)S(1)} %slice_select_fusion), channel_id=1, source_target_pairs={{1,480},{2,481},{3,482},{4,483},{5,484},{6,485},{7,486},{8,487},{9... | collective-permute-start | bytes 196616 | tf_op jit(solution)/shard_map/ppermute | solution.py:45
  84.6 16.0 %collective-permute-start.27 = (bf16[128,256]{1,0:T(8,128)(2,1)S(1)}, bf16[128,256]{1,0:T(8,128)(2,1)S(1)}, u32[]{:S(2)}, u32[]{:S(2)}) collective-permute-start(bf16[128,256]{1,0:T(8,128)(2,1)S(1)} %get-tuple-element.37), channel_id=1, source_target_pairs={{258,353},{257,354},{260,355},{259,356},{262,357},{261,358},{264,3... | collective-permute-start | bytes 196616 | tf_op jit(solution)/shard_map/ppermute | solution.py:358
  85.3 15.3 %collective-permute-start.26 = (bf16[128,256]{1,0:T(8,128)(2,1)S(1)}, bf16[128,256]{1,0:T(8,128)(2,1)S(1)}, u32[]{:S(2)}, u32[]{:S(2)}) collective-permute-start(bf16[128,256]{1,0:T(8,128)(2,1)S(1)} %collective-permute-done.25.refs_1_), channel_id=1, source_target_pairs={{224,225},{225,224},{226,227},{227,226},{228,229},{229,228},{230,2... | collective-permute-start | bytes 196616 | tf_op jit(solution)/shard_map/ppermute | solution.py:370
  103.8 41.5 %collective-permute-start.34 = (bf16[128,256]{1,0:T(8,128)(2,1)S(1)}, bf16[128,256]{1,0:T(8,128)(2,1)S(1)}, u32[]{:S(2)}, u32[]{:S(2)}) collective-permute-start(bf16[128,256]{1,0:T(8,128)(2,1)S(1)} %get-tuple-element.41), channel_id=1, source_target_pairs={{384,480},{385,481},{386,482},{387,483},{388,484},{389,485},{390,4... | collective-permute-start | bytes 196616 | tf_op jit(solution)/shard_map/ppermute | solution.py:45
  105.1 42.1 %collective-permute-start.36 = (bf16[128,256]{1,0:T(8,128)(2,1)S(1)}, bf16[128,256]{1,0:T(8,128)(2,1)S(1)}, u32[]{:S(2)}, u32[]{:S(2)}) collective-permute-start(bf16[128,256]{1,0:T(8,128)(2,1)S(1)} %get-tuple-element.41), channel_id=1, source_target_pairs={{386,481},{385,482},{388,483},{387,484},{390,485},{389,486},{392,4... | collective-permute-start | bytes 196616 | tf_op jit(solution)/shard_map/ppermute | solution.py:358
  145.3 3.1 %collective-permute-start.35 = (bf16[128,256]{1,0:T(8,128)(2,1)S(1)}, bf16[128,256]{1,0:T(8,128)(2,1)S(1)}, u32[]{:S(2)}, u32[]{:S(2)}) collective-permute-start(bf16[128,256]{1,0:T(8,128)(2,1)S(1)} %collective-permute-done.34.refs_1_), channel_id=1, source_target_pairs={{224,225},{225,224},{226,227},{227,226},{228,229},{229,228},{230,2... | collective-permute-start | bytes 196616 | tf_op jit(solution)/shard_map/ppermute | solution.py:370
  152.7 6.2 %collective-permute-start.37 = (bf16[128,256]{1,0:T(8,128)(2,1)S(1)}, bf16[128,256]{1,0:T(8,128)(2,1)S(1)}, u32[]{:S(2)}, u32[]{:S(2)}) collective-permute-start(bf16[128,256]{1,0:T(8,128)(2,1)S(1)} %get-tuple-element.54), channel_id=1, source_target_pairs={{0,32},{32,0},{64,96},{96,64},{128,160},{160,128},{192,224},{224,1... | collective-permute-start | bytes 196616 | tf_op jit(solution)/shard_map/ppermute | solution.py:276
  (14 other events, 41.9 us)

commit v6 on v4

--- a/solution.py
+++ b/solution.py
@@ -129,15 +129,12 @@
     def kernel(*refs):
         refs = list(refs)
         info = refs.pop(0)
-        xs = [refs.pop(0) for _ in range(6 if doubled else 3)]
+        xs = [refs.pop(0) for _ in range(6 if doubled else 4 if shared else 3)]
         if mated:
-            straight, mate, far = xs
-            if shared:
-                mate = mate.at[2 * BLOCK : 3 * BLOCK]
-            own_rows = straight.at[2 * BLOCK : 3 * BLOCK] if shared else straight
+            own_rows, mate, far = xs[:3]
         if decoder:
             if shared:
-                skip_narrow = straight.at[0 : 2 * BLOCK]
+                skip_narrow = xs[3]
             else:
                 skips = [refs.pop(0) for _ in range(3)]
                 skip_narrow = skips[1].at[0 : 2 * BLOCK]
@@ -394,7 +391,9 @@
             [*own[:2], *taken, *passed] if phase == 1 else encode_weights,
             kept,
         )
-        xs = onward(last, phase, kept if phase + 1 == middle else None)
+        xs = onward(last, phase)
+        if phase + 1 == middle:
+            xs = (*xs, send(kept[: 2 * BLOCK], [(phase, middle, 0)]))
         if phase == middle - 2:
             mirror = [(g, GROUPS - 1 - g) for g in range(middle - 1)]
             kept = jnp.where(group_zero, level, kept)

time: 159 us -> 156 us (0.981)
  the two profiles are of different devices: /device:TPU:254 before, /device:TPU:446 now
where the time goes in v6:
time: 156 us
  waiting for transfers between devices  101 us (65%)
  starting transfers between devices  39 us (25%)
  Pallas kernels  8.76 us (6%)
  local copies, waits for them, and re-layouts  3.62 us (2%)
  other arithmetic  2.4 us (2%)
    ppermute x16, waiting for transfers between devices, send(): return lax.ppermute(block, JOINT, route(moves))  52.4 us
    ppermute x2, waiting for transfers between devices, body(): lax.ppermute(own[c], JOINT, [(i * STRIPS + p, (i ^ 1) * STRIPS + p) for i...  25.6 us
    ppermute x4, waiting for transfers between devices, partner(): return lax.ppermute(block, 'section', [(i, i ^ 1) for i in sections])  23.1 us
    ppermute x16, starting transfers between devices, send(): return lax.ppermute(block, JOINT, route(moves))  14.5 us
    ppermute x4, starting transfers between devices, partner(): return lax.ppermute(block, 'section', [(i, i ^ 1) for i in sections])  8.06 us
    pallas_call x7, Pallas kernels, call(): pl.pallas_call(kernel, out_shape=(jax.ShapeDtypeStruct((3 * BLOCK, CH), B...  7.63 us
    ppermute x6, starting transfers between devices, body(): lax.ppermute(close[to], JOINT, [(STRIPS + p, place(1, to) * STRIPS + p +...  3.98 us
    unnamed x20, local copies, waits for them, and re-layouts  3.48 us
  transfers between devices with their start and end apart: 39, of which 8 were waited for; matrix products, arithmetic and copies ran while one was open for 1% of the time, Pallas kernels for 2%

profile of v6, /device:TPU:446, one launch (start us, length us, event | category | flops | bytes accessed | tf_op | source)
XLA Modules:
  0.0 155.7 jit_solution(9635388651458919472)
XLA Ops:
  0.0 2.7 %collective-permute-start.10 = (bf16[2304,256]{1,0:T(8,128)(2,1)}, bf16[2304,256]{1,0:T(8,128)(2,1)S(1)}, u32[]{:S(2)}, u32[]{:S(2)}) collective-permute-start(bf16[2304,256]{1,0:T(8,128)(2,1)} %bitcast.32), channel_id=1, source_target_pairs={{64,96},{66,98},{68,100},{70,102},{72,104},{74,106},{76,108},{78,1... | collective-permute-start | bytes 3538952 | tf_op jit(solution)/shard_map/ppermute | solution.py:280
  2.7 0.7 collective-permute-start.11
  4.3 0.7 collective-permute-start.1
  5.0 25.6 %collective-permute-done.10.refs_10_ = bf16[2304,256]{1,0:T(8,128)(2,1)S(1)} collective-permute-done((bf16[2304,256]{1,0:T(8,128)(2,1)}, bf16[2304,256]{1,0:T(8,128)(2,1)S(1)}, u32[]{:S(2)}, u32[]{:S(2)}) %collective-permute-start.10) | collective-permute-done | bytes 1179680 | tf_op jit(solution)/shard_map/ppermute | solution.py:280
  30.5 1.4 collective-permute-start.12
  31.9 1.3 collective-permute-start.13
  33.2 0.7 pad_maximum_fusion.refs_3_.refs_1_
  34.0 1.3 copy-done
  35.2 1.3 copy-done.2
  36.5 0.9 copy-done.4
  38.0 0.8 collective-permute-start.2
  39.4 0.7 collective-permute-start.3
  40.1 0.7 collective-permute-start.20
  40.8 2.7 %collective-permute-start.9 = (f32[2,256]{1,0:T(2,128)S(1)}, f32[2,256]{1,0:T(2,128)S(1)}, u32[]{:S(2)}, u32[]{:S(2)}) collective-permute-start(f32[2,256]{1,0:T(2,128)S(1)} %pad_maximum_fusion.refs_3_.refs_1_), channel_id=1, source_target_pairs={{0,32},{32,0},{64,96},{96,64},{128,160},{160,128},{192,224},{224,1... | collective-permute-start | bytes 6152 | tf_op jit(solution)/shard_map/ppermute | solution.py:273
  43.6 2.7 %collective-permute-done.9 = f32[2,256]{1,0:T(2,128)S(1)} collective-permute-done((f32[2,256]{1,0:T(2,128)S(1)}, f32[2,256]{1,0:T(2,128)S(1)}, u32[]{:S(2)}, u32[]{:S(2)}) %collective-permute-start.9) | collective-permute-done | bytes 2080 | tf_op jit(solution)/shard_map/ppermute | solution.py:273
  49.8 2.7 %collective-permute-start.25 = (bf16[2304,256]{1,0:T(8,128)(2,1)S(1)}, bf16[2304,256]{1,0:T(8,128)(2,1)S(1)}, u32[]{:S(2)}, u32[]{:S(2)}) collective-permute-start(bf16[2304,256]{1,0:T(8,128)(2,1)S(1)} %bitcast.39), channel_id=1, source_target_pairs={{256,288},{288,256},{320,352},{352,320},{384,416},{416,384},{448,4... | collective-permute-start | bytes 3538952 | tf_op jit(solution)/shard_map/ppermute | solution.py:273
  53.2 0.8 collective-permute-start.14
  55.0 0.8 collective-permute-start.15
  59.0 1.3 collective-permute-start.30
  61.6 1.3 collective-permute-start.29
  63.6 16.1 %collective-permute-done.25 = bf16[2304,256]{1,0:T(8,128)(2,1)S(1)} collective-permute-done((bf16[2304,256]{1,0:T(8,128)(2,1)S(1)}, bf16[2304,256]{1,0:T(8,128)(2,1)S(1)}, u32[]{:S(2)}, u32[]{:S(2)}) %collective-permute-start.25) | collective-permute-done | bytes 1179680 | tf_op jit(solution)/shard_map/ppermute | solution.py:273
  81.3 1.3 collective-permute-start.31
  85.2 6.5 %collective-permute-done.31.refs_6_ = bf16[128,256]{1,0:T(8,128)(2,1)S(1)} collective-permute-done((bf16[128,256]{1,0:T(8,128)(2,1)S(1)}, bf16[128,256]{1,0:T(8,128)(2,1)S(1)}, u32[]{:S(2)}, u32[]{:S(2)}) %collective-permute-start.31) | collective-permute-done | bytes 65568 | tf_op jit(solution)/shard_map/ppermute | solution.py:45
  94.9 1.3 collective-permute-start.35
  96.2 1.3 collective-permute-start.36
  97.5 1.3 collective-permute-start.37
  98.8 40.4 %collective-permute-done.35.refs_1_ = bf16[128,256]{1,0:T(8,128)(2,1)S(1)} collective-permute-done((bf16[128,256]{1,0:T(8,128)(2,1)S(1)}, bf16[128,256]{1,0:T(8,128)(2,1)S(1)}, u32[]{:S(2)}, u32[]{:S(2)}) %collective-permute-start.35) | collective-permute-done | bytes 65568 | tf_op jit(solution)/shard_map/ppermute | solution.py:45
  139.1 5.1 %collective-permute-done.36.refs_2_ = bf16[128,256]{1,0:T(8,128)(2,1)S(1)} collective-permute-done((bf16[128,256]{1,0:T(8,128)(2,1)S(1)}, bf16[128,256]{1,0:T(8,128)(2,1)S(1)}, u32[]{:S(2)}, u32[]{:S(2)}) %collective-permute-start.36) | collective-permute-done | bytes 65568 | tf_op jit(solution)/shard_map/ppermute | solution.py:45
  144.7 4.2 %decode.7 = (bf16[384,256]{1,0:T(8,128)(2,1)S(1)}, bf16[128,256]{1,0:T(8,128)(2,1)S(1)}) custom-call(s32[6]{0:T(128)S(1)} %stack.41.info.refs_0_, bf16[128,256]{1,0:T(8,128)(2,1)S(1)} %collective-permute-done.35.refs_1_, bf16[128,256]{1,0:T(8,128)(2,1)S(1)} %collective-permute-done.36.refs_2_, bf16[128,256]{1,0:T(8,128)(2,1)S(1)} %collective-permute-done.37.refs_3_, ...), custom_call_target="tpu_custom_call" | custom-call | tf_op jit(solution)/shard_map/decode/pallas_call | solution.py:229
  148.9 1.9 %collective-permute-start.38 = (bf16[128,256]{1,0:T(8,128)(2,1)S(1)}, bf16[128,256]{1,0:T(8,128)(2,1)S(1)}, u32[]{:S(2)}, u32[]{:S(2)}) collective-permute-start(bf16[128,256]{1,0:T(8,128)(2,1)S(1)} %get-tuple-element.54), channel_id=1, source_target_pairs={{0,32},{32,0},{64,96},{96,64},{128,160},{160,128},{192,224},{224,1... | collective-permute-start | bytes 196616 | tf_op jit(solution)/shard_map/ppermute | solution.py:273
  150.8 4.2 %collective-permute-done.38 = bf16[128,256]{1,0:T(8,128)(2,1)S(1)} collective-permute-done((bf16[128,256]{1,0:T(8,128)(2,1)S(1)}, bf16[128,256]{1,0:T(8,128)(2,1)S(1)}, u32[]{:S(2)}, u32[]{:S(2)}) %collective-permute-start.38) | collective-permute-done | bytes 65568 | tf_op jit(solution)/shard_map/ppermute | solution.py:273
  155.0 0.7 maximum_select_fusion.1
  (92 shorter events, 19.6 us)
Async XLA Ops:
  0.0 30.5 %collective-permute-start.10 = (bf16[2304,256]{1,0:T(8,128)(2,1)}, bf16[2304,256]{1,0:T(8,128)(2,1)S(1)}, u32[]{:S(2)}, u32[]{:S(2)}) collective-permute-start(bf16[2304,256]{1,0:T(8,128)(2,1)} %bitcast.32), channel_id=1, source_target_pairs={{64,96},{66,98},{68,100},{70,102},{72,104},{74,106},{76,108},{78,1... | collective-permute-start | bytes 3538952 | tf_op jit(solution)/shard_map/ppermute | solution.py:280
  2.7 29.2 %collective-permute-start.11 = (bf16[2304,256]{1,0:T(8,128)(2,1)}, bf16[2304,256]{1,0:T(8,128)(2,1)S(1)}, u32[]{:S(2)}, u32[]{:S(2)}) collective-permute-start(bf16[2304,256]{1,0:T(8,128)(2,1)} %bitcast.28), channel_id=1, source_target_pairs={{65,97},{67,99},{69,101},{71,103},{73,105},{75,107},{77,109},{79,1... | collective-permute-start | bytes 3538952 | tf_op jit(solution)/shard_map/ppermute | solution.py:280
  3.6 30.3 %collective-permute-start = (bf16[2,128,256]{2,1,0:T(8,128)(2,1)}, bf16[2,128,256]{2,1,0:T(8,128)(2,1)S(1)}, u32[]{:S(2)}, u32[]{:S(2)}) collective-permute-start(bf16[2,128,256]{2,1,0:T(8,128)(2,1)} %bitcast.36), channel_id=1, source_target_pairs={{0,1},{1,2},{2,3},{3,4},{4,5},{5,6},{6,7},{7,8},{8,9},{9,10},{10,1... | collective-permute-start | bytes 393224 | tf_op jit(solution)/shard_map/ppermute | solution.py:262
  4.3 29.6 %collective-permute-start.1 = (bf16[2,128,256]{2,1,0:T(8,128)(2,1)}, bf16[2,128,256]{2,1,0:T(8,128)(2,1)S(1)}, u32[]{:S(2)}, u32[]{:S(2)}) collective-permute-start(bf16[2,128,256]{2,1,0:T(8,128)(2,1)} %bitcast.37), channel_id=1, source_target_pairs={{1,0},{2,1},{3,2},{4,3},{5,4},{6,5},{7,6},{8,7},{9,8},{10,9},{11,1... | collective-permute-start | bytes 393224 | tf_op jit(solution)/shard_map/ppermute | solution.py:262
  30.5 22.0 %collective-permute-start.12 = (bf16[2304,256]{1,0:T(8,128)(2,1)S(1)}, bf16[2304,256]{1,0:T(8,128)(2,1)S(1)}, u32[]{:S(2)}, u32[]{:S(2)}) collective-permute-start(bf16[2304,256]{1,0:T(8,128)(2,1)S(1)} %collective-permute-done.10.refs_10_), channel_id=1, source_target_pairs={{64,65},{66,67},{68,69},{70,71},{72,73},{74,75},{76,77},{78,79},{8... | collective-permute-start | bytes 3538952 | tf_op jit(solution)/shard_map/ppermute | solution.py:318
  31.9 20.6 %collective-permute-start.13 = (bf16[2304,256]{1,0:T(8,128)(2,1)S(1)}, bf16[2304,256]{1,0:T(8,128)(2,1)S(1)}, u32[]{:S(2)}, u32[]{:S(2)}) collective-permute-start(bf16[2304,256]{1,0:T(8,128)(2,1)S(1)} %collective-permute-done.11.refs_11_), channel_id=1, source_target_pairs={{65,64},{67,66},{69,68},{71,70},{73,72},{75,74},{77,76},{79,78},{8... | collective-permute-start | bytes 3538952 | tf_op jit(solution)/shard_map/ppermute | solution.py:318
  39.4 7.5 %collective-permute-start.3 = (bf16[128,256]{1,0:T(8,128)(2,1)S(1)}, bf16[128,256]{1,0:T(8,128)(2,1)S(1)}, u32[]{:S(2)}, u32[]{:S(2)}) collective-permute-start(bf16[128,256]{1,0:T(8,128)(2,1)S(1)} %get-tuple-element.56), channel_id=1, source_target_pairs={{32,97},{33,98},{34,99},{35,100},{36,101},{37,102},{38,103},{39,10... | collective-permute-start | bytes 196616 | tf_op jit(solution)/shard_map/ppermute | solution.py:298
  40.1 8.9 %collective-permute-start.20 = (bf16[256,256]{1,0:T(8,128)(2,1)S(1)}, bf16[256,256]{1,0:T(8,128)(2,1)S(1)}, u32[]{:S(2)}, u32[]{:S(2)}) collective-permute-start(bf16[256,256]{1,0:T(8,128)(2,1)S(1)} %fusion), channel_id=1, source_target_pairs={{0,32},{32,0},{1,33},{33,1},{2,34},{34,2},{3,35},{35,3},{4,36},{36... | collective-permute-start | bytes 393224 | tf_op jit(solution)/shard_map/ppermute | solution.py:273
  40.8 5.5 %collective-permute-start.9 = (f32[2,256]{1,0:T(2,128)S(1)}, f32[2,256]{1,0:T(2,128)S(1)}, u32[]{:S(2)}, u32[]{:S(2)}) collective-permute-start(f32[2,256]{1,0:T(2,128)S(1)} %pad_maximum_fusion.refs_3_.refs_1_), channel_id=1, source_target_pairs={{0,32},{32,0},{64,96},{96,64},{128,160},{160,128},{192,224},{224,1... | collective-permute-start | bytes 6152 | tf_op jit(solution)/shard_map/ppermute | solution.py:273
  47.7 2.1 %collective-permute-start.6 = (bf16[128,256]{1,0:T(8,128)(2,1)S(1)}, bf16[128,256]{1,0:T(8,128)(2,1)S(1)}, u32[]{:S(2)}, u32[]{:S(2)}) collective-permute-start(bf16[128,256]{1,0:T(8,128)(2,1)S(1)} %get-tuple-element.55), channel_id=1, source_target_pairs={{32,65},{33,66},{34,67},{35,68},{36,69},{37,70},{38,71},{39,72},{4... | collective-permute-start | bytes 196616 | tf_op jit(solution)/shard_map/ppermute | solution.py:298
  48.4 4.2 %collective-permute-start.7 = (bf16[128,256]{1,0:T(8,128)(2,1)S(1)}, bf16[128,256]{1,0:T(8,128)(2,1)S(1)}, u32[]{:S(2)}, u32[]{:S(2)}) collective-permute-start(bf16[128,256]{1,0:T(8,128)(2,1)S(1)} %get-tuple-element.55), channel_id=1, source_target_pairs={{32,64},{33,65},{34,66},{35,67},{36,68},{37,69},{38,70},{39,71},{4... | collective-permute-start | bytes 196616 | tf_op jit(solution)/shard_map/ppermute | solution.py:298
  49.1 3.5 %collective-permute-start.8 = (bf16[128,256]{1,0:T(8,128)(2,1)S(1)}, bf16[128,256]{1,0:T(8,128)(2,1)S(1)}, u32[]{:S(2)}, u32[]{:S(2)}) collective-permute-start(bf16[128,256]{1,0:T(8,128)(2,1)S(1)} %get-tuple-element.55), channel_id=1, source_target_pairs={{33,64},{34,65},{35,66},{36,67},{37,68},{38,69},{39,70},{40,71},{4... | collective-permute-start | bytes 196616 | tf_op jit(solution)/shard_map/ppermute | solution.py:298
  49.8 29.9 %collective-permute-start.25 = (bf16[2304,256]{1,0:T(8,128)(2,1)S(1)}, bf16[2304,256]{1,0:T(8,128)(2,1)S(1)}, u32[]{:S(2)}, u32[]{:S(2)}) collective-permute-start(bf16[2304,256]{1,0:T(8,128)(2,1)S(1)} %bitcast.39), channel_id=1, source_target_pairs={{256,288},{288,256},{320,352},{352,320},{384,416},{416,384},{448,4... | collective-permute-start | bytes 3538952 | tf_op jit(solution)/shard_map/ppermute | solution.py:273
  53.2 1.8 %collective-permute-start.14 = (bf16[128,256]{1,0:T(8,128)(2,1)S(1)}, bf16[128,256]{1,0:T(8,128)(2,1)S(1)}, u32[]{:S(2)}, u32[]{:S(2)}) collective-permute-start(bf16[128,256]{1,0:T(8,128)(2,1)S(1)} %get-tuple-element.29), channel_id=1, source_target_pairs={{96,128},{97,129},{98,130},{99,131},{100,132},{101,133},{102,134},... | collective-permute-start | bytes 196616 | tf_op jit(solution)/shard_map/ppermute | solution.py:45
  54.0 2.2 %collective-permute-start.16 = (bf16[128,256]{1,0:T(8,128)(2,1)S(1)}, bf16[128,256]{1,0:T(8,128)(2,1)S(1)}, u32[]{:S(2)}, u32[]{:S(2)}) collective-permute-start(bf16[128,256]{1,0:T(8,128)(2,1)S(1)} %get-tuple-element.29), channel_id=1, source_target_pairs={{98,129},{97,130},{100,131},{99,132},{102,133},{101,134},{104,135}... | collective-permute-start | bytes 196616 | tf_op jit(solution)/shard_map/ppermute | solution.py:356
  56.8 3.4 %collective-permute-start.17 = (bf16[128,256]{1,0:T(8,128)(2,1)S(1)}, bf16[128,256]{1,0:T(8,128)(2,1)S(1)}, u32[]{:S(2)}, u32[]{:S(2)}) collective-permute-start(bf16[128,256]{1,0:T(8,128)(2,1)S(1)} %get-tuple-element.32), channel_id=1, source_target_pairs={{128,225},{129,226},{130,227},{131,228},{132,229},{133,230},{134,2... | collective-permute-start | bytes 196616 | tf_op jit(solution)/shard_map/ppermute | solution.py:45
  57.5 2.8 %collective-permute-start.18 = (bf16[128,256]{1,0:T(8,128)(2,1)S(1)}, bf16[128,256]{1,0:T(8,128)(2,1)S(1)}, u32[]{:S(2)}, u32[]{:S(2)}) collective-permute-start(bf16[128,256]{1,0:T(8,128)(2,1)S(1)} %get-tuple-element.32), channel_id=1, source_target_pairs={{128,224},{129,225},{130,226},{131,227},{132,228},{133,229},{134,2... | collective-permute-start | bytes 196616 | tf_op jit(solution)/shard_map/ppermute | solution.py:45
  58.2 2.1 %collective-permute-start.19 = (bf16[128,256]{1,0:T(8,128)(2,1)S(1)}, bf16[128,256]{1,0:T(8,128)(2,1)S(1)}, u32[]{:S(2)}, u32[]{:S(2)}) collective-permute-start(bf16[128,256]{1,0:T(8,128)(2,1)S(1)} %get-tuple-element.32), channel_id=1, source_target_pairs={{129,224},{130,225},{131,226},{132,227},{133,228},{134,229},{135,2... | collective-permute-start | bytes 196616 | tf_op jit(solution)/shard_map/ppermute | solution.py:45
  59.0 32.7 %collective-permute-start.30 = (bf16[384,256]{1,0:T(8,128)(2,1)S(1)}, bf16[384,256]{1,0:T(8,128)(2,1)S(1)}, u32[]{:S(2)}, u32[]{:S(2)}) collective-permute-start(bf16[384,256]{1,0:T(8,128)(2,1)S(1)} %get-tuple-element.45.refs_9_), channel_id=1, source_target_pairs={{0,480},{1,481},{2,482},{3,483},{4,484},{5,485},{6,486},{7,487},{8... | collective-permute-start | bytes 589832 | tf_op jit(solution)/shard_map/ppermute | solution.py:45
  60.9 19.5 %collective-permute-start.21 = (bf16[128,256]{1,0:T(8,128)(2,1)S(1)}, bf16[128,256]{1,0:T(8,128)(2,1)S(1)}, u32[]{:S(2)}, u32[]{:S(2)}) collective-permute-start(bf16[128,256]{1,0:T(8,128)(2,1)S(1)} %get-tuple-element.35), channel_id=1, source_target_pairs={{224,256},{225,257},{226,258},{227,259},{228,260},{229,261},{230,2... | collective-permute-start | bytes 196616 | tf_op jit(solution)/shard_map/ppermute | solution.py:45
  61.6 22.9 %collective-permute-start.29 = (bf16[128,256]{1,0:T(8,128)(2,1)S(1)}, bf16[128,256]{1,0:T(8,128)(2,1)S(1)}, u32[]{:S(2)}, u32[]{:S(2)}) collective-permute-start(bf16[128,256]{1,0:T(8,128)(2,1)S(1)} %slice_select_fusion), channel_id=1, source_target_pairs={{0,481},{1,482},{2,483},{3,484},{4,485},{5,486},{6,487},{7,488},{8... | collective-permute-start | bytes 196616 | tf_op jit(solution)/shard_map/ppermute | solution.py:45
  62.9 18.4 %collective-permute-start.23 = (bf16[128,256]{1,0:T(8,128)(2,1)S(1)}, bf16[128,256]{1,0:T(8,128)(2,1)S(1)}, u32[]{:S(2)}, u32[]{:S(2)}) collective-permute-start(bf16[128,256]{1,0:T(8,128)(2,1)S(1)} %get-tuple-element.35), channel_id=1, source_target_pairs={{226,257},{225,258},{228,259},{227,260},{230,261},{229,262},{232,2... | collective-permute-start | bytes 196616 | tf_op jit(solution)/shard_map/ppermute | solution.py:356
  79.7 2.9 %collective-permute-start.24 = (bf16[256,256]{1,0:T(8,128)(2,1)S(1)}, bf16[256,256]{1,0:T(8,128)(2,1)S(1)}, u32[]{:S(2)}, u32[]{:S(2)}) collective-permute-start(bf16[256,256]{1,0:T(8,128)(2,1)S(1)} %slice.36), channel_id=1, source_target_pairs={{224,256},{225,257},{226,258},{227,259},{228,260},{229,261},{230,2... | collective-permute-start | bytes 393224 | tf_op jit(solution)/shard_map/ppermute | solution.py:45
  80.3 2.2 %collective-permute-start.22 = (bf16[128,256]{1,0:T(8,128)(2,1)S(1)}, bf16[128,256]{1,0:T(8,128)(2,1)S(1)}, u32[]{:S(2)}, u32[]{:S(2)}) collective-permute-start(bf16[128,256]{1,0:T(8,128)(2,1)S(1)} %collective-permute-done.21.refs_1_), channel_id=1, source_target_pairs={{128,129},{129,128},{130,131},{131,130},{132,133},{133,132},{134,1... | collective-permute-start | bytes 196616 | tf_op jit(solution)/shard_map/ppermute | solution.py:372
  81.3 10.4 %collective-permute-start.31 = (bf16[128,256]{1,0:T(8,128)(2,1)S(1)}, bf16[128,256]{1,0:T(8,128)(2,1)S(1)}, u32[]{:S(2)}, u32[]{:S(2)}) collective-permute-start(bf16[128,256]{1,0:T(8,128)(2,1)S(1)} %slice_select_fusion), channel_id=1, source_target_pairs={{1,480},{2,481},{3,482},{4,483},{5,484},{6,485},{7,486},{8,487},{9... | collective-permute-start | bytes 196616 | tf_op jit(solution)/shard_map/ppermute | solution.py:45
  83.2 8.5 %collective-permute-start.26 = (bf16[128,256]{1,0:T(8,128)(2,1)S(1)}, bf16[128,256]{1,0:T(8,128)(2,1)S(1)}, u32[]{:S(2)}, u32[]{:S(2)}) collective-permute-start(bf16[128,256]{1,0:T(8,128)(2,1)S(1)} %get-tuple-element.37), channel_id=1, source_target_pairs={{256,353},{257,354},{258,355},{259,356},{260,357},{261,358},{262,3... | collective-permute-start | bytes 196616 | tf_op jit(solution)/shard_map/ppermute | solution.py:45
  83.8 7.8 %collective-permute-start.27 = (bf16[128,256]{1,0:T(8,128)(2,1)S(1)}, bf16[128,256]{1,0:T(8,128)(2,1)S(1)}, u32[]{:S(2)}, u32[]{:S(2)}) collective-permute-start(bf16[128,256]{1,0:T(8,128)(2,1)S(1)} %get-tuple-element.37), channel_id=1, source_target_pairs={{256,352},{257,353},{258,354},{259,355},{260,356},{261,357},{262,3... | collective-permute-start | bytes 196616 | tf_op jit(solution)/shard_map/ppermute | solution.py:45
  84.5 7.1 %collective-permute-start.28 = (bf16[128,256]{1,0:T(8,128)(2,1)S(1)}, bf16[128,256]{1,0:T(8,128)(2,1)S(1)}, u32[]{:S(2)}, u32[]{:S(2)}) collective-permute-start(bf16[128,256]{1,0:T(8,128)(2,1)S(1)} %get-tuple-element.37), channel_id=1, source_target_pairs={{257,352},{258,353},{259,354},{260,355},{261,356},{262,357},{263,3... | collective-permute-start | bytes 196616 | tf_op jit(solution)/shard_map/ppermute | solution.py:45
  94.9 44.3 %collective-permute-start.35 = (bf16[128,256]{1,0:T(8,128)(2,1)S(1)}, bf16[128,256]{1,0:T(8,128)(2,1)S(1)}, u32[]{:S(2)}, u32[]{:S(2)}) collective-permute-start(bf16[128,256]{1,0:T(8,128)(2,1)S(1)} %get-tuple-element.41), channel_id=1, source_target_pairs={{384,481},{385,482},{386,483},{387,484},{388,485},{389,486},{390,4... | collective-permute-start | bytes 196616 | tf_op jit(solution)/shard_map/ppermute | solution.py:45
  96.2 48.0 %collective-permute-start.36 = (bf16[128,256]{1,0:T(8,128)(2,1)S(1)}, bf16[128,256]{1,0:T(8,128)(2,1)S(1)}, u32[]{:S(2)}, u32[]{:S(2)}) collective-permute-start(bf16[128,256]{1,0:T(8,128)(2,1)S(1)} %get-tuple-element.41), channel_id=1, source_target_pairs={{384,480},{385,481},{386,482},{387,483},{388,484},{389,485},{390,4... | collective-permute-start | bytes 196616 | tf_op jit(solution)/shard_map/ppermute | solution.py:45
  97.5 47.2 %collective-permute-start.37 = (bf16[128,256]{1,0:T(8,128)(2,1)S(1)}, bf16[128,256]{1,0:T(8,128)(2,1)S(1)}, u32[]{:S(2)}, u32[]{:S(2)}) collective-permute-start(bf16[128,256]{1,0:T(8,128)(2,1)S(1)} %get-tuple-element.41), channel_id=1, source_target_pairs={{385,480},{386,481},{387,482},{388,483},{389,484},{390,485},{391,4... | collective-permute-start | bytes 196616 | tf_op jit(solution)/shard_map/ppermute | solution.py:45
  148.9 6.2 %collective-permute-start.38 = (bf16[128,256]{1,0:T(8,128)(2,1)S(1)}, bf16[128,256]{1,0:T(8,128)(2,1)S(1)}, u32[]{:S(2)}, u32[]{:S(2)}) collective-permute-start(bf16[128,256]{1,0:T(8,128)(2,1)S(1)} %get-tuple-element.54), channel_id=1, source_target_pairs={{0,32},{32,0},{64,96},{96,64},{128,160},{160,128},{192,224},{224,1... | collective-permute-start | bytes 196616 | tf_op jit(solution)/shard_map/ppermute | solution.py:273
  (18 other events, 56.3 us)
